TPU v7x, 256 devices: a whole 4x4x8 slice. The times are simulated.
256 devices in a mesh: rep: 8 (over y, x_lo), blk: 32 (over x_hi, z, core).
Axes of the slice: x: 4 (x_hi: 2, x_lo: 2; x = x_hi * 2 + x_lo), y: 4, z: 8, core: 2. Of those that a mesh axis runs over, the one named last changes fastest.
Arguments:
- features: bfloat16 [32, 2048, 128], P('blk', 'rep'), may hold values from -6 to 6
- node_ids: int32 [32, 2048], P('blk', 'rep'), may hold values from 0 to 8388607
- labels: int32 [32, 2048], P('blk', 'rep'), may hold values from 0 to 171
- train_mask: int32 [32, 2048], P('blk', 'rep'), may hold values 0 or 1
- tile_values: bfloat16 [32, 8, 4, 16, 128, 128], P('blk', 'rep'), may hold values from -0.125 to 0.125
- tile_place: int32 [32, 8, 4, 16], P('blk', 'rep'), may hold values from 0 to 255, as said below
- tile_count: int32 [32, 8, 4], P('blk', 'rep'), may hold values from 1 to 16, as said below
- weight_in: bfloat16 [128, 256], replicated, may hold values from -0.5 to 0.5
- weight_out: bfloat16 [256, 172], replicated, may hold values from -8 to 8
- class_bias: float32 [172], replicated, may hold values from -5 to 5
Outputs:
- logits: float32 [32, 2048, 172], P('blk', 'rep')
- grad_in: float32 [128, 256], replicated
- grad_out: float32 [256, 172], replicated
Inputs may be any that keep to these rules, and one draw needn't show every extreme that they name: `tile_place`: within one block pair the slots name distinct positions. `tile_count`: the live slots of a pair are its first ones; some device has 16 live slots in each of its pairs.
All inputs are finite; a program needn't handle non-finite values. No bound on the sum of `train_mask` on one device may be relied on, other than what follows from the above.
Results may differ from a plain program's by a relative error of at most 0.015.
The roundings to bfloat16 on the way count: a program that leaves them out, or rounds other values in their place, can miss the bound.
Values may be sent and summed in bfloat16 or wider, within the bound.
A program may use at most 128 MiB of HBM per device.

v0:
```python
import math

import jax
import jax.numpy as jnp
from jax import lax
from jax.sharding import PartitionSpec as P


def from_behind(value, axis, steps):
    count = lax.axis_size(axis)
    pairs = [(source, (source + steps) % count) for source in range(count)]
    return lax.ppermute(value, axis, pairs)


def keep_factor(id_values, unit_count):
    columns = jnp.arange(unit_count, dtype=jnp.int32)
    mixed = id_values[:, None] * 73244475 + columns[None, :] * 19349663 + 12345
    mixed = mixed ^ jnp.right_shift(mixed, 15)
    mixed = mixed * 40503
    mixed = mixed ^ jnp.right_shift(mixed, 13)
    kept_mask = jnp.bitwise_and(mixed, 3) != 0
    return jnp.where(kept_mask, jnp.float32(4.0 / 3.0), jnp.float32(0.0))


def place_rows(tile_group, place_group, live_slots, source, tile_side, backward):
    tile_edge = tile_group.shape[-1]
    feat_width = source.shape[-1]
    pieces = source.reshape(tile_side, tile_edge, feat_width)
    if backward:
        gathered = jnp.take(pieces, place_group // tile_side, axis=0)
        products = jnp.einsum(
            "tji,tjf->tif", tile_group, gathered, preferred_element_type=jnp.float32
        )
        target = place_group % tile_side
    else:
        gathered = jnp.take(pieces, place_group % tile_side, axis=0)
        products = jnp.einsum(
            "tij,tjf->tif", tile_group, gathered, preferred_element_type=jnp.float32
        )
        target = place_group // tile_side
    masked = products * live_slots.astype(jnp.float32)[:, None, None]
    summed = jnp.zeros((tile_side, tile_edge, feat_width), jnp.float32).at[target].add(masked)
    return summed.reshape(tile_side * tile_edge, feat_width)


def section_terms(section_tiles, section_place, section_count, source, tile_side, backward):
    slot_count = section_tiles.shape[0]
    live_slots = jnp.arange(slot_count, dtype=jnp.int32) < section_count
    return place_rows(section_tiles, section_place, live_slots, source, tile_side, backward)


def slope_of(logits, label_ids, node_mask, scale):
    likelihood = jax.nn.softmax(logits, axis=-1)
    onehot = (label_ids[:, None] == jnp.arange(logits.shape[-1], dtype=jnp.int32)[None, :]).astype(
        jnp.float32
    )
    return ((likelihood - onehot) * node_mask[:, None].astype(jnp.float32) * scale).astype(
        jnp.bfloat16
    )


def on_device(
    features,
    node_ids,
    labels,
    train_mask,
    tile_values,
    tile_place,
    tile_count,
    weight_in,
    weight_out,
    class_bias,
):
    own_rows = features.shape[1]
    rep_size = lax.axis_size("rep")
    blk_size = lax.axis_size("blk")
    rep_index = lax.axis_index("rep")
    rep_bits = (rep_size - 1).bit_length()
    section_total = tile_values.shape[2]
    tile_edge = tile_values.shape[-1]
    group_rows = own_rows * rep_size
    tile_side = group_rows // tile_edge
    hidden_width = weight_in.shape[1]
    tiles_here = tile_values[0, 0]
    place_here = tile_place[0, 0]
    count_here = tile_count[0, 0]
    scale = 1.0 / math.sqrt(group_rows * blk_size)

    def spread(source):
        for bit_index in range(rep_bits):
            shifted = from_behind(source, "blk", section_total * (1 << bit_index))
            source = jnp.where(jnp.right_shift(rep_index, bit_index) % 2 == 1, shifted, source)
        running_sum = jnp.zeros((group_rows, source.shape[1]), jnp.float32)
        for section_index in range(section_total):
            running_sum = running_sum + section_terms(
                tiles_here[section_index],
                place_here[section_index],
                count_here[section_index],
                source,
                tile_side,
                False,
            )
            if section_index + 1 < section_total:
                source = from_behind(source, "blk", 1)
        return running_sum

    feature_block = lax.all_gather(features[0], "rep", axis=0, tiled=True)
    z_input = lax.psum_scatter(
        spread(feature_block), "rep", scatter_dimension=0, tiled=True
    ).astype(jnp.bfloat16)
    kept = keep_factor(node_ids[0], hidden_width)
    pre_act = jnp.dot(z_input, weight_in, preferred_element_type=jnp.float32)
    dropped = (jnp.maximum(pre_act, 0.0) * kept).astype(jnp.bfloat16)
    hidden_block = lax.all_gather(dropped, "rep", axis=0, tiled=True)
    z_output = lax.psum_scatter(
        spread(hidden_block), "rep", scatter_dimension=0, tiled=True
    ).astype(jnp.bfloat16)
    logits = jnp.dot(z_output, weight_out, preferred_element_type=jnp.float32) + class_bias
    slope = slope_of(logits, labels[0], train_mask[0], scale)
    grad_rows = jnp.einsum(
        "nc,hc->nh", slope, weight_out, preferred_element_type=jnp.float32
    ).astype(jnp.bfloat16)
    gradient_block = lax.all_gather(grad_rows, "rep", axis=0, tiled=True)
    out_terms = jnp.einsum("nh,nc->hc", z_output, slope, preferred_element_type=jnp.float32)
    grad_out = lax.psum(out_terms, ("rep", "blk"))
    running_sum = jnp.zeros((group_rows, gradient_block.shape[1]), jnp.float32)
    for section_index in reversed(range(section_total)):
        running_sum = running_sum + section_terms(
            tiles_here[section_index],
            place_here[section_index],
            count_here[section_index],
            gradient_block,
            tile_side,
            True,
        )
        if section_index > 0:
            running_sum = from_behind(running_sum.astype(jnp.bfloat16), "blk", -1).astype(
                running_sum.dtype
            )
    for bit_index in range(rep_bits):
        shifted = from_behind(
            running_sum.astype(jnp.bfloat16), "blk", -section_total * (1 << bit_index)
        ).astype(running_sum.dtype)
        running_sum = jnp.where(
            jnp.right_shift(rep_index, bit_index) % 2 == 1, shifted, running_sum
        )
    back_rows = lax.psum_scatter(
        running_sum.astype(jnp.bfloat16), "rep", scatter_dimension=0, tiled=True
    ).astype(jnp.float32)
    pre_slope = (back_rows * kept * (pre_act > 0)).astype(jnp.bfloat16)
    in_terms = jnp.einsum("nf,nh->fh", z_input, pre_slope, preferred_element_type=jnp.float32)
    grad_in = lax.psum(in_terms, ("rep", "blk"))
    return (logits[None], grad_in, grad_out)


def solution(mesh):
    placed = (
        P("blk", "rep", None),
        P("blk", "rep"),
        P("blk", "rep"),
        P("blk", "rep"),
        P("blk", "rep", None, None, None, None),
        P("blk", "rep", None, None),
        P("blk", "rep", None),
        P(),
        P(),
        P(),
    )
    return jax.shard_map(
        on_device,
        mesh=mesh,
        in_specs=placed,
        out_specs=(P("blk", "rep", None), P(), P()),
        check_vma=False,
    )
```

profile of v0, /device:TPU:1, one launch (start us, length us, event | category | flops | bytes accessed | tf_op | source)
XLA Modules:
  0.0 1080.6 jit_solution(6078047750428248411)
XLA Ops:
  7.2 25.7 %all-gather = bf16[1,2048,128]{2,1,0:T(8,128)(2,1)S(1)} all-gather(bf16[1,256,128]{2,1,0:T(8,128)(2,1)} %param.14), channel_id=2, replica_groups=mesh['rep'=8,'blk'=32] {'rep'}, dimensions={1}, use_global_device_ids=true | all-gather | bytes 589824 | tf_op jit(solution)/shard_map/all_gather | solution.py:107
  33.0 3.0 collective-permute-start
  38.9 12.6 %collective-permute-done = bf16[2048,128]{1,0:T(8,128)(2,1)S(1)} collective-permute-done((bf16[2048,128]{1,0:T(8,128)(2,1)S(1)}, bf16[2048,128]{1,0:T(8,128)(2,1)S(1)}, u32[]{:S(2)}, u32[]{:S(2)}) %collective-permute-start) | collective-permute-done | bytes 524320 | tf_op jit(solution)/shard_map/ppermute | solution.py:12
  53.8 20.8 %collective-permute-done.1 = bf16[2048,128]{1,0:T(8,128)(2,1)S(1)} collective-permute-done((bf16[2048,128]{1,0:T(8,128)(2,1)S(1)}, bf16[2048,128]{1,0:T(8,128)(2,1)S(1)}, u32[]{:S(2)}, u32[]{:S(2)}) %collective-permute-start.1) | collective-permute-done | bytes 524320 | tf_op jit(solution)/shard_map/ppermute | solution.py:12
  75.4 9.2 collective-permute-done.2
  84.6 28.6 %collective-permute-start.3 = (bf16[2048,128]{1,0:T(8,128)(2,1)S(1)}, bf16[2048,128]{1,0:T(8,128)(2,1)}, u32[]{:S(2)}, u32[]{:S(2)}) collective-permute-start(bf16[2048,128]{1,0:T(8,128)(2,1)S(1)} %broadcast_select_fusion.5), channel_id=1, source_target_pairs={{0,1},{1,2},{2,3},{3,4},{4,5},{5,6},{6,7},{7,8},{8,9},{9,10},{10,1... | collective-permute-start | bytes 1572872 | tf_op jit(solution)/shard_map/ppermute | solution.py:12
  113.3 6.1 collective-permute-done.3
  119.3 2.6 collective-permute-start.4
  127.0 2.6 scatter_fusion
  129.7 2.8 gather_fusion.1
  132.7 2.6 fusion.5
  135.3 2.6 copy.29
  139.0 3.8 scatter_fusion.1
  146.9 2.6 fusion.4
  149.5 2.6 copy.31
  152.0 2.6 scatter_fusion.2
  157.1 2.6 fusion.3
  159.7 2.5 copy.33
  163.4 3.7 scatter_fusion.3
  169.7 35.7 %reduce-scatter.4.cloned.1.call-done = f32[256,128]{1,0:T(8,128)} async-done(((f32[2048,128]{1,0:T(8,128)}), f32[256,128]{1,0:T(8,128)}) %reduce-scatter.4.cloned.1.call-update) | async-done | bytes 131088 | tf_op jit(solution)/shard_map/reduce_scatter | solution.py:108
  207.3 42.5 %all-gather.4.cloned.1.call-done = bf16[2048,256]{1,0:T(8,128)(2,1)} async-done(((bf16[256,256]{1,0:T(8,128)(2,1)}), bf16[2048,256]{1,0:T(8,128)(2,1)}) %all-gather.4.cloned.1.call-update) | async-done | bytes 1048592 | tf_op jit(solution)/shard_map/all_gather | solution.py:114
  251.9 36.6 %collective-permute-done.6 = bf16[2048,256]{1,0:T(8,128)(2,1)S(1)} collective-permute-done((bf16[2048,256]{1,0:T(8,128)(2,1)}, bf16[2048,256]{1,0:T(8,128)(2,1)S(1)}, u32[]{:S(2)}, u32[]{:S(2)}) %collective-permute-start.6) | collective-permute-done | bytes 1048608 | tf_op jit(solution)/shard_map/ppermute | solution.py:12
  290.1 52.6 %collective-permute-done.7 = bf16[2048,256]{1,0:T(8,128)(2,1)S(1)} collective-permute-done((bf16[2048,256]{1,0:T(8,128)(2,1)S(1)}, bf16[2048,256]{1,0:T(8,128)(2,1)S(1)}, u32[]{:S(2)}, u32[]{:S(2)}) %collective-permute-start.7) | collective-permute-done | bytes 1048608 | tf_op jit(solution)/shard_map/ppermute | solution.py:12
  342.8 4.2 collective-permute-start.8
  347.0 20.0 %collective-permute-done.8 = bf16[2048,256]{1,0:T(8,128)(2,1)S(1)} collective-permute-done((bf16[2048,256]{1,0:T(8,128)(2,1)S(1)}, bf16[2048,256]{1,0:T(8,128)(2,1)S(1)}, u32[]{:S(2)}, u32[]{:S(2)}) %collective-permute-start.8) | collective-permute-done | bytes 1048608 | tf_op jit(solution)/shard_map/ppermute | solution.py:12
  367.2 24.7 %collective-permute-start.9 = (bf16[2048,256]{1,0:T(8,128)(2,1)S(1)}, bf16[2048,256]{1,0:T(8,128)(2,1)S(1)}, u32[]{:S(2)}, u32[]{:S(2)}) collective-permute-start(bf16[2048,256]{1,0:T(8,128)(2,1)S(1)} %broadcast_select_fusion.2), channel_id=1, source_target_pairs={{0,1},{1,2},{2,3},{3,4},{4,5},{5,6},{6,7},{7,8},{8,9},{9,10},{10,1... | collective-permute-start | bytes 3145736 | tf_op jit(solution)/shard_map/ppermute | solution.py:12
  391.9 11.7 %collective-permute-done.9 = bf16[2048,256]{1,0:T(8,128)(2,1)S(1)} collective-permute-done((bf16[2048,256]{1,0:T(8,128)(2,1)S(1)}, bf16[2048,256]{1,0:T(8,128)(2,1)S(1)}, u32[]{:S(2)}, u32[]{:S(2)}) %collective-permute-start.9) | collective-permute-done | bytes 1048608 | tf_op jit(solution)/shard_map/ppermute | solution.py:12
  407.1 11.7 %collective-permute-done.10 = bf16[2048,256]{1,0:T(8,128)(2,1)} collective-permute-done((bf16[2048,256]{1,0:T(8,128)(2,1)S(1)}, bf16[2048,256]{1,0:T(8,128)(2,1)}, u32[]{:S(2)}, u32[]{:S(2)}) %collective-permute-start.10) | collective-permute-done | bytes 1048608 | tf_op jit(solution)/shard_map/ppermute | solution.py:12
  418.8 2.8 collective-permute-start.11
  423.2 3.1 multiply_bitcast_fusion.7
  426.4 2.9 copy.35
  429.5 3.5 scatter_fusion.4
  433.0 2.6 gather_fusion.5
  435.6 3.0 multiply_bitcast_fusion.6
  438.6 2.9 copy.37
  443.8 4.5 scatter_fusion.5
  452.7 3.0 multiply_bitcast_fusion.5
  455.6 2.9 copy.39
  458.5 3.5 scatter_fusion.6
  463.9 2.9 multiply_bitcast_fusion.4
  466.9 2.9 copy.41
  471.3 5.2 scatter_fusion.7
  476.5 3.5 add.324
  480.6 48.7 %reduce-scatter.6.cloned.1.call-done = f32[256,256]{1,0:T(8,128)} async-done(((f32[2048,256]{1,0:T(8,128)}), f32[256,256]{1,0:T(8,128)}) %reduce-scatter.6.cloned.1.call-update) | async-done | bytes 262160 | tf_op jit(solution)/shard_map/reduce_scatter | solution.py:115
  532.0 37.7 %all-gather.6.cloned.1.call-done = bf16[2048,256]{1,0:T(8,128)(2,1)} async-done(((bf16[256,256]{1,0:T(8,128)(2,1)}), bf16[2048,256]{1,0:T(8,128)(2,1)}) %all-gather.6.cloned.1.call-update) | async-done | bytes 1048592 | tf_op jit(solution)/shard_map/all_gather | solution.py:123
  575.2 3.5 scatter_fusion.8
  579.9 5.1 collective-permute-start.12
  590.6 3.5 scatter_fusion.9
  594.1 4.8 collective-permute-done.12
  599.0 2.7 fusion.1
  607.3 3.5 scatter_fusion.10
  610.8 5.4 collective-permute-done.13
  616.2 2.7 fusion
  618.9 2.9 collective-permute-start.14
  626.1 3.5 scatter_fusion.11
  629.6 4.0 collective-permute-done.14
  635.3 5.1 collective-permute-start.15
  640.5 43.2 %collective-permute-done.15 = bf16[2048,256]{1,0:T(8,128)(2,1)S(1)} collective-permute-done((bf16[2048,256]{1,0:T(8,128)(2,1)S(1)}, bf16[2048,256]{1,0:T(8,128)(2,1)S(1)}, u32[]{:S(2)}, u32[]{:S(2)}) %collective-permute-start.15) | collective-permute-done | bytes 1048608 | tf_op jit(solution)/shard_map/ppermute | solution.py:12
  685.6 7.0 collective-permute-start.16
  692.6 44.1 %collective-permute-done.16 = bf16[2048,256]{1,0:T(8,128)(2,1)S(1)} collective-permute-done((bf16[2048,256]{1,0:T(8,128)(2,1)S(1)}, bf16[2048,256]{1,0:T(8,128)(2,1)S(1)}, u32[]{:S(2)}, u32[]{:S(2)}) %collective-permute-start.16) | collective-permute-done | bytes 1048608 | tf_op jit(solution)/shard_map/ppermute | solution.py:12
  738.8 24.3 %collective-permute-done.17 = bf16[2048,256]{1,0:T(8,128)(2,1)S(1)} collective-permute-done((bf16[2048,256]{1,0:T(8,128)(2,1)S(1)}, bf16[2048,256]{1,0:T(8,128)(2,1)S(1)}, u32[]{:S(2)}, u32[]{:S(2)}) %collective-permute-start.17) | collective-permute-done | bytes 1048608 | tf_op jit(solution)/shard_map/ppermute | solution.py:12
  763.1 3.2 select_convert_fusion
  768.2 46.2 %reduce-scatter.8.cloned.1.call-done = bf16[256,256]{1,0:T(8,128)(2,1)} async-done(((bf16[2048,256]{1,0:T(8,128)(2,1)}), bf16[256,256]{1,0:T(8,128)(2,1)}) %reduce-scatter.8.cloned.1.call-update) | async-done | bytes 131088 | tf_op jit(solution)/shard_map/reduce_scatter | solution.py:147
  817.3 253.1 %all-reduce.3.cloned.1.call-done = (f32[128,256]{1,0:T(8,128)}, f32[256,172]{0,1:T(8,128)}) async-done(((f32[128,256]{1,0:T(8,128)}, f32[256,172]{0,1:T(8,128)}), (f32[128,256]{1,0:T(8,128)}, f32[256,172]{0,1:T(8,128)})) %all-reduce.3.cloned.1.call-update) | async-done | bytes 307216 | tf_op jit(solution)/shard_map/psum | solution.py:152
  (123 shorter events, 82.8 us)
Async XLA Ops:
  7.2 522.2 %copy-start = (bf16[256,172]{0,1:T(8,128)(2,1)S(1)}, bf16[256,172]{0,1:T(8,128)(2,1)}, u32[]{:S(2)}) copy-start(bf16[256,172]{0,1:T(8,128)(2,1)} %param.22) | copy-start | bytes 264196
  7.2 198.3 %reduce-scatter.4.cloned.1.call-start = ((), (), s32[]{:S(2)}) async-start(), calls=%async_computation.3 | async-start | bytes 1179648 | tf_op jit(solution)/shard_map/reduce_scatter | solution.py:108
  33.0 18.6 %collective-permute-start = (bf16[2048,128]{1,0:T(8,128)(2,1)S(1)}, bf16[2048,128]{1,0:T(8,128)(2,1)S(1)}, u32[]{:S(2)}, u32[]{:S(2)}) collective-permute-start(bf16[2048,128]{1,0:T(8,128)(2,1)S(1)} %bitcast.236), channel_id=1, source_target_pairs={{0,4},{1,5},{2,6},{3,7},{4,8},{5,9},{6,10},{7,11},{8,12},{9,13},{1... | collective-permute-start | bytes 1572872 | tf_op jit(solution)/shard_map/ppermute | solution.py:12
  38.9 74.3 %copy-start.8 = (s32[1,1,4,16]{3,2,1,0:T(4,128)S(1)}, s32[1,1,4,16]{3,2,1,0:T(4,128)}, u32[]{:S(2)}) copy-start(s32[1,1,4,16]{3,2,1,0:T(4,128)} %param.19) | copy-start | bytes 772
  51.6 22.9 %collective-permute-start.1 = (bf16[2048,128]{1,0:T(8,128)(2,1)S(1)}, bf16[2048,128]{1,0:T(8,128)(2,1)S(1)}, u32[]{:S(2)}, u32[]{:S(2)}) collective-permute-start(bf16[2048,128]{1,0:T(8,128)(2,1)S(1)} %broadcast_select_fusion.3), channel_id=1, source_target_pairs={{0,8},{1,9},{2,10},{3,11},{4,12},{5,13},{6,14},{7,15},{8,16},{9,17... | collective-permute-start | bytes 1572872 | tf_op jit(solution)/shard_map/ppermute | solution.py:12
  53.8 70.3 %copy-start.3 = (bf16[1,1,4,16,128,128]{5,4,3,2,1,0:T(8,128)(2,1)S(1)}, bf16[1,1,4,16,128,128]{5,4,3,2,1,0:T(8,128)(2,1)}, u32[]{:S(2)}) copy-start(bf16[1,1,4,16,128,128]{5,4,3,2,1,0:T(8,128)(2,1)} %param.18) | copy-start | bytes 6291460
  74.6 10.0 collective-permute-start.2
  84.6 34.7 %collective-permute-start.3 = (bf16[2048,128]{1,0:T(8,128)(2,1)S(1)}, bf16[2048,128]{1,0:T(8,128)(2,1)}, u32[]{:S(2)}, u32[]{:S(2)}) collective-permute-start(bf16[2048,128]{1,0:T(8,128)(2,1)S(1)} %broadcast_select_fusion.5), channel_id=1, source_target_pairs={{0,1},{1,2},{2,3},{3,4},{4,5},{5,6},{6,7},{7,8},{8,9},{9,10},{10,1... | collective-permute-start | bytes 1572872 | tf_op jit(solution)/shard_map/ppermute | solution.py:12
  119.3 13.2 %collective-permute-start.4 = (bf16[2048,128]{1,0:T(8,128)(2,1)}, bf16[2048,128]{1,0:T(8,128)(2,1)}, u32[]{:S(2)}, u32[]{:S(2)}) collective-permute-start(bf16[2048,128]{1,0:T(8,128)(2,1)} %collective-permute-done.3), channel_id=1, source_target_pairs={{0,1},{1,2},{2,3},{3,4},{4,5},{5,6},{6,7},{7,8},{8,9},{9,10},{10,1... | collective-permute-start | bytes 1572872 | tf_op jit(solution)/shard_map/ppermute | solution.py:12
  129.7 8.2 copy-start.5
  132.5 22.2 %collective-permute-start.5 = (bf16[2048,128]{1,0:T(8,128)(2,1)}, bf16[2048,128]{1,0:T(8,128)(2,1)}, u32[]{:S(2)}, u32[]{:S(2)}) collective-permute-start(bf16[2048,128]{1,0:T(8,128)(2,1)} %collective-permute-done.4), channel_id=1, source_target_pairs={{0,1},{1,2},{2,3},{3,4},{4,5},{5,6},{6,7},{7,8},{8,9},{9,10},{10,1... | collective-permute-start | bytes 1572872 | tf_op jit(solution)/shard_map/ppermute | solution.py:12
  167.1 2.5 copy-start.10
  167.1 38.3 %copy-start.12 = (bf16[128,256]{1,0:T(8,128)(2,1)S(1)}, bf16[128,256]{1,0:T(8,128)(2,1)}, u32[]{:S(2)}) copy-start(bf16[128,256]{1,0:T(8,128)(2,1)} %param.21) | copy-start | bytes 196612
  169.6 80.3 %all-gather.4.cloned.1.call-start = ((), (), s32[]{:S(2)}) async-start(), calls=%async_computation.4 | async-start | bytes 1179648 | tf_op jit(solution)/shard_map/all_gather | solution.py:114
  207.3 322.0 %reduce-scatter.6.cloned.1.call-start = ((), (), s32[]{:S(2)}) async-start(), calls=%async_computation.5 | async-start | bytes 2359296 | tf_op jit(solution)/shard_map/reduce_scatter | solution.py:115
  249.9 38.7 %collective-permute-start.6 = (bf16[2048,256]{1,0:T(8,128)(2,1)}, bf16[2048,256]{1,0:T(8,128)(2,1)S(1)}, u32[]{:S(2)}, u32[]{:S(2)}) collective-permute-start(bf16[2048,256]{1,0:T(8,128)(2,1)} %all-gather.4.cloned.1.call-done), channel_id=1, source_target_pairs={{0,4},{1,5},{2,6},{3,7},{4,8},{5,9},{6,10},{7,11},{8,12},{9,13},{1... | collective-permute-start | bytes 3145736 | tf_op jit(solution)/shard_map/ppermute | solution.py:12
  290.0 52.7 %collective-permute-start.7 = (bf16[2048,256]{1,0:T(8,128)(2,1)S(1)}, bf16[2048,256]{1,0:T(8,128)(2,1)S(1)}, u32[]{:S(2)}, u32[]{:S(2)}) collective-permute-start(bf16[2048,256]{1,0:T(8,128)(2,1)S(1)} %broadcast_select_fusion), channel_id=1, source_target_pairs={{0,8},{1,9},{2,10},{3,11},{4,12},{5,13},{6,14},{7,15},{8,16},{9,17... | collective-permute-start | bytes 3145736 | tf_op jit(solution)/shard_map/ppermute | solution.py:12
  342.8 24.3 %collective-permute-start.8 = (bf16[2048,256]{1,0:T(8,128)(2,1)S(1)}, bf16[2048,256]{1,0:T(8,128)(2,1)S(1)}, u32[]{:S(2)}, u32[]{:S(2)}) collective-permute-start(bf16[2048,256]{1,0:T(8,128)(2,1)S(1)} %broadcast_select_fusion.1), channel_id=1, source_target_pairs={{0,16},{1,17},{2,18},{3,19},{4,20},{5,21},{6,22},{7,23},{8,24},{9,... | collective-permute-start | bytes 3145736 | tf_op jit(solution)/shard_map/ppermute | solution.py:12
  367.2 36.4 %collective-permute-start.9 = (bf16[2048,256]{1,0:T(8,128)(2,1)S(1)}, bf16[2048,256]{1,0:T(8,128)(2,1)S(1)}, u32[]{:S(2)}, u32[]{:S(2)}) collective-permute-start(bf16[2048,256]{1,0:T(8,128)(2,1)S(1)} %broadcast_select_fusion.2), channel_id=1, source_target_pairs={{0,1},{1,2},{2,3},{3,4},{4,5},{5,6},{6,7},{7,8},{8,9},{9,10},{10,1... | collective-permute-start | bytes 3145736 | tf_op jit(solution)/shard_map/ppermute | solution.py:12
  403.7 1.0 copy-start.7
  404.6 14.2 %collective-permute-start.10 = (bf16[2048,256]{1,0:T(8,128)(2,1)S(1)}, bf16[2048,256]{1,0:T(8,128)(2,1)}, u32[]{:S(2)}, u32[]{:S(2)}) collective-permute-start(bf16[2048,256]{1,0:T(8,128)(2,1)S(1)} %collective-permute-done.9), channel_id=1, source_target_pairs={{0,1},{1,2},{2,3},{3,4},{4,5},{5,6},{6,7},{7,8},{8,9},{9,10},{10,1... | collective-permute-start | bytes 3145736 | tf_op jit(solution)/shard_map/ppermute | solution.py:12
  418.8 43.2 %collective-permute-start.11 = (bf16[2048,256]{1,0:T(8,128)(2,1)}, bf16[2048,256]{1,0:T(8,128)(2,1)}, u32[]{:S(2)}, u32[]{:S(2)}) collective-permute-start(bf16[2048,256]{1,0:T(8,128)(2,1)} %collective-permute-done.10), channel_id=1, source_target_pairs={{0,1},{1,2},{2,3},{3,4},{4,5},{5,6},{6,7},{7,8},{8,9},{9,10},{10,1... | collective-permute-start | bytes 3145736 | tf_op jit(solution)/shard_map/ppermute | solution.py:12
  433.0 5.6 copy-start.2
  441.5 2.3 copy-start.6
  479.9 0.7 copy-start.11
  479.9 49.4 %copy-start.9 = (f32[172]{0:T(256)S(1)}, f32[172]{0:T(256)}, u32[]{:S(2)}) copy-start(f32[172]{0:T(256)} %param.23) | copy-start | bytes 2068
  479.9 50.7 %copy-start.13 = (s32[1,256]{1,0:T(1,128)S(1)}, s32[1,256]{1,0:T(1,128)}, u32[]{:S(2)}) copy-start(s32[1,256]{1,0:T(1,128)} %param.16) | copy-start | bytes 3076
  480.0 89.7 %all-gather.6.cloned.1.call-start = ((), (), s32[]{:S(2)}) async-start(), calls=%async_computation.6 | async-start | bytes 1179648 | tf_op jit(solution)/shard_map/all_gather | solution.py:123
  531.6 282.8 %reduce-scatter.8.cloned.1.call-start = ((), (), s32[]{:S(2)}) async-start(), calls=%async_computation.7 | async-start | bytes 1179648 | tf_op jit(solution)/shard_map/reduce_scatter | solution.py:147
  578.8 6.2 copy-start.4
  579.9 19.1 %collective-permute-start.12 = (bf16[2048,256]{1,0:T(8,128)(2,1)}, bf16[2048,256]{1,0:T(8,128)(2,1)}, u32[]{:S(2)}, u32[]{:S(2)}) collective-permute-start(bf16[2048,256]{1,0:T(8,128)(2,1)} %bitcast.46), channel_id=1, source_target_pairs={{0,31},{1,0},{2,1},{3,2},{4,3},{5,4},{6,5},{7,6},{8,7},{9,8},{10,9... | collective-permute-start | bytes 3145736 | tf_op jit(solution)/shard_map/ppermute | solution.py:12
  601.7 14.5 %collective-permute-start.13 = (bf16[2048,256]{1,0:T(8,128)(2,1)}, bf16[2048,256]{1,0:T(8,128)(2,1)}, u32[]{:S(2)}, u32[]{:S(2)}) collective-permute-start(bf16[2048,256]{1,0:T(8,128)(2,1)} %fusion.1), channel_id=1, source_target_pairs={{0,31},{1,0},{2,1},{3,2},{4,3},{5,4},{6,5},{7,6},{8,7},{9,8},{10,9... | collective-permute-start | bytes 3145736 | tf_op jit(solution)/shard_map/ppermute | solution.py:12
  618.9 14.7 %collective-permute-start.14 = (bf16[2048,256]{1,0:T(8,128)(2,1)}, bf16[2048,256]{1,0:T(8,128)(2,1)}, u32[]{:S(2)}, u32[]{:S(2)}) collective-permute-start(bf16[2048,256]{1,0:T(8,128)(2,1)} %fusion), channel_id=1, source_target_pairs={{0,31},{1,0},{2,1},{3,2},{4,3},{5,4},{6,5},{7,6},{8,7},{9,8},{10,9... | collective-permute-start | bytes 3145736 | tf_op jit(solution)/shard_map/ppermute | solution.py:12
  635.3 48.4 %collective-permute-start.15 = (bf16[2048,256]{1,0:T(8,128)(2,1)S(1)}, bf16[2048,256]{1,0:T(8,128)(2,1)S(1)}, u32[]{:S(2)}, u32[]{:S(2)}) collective-permute-start(bf16[2048,256]{1,0:T(8,128)(2,1)S(1)} %fusion.23), channel_id=1, source_target_pairs={{0,28},{1,29},{2,30},{3,31},{4,0},{5,1},{6,2},{7,3},{8,4},{9,5},{1... | collective-permute-start | bytes 3145736 | tf_op jit(solution)/shard_map/ppermute | solution.py:12
  685.6 51.0 %collective-permute-start.16 = (bf16[2048,256]{1,0:T(8,128)(2,1)S(1)}, bf16[2048,256]{1,0:T(8,128)(2,1)S(1)}, u32[]{:S(2)}, u32[]{:S(2)}) collective-permute-start(bf16[2048,256]{1,0:T(8,128)(2,1)S(1)} %fusion.2), channel_id=1, source_target_pairs={{0,24},{1,25},{2,26},{3,27},{4,28},{5,29},{6,30},{7,31},{8,0},{9,1... | collective-permute-start | bytes 3145736 | tf_op jit(solution)/shard_map/ppermute | solution.py:12
  738.7 24.4 %collective-permute-start.17 = (bf16[2048,256]{1,0:T(8,128)(2,1)S(1)}, bf16[2048,256]{1,0:T(8,128)(2,1)S(1)}, u32[]{:S(2)}, u32[]{:S(2)}) collective-permute-start(bf16[2048,256]{1,0:T(8,128)(2,1)S(1)} %fusion.75), channel_id=1, source_target_pairs={{0,16},{1,17},{2,18},{3,19},{4,20},{5,21},{6,22},{7,23},{8,24},{9,... | collective-permute-start | bytes 3145736 | tf_op jit(solution)/shard_map/ppermute | solution.py:12
  766.3 307.3 %copy-start.1 = (bf16[256,172]{0,1:T(8,128)(2,1)S(1)}, bf16[256,172]{0,1:T(8,128)(2,1)}, u32[]{:S(2)}) copy-start(bf16[256,172]{0,1:T(8,128)(2,1)} %param.22) | copy-start | bytes 264196
  766.3 304.1 %all-reduce.3.cloned.1.call-start = ((), (), s32[]{:S(2)}) async-start(), calls=%async_computation.8 | async-start | bytes 622592 | tf_op jit(solution)/shard_map/psum | solution.py:152
Sparse Core Ops, SparseCore 0:
  169.7 35.6 reduce-scatter.3
  207.8 42.0 all-gather.3
  480.1 49.2 reduce-scatter.5
  531.7 37.9 all-gather.5
  766.4 47.8 reduce-scatter.7
  820.4 249.9 all-reduce.2
where the time goes:
time: 1090 us; the launch traced here: 1080 us
  waiting for transfers between devices  771 us (71%)
  starting transfers between devices  93.1 us (9%)
  other arithmetic  74.4 us (7%)
  local copies, waits for them, and re-layouts  65 us (6%)
  matrix products  36.4 us (3%)
  blocking collectives  25.7 us (2%)
  between operations  14.8 us (1%)
    ppermute x18, waiting for transfers between devices, from_behind(): return lax.ppermute(value, axis, pairs)  307 us
    psum x1, waiting for transfers between devices, on_device(): grad_in = lax.psum(in_terms, ('rep', 'blk'))  253 us
    ppermute x18, starting transfers between devices, from_behind(): return lax.ppermute(value, axis, pairs)  92.4 us
    reduce_scatter x1, waiting for transfers between devices, on_device(): lax.psum_scatter(spread(hidden_block), 'rep', scatter_dimension=0, tiled=...  48.7 us
    reduce_scatter x1, waiting for transfers between devices, on_device(): lax.psum_scatter(running_sum.astype(jnp.bfloat16), 'rep', scatter_dimensi...  46.2 us
    scatter-add x12, other arithmetic, place_rows(): jnp.zeros((tile_side, tile_edge, feat_width), jnp.float32).at[target]  43.4 us
    all_gather x1, waiting for transfers between devices, on_device(): hidden_block = lax.all_gather(dropped, 'rep', axis=0, tiled=True)  42.5 us
    all_gather x1, waiting for transfers between devices, on_device(): gradient_block = lax.all_gather(grad_rows, 'rep', axis=0, tiled=True)  37.7 us
  transfers between devices with their start and end apart: 24, of which 21 were waited for; matrix products, arithmetic and copies ran while one was open for 10% of the time, Pallas kernels for 0%

commit v1 on v0

v1 whole, which is shorter than its diff:
```python
import functools
import math

import jax
import jax.numpy as jnp
from jax import lax
from jax.experimental import pallas as pl
from jax.experimental.pallas import tpu as pltpu
from jax.sharding import PartitionSpec as P

MESH = pl.DeviceIdType.MESH
F32 = jnp.float32
BF16 = jnp.bfloat16
REP = 8
BLK = 32
SEC = 4
TILE = 128
SLOTS = 16
WIDE = 256
CLASSES = 172
VMEM_LIMIT = 56 << 20


def whole():
    return pl.BlockSpec(memory_space=pltpu.VMEM)


def in_smem():
    return pl.BlockSpec(memory_space=pltpu.SMEM)


def params(collective):
    if collective is None:
        return pltpu.CompilerParams(vmem_limit_bytes=VMEM_LIMIT)
    return pltpu.CompilerParams(
        collective_id=collective, has_side_effects=True, vmem_limit_bytes=VMEM_LIMIT
    )


def where_am_i():
    return lax.axis_index("rep"), lax.axis_index("blk")


def remote(source, target, send, arrive, device):
    return pltpu.make_async_remote_copy(
        src_ref=source,
        dst_ref=target,
        send_sem=send,
        recv_sem=arrive,
        device_id=device,
        device_id_type=MESH,
    )


def landed(target, send, arrive, device):
    remote(target, target, send, arrive, device).wait_recv()


def greet(device):
    pl.semaphore_signal(
        pltpu.get_barrier_semaphore(), inc=1, device_id=device, device_id_type=MESH
    )


def greet_group():
    rep, blk = where_am_i()
    for step in range(1, REP):
        greet((lax.rem(rep + step, REP), blk))
    return REP - 1


def greet_spread_sources():
    rep, blk = where_am_i()
    count = 0
    for other in range(REP):
        first = lax.rem(blk - SEC * rep + BLK, BLK)
        last = lax.rem(blk - SEC * rep - (SEC - 1) + 2 * BLK, BLK)
        if other == 0:
            @pl.when(rep != 0)
            def _():
                greet((0, first))
        else:
            greet((other, first))
        greet((other, last))
        count += 2
    greet((rep, lax.rem(blk + 1, BLK)))
    greet((rep, lax.rem(blk + BLK - 1, BLK)))
    return count + 2


def greet_fold_sources():
    rep, blk = where_am_i()
    count = 0
    for other in range(REP):
        first = lax.rem(blk + SEC * other, BLK)
        last = lax.rem(blk + SEC * other + (SEC - 1), BLK)
        if other == 0:
            @pl.when(rep != 0)
            def _():
                greet((0, first))
        else:
            greet((other, first))
        greet((other, last))
        count += 2
    greet((rep, lax.rem(blk + 1, BLK)))
    greet((rep, lax.rem(blk + BLK - 1, BLK)))
    return count + 2


def spread(shard, sections, send, chain_send, arrive):
    rep, blk = where_am_i()
    here = (rep, blk)
    up = lax.rem(blk + 1, BLK)
    down = lax.rem(blk + BLK - 1, BLK)

    def first_copy(other):
        return remote(
            shard.at[0],
            sections.at[0, 0, rep],
            send.at[0, other],
            arrive.at[0, 0, rep],
            (other, lax.rem(blk + SEC * other, BLK)),
        )

    def last_copy(other):
        return remote(
            shard.at[1],
            sections.at[SEC - 1, 1, rep],
            send.at[1, other],
            arrive.at[SEC - 1, 1, rep],
            (other, lax.rem(blk + SEC * other + SEC - 1, BLK)),
        )

    for step in range(REP):
        other = lax.rem(rep + step, REP)
        if step == 0:
            @pl.when(rep == 0)
            def _():
                sections[0, 0, 0] = shard[0]

            @pl.when(rep != 0)
            def _():
                first_copy(other).start()
        else:
            first_copy(other).start()
        last_copy(other).start()

    def hop(index, carry):
        section = index // REP
        step = lax.rem(index, REP)
        piece = lax.rem(rep + REP - step, REP)
        local = jnp.logical_and(jnp.logical_and(rep == 0, piece == 0), section == 0)
        other_section = SEC - 1 - section

        @pl.when(jnp.logical_not(local))
        def _():
            landed(
                sections.at[section, 0, piece],
                chain_send.at[0, 0, 0],
                arrive.at[section, 0, piece],
                here,
            )

        remote(
            sections.at[section, 0, piece],
            sections.at[section + 1, 0, piece],
            chain_send.at[0, section, piece],
            arrive.at[section + 1, 0, piece],
            (rep, up),
        ).start()
        landed(
            sections.at[other_section, 1, piece],
            chain_send.at[0, 0, 0],
            arrive.at[other_section, 1, piece],
            here,
        )
        remote(
            sections.at[other_section, 1, piece],
            sections.at[other_section - 1, 1, piece],
            chain_send.at[1, section, piece],
            arrive.at[other_section - 1, 1, piece],
            (rep, down),
        ).start()
        return carry

    lax.fori_loop(0, (SEC - 1) * REP, hop, 0)

    def finish(piece, carry):
        landed(
            sections.at[SEC - 1, 0, piece],
            chain_send.at[0, 0, 0],
            arrive.at[SEC - 1, 0, piece],
            here,
        )
        landed(
            sections.at[0, 1, piece], chain_send.at[0, 0, 0], arrive.at[0, 1, piece], here
        )
        @pl.when(jnp.logical_not(jnp.logical_and(rep == 0, piece == 0)))
        def _():
            first_copy(piece).wait_send()

        last_copy(piece).wait_send()
        for section in range(SEC - 1):
            remote(
                sections.at[section, 0, piece],
                sections.at[section + 1, 0, piece],
                chain_send.at[0, section, piece],
                arrive.at[section + 1, 0, piece],
                (rep, up),
            ).wait_send()
            remote(
                sections.at[SEC - 1 - section, 1, piece],
                sections.at[SEC - 2 - section, 1, piece],
                chain_send.at[1, section, piece],
                arrive.at[SEC - 2 - section, 1, piece],
                (rep, down),
            ).wait_send()
        return carry

    lax.fori_loop(0, REP, finish, 0)


SPREAD_SEMS = (
    pltpu.SemaphoreType.DMA((2, REP)),
    pltpu.SemaphoreType.DMA((2, SEC - 1, REP)),
    pltpu.SemaphoreType.DMA((SEC, 2, REP)),
)


def group_send(pieces, landing, send, arrive):
    rep, blk = where_am_i()
    for step in range(1, REP):
        other = lax.rem(rep + step, REP)
        remote(
            pieces.at[other], landing.at[rep], send.at[other], arrive.at[rep], (other, blk)
        ).start()


def group_wait(pieces, landing, send, arrive):
    rep, blk = where_am_i()
    for step in range(1, REP):
        other = lax.rem(rep + step, REP)
        copy = remote(
            pieces.at[other], landing.at[other], send.at[other], arrive.at[other], (other, blk)
        )
        copy.wait_recv()
        copy.wait_send()


def group_sum(pieces, landing):
    rep, blk = where_am_i()
    landing[rep] = pieces[rep]
    total = landing[0].astype(F32)
    for index in range(1, REP):
        total = total + landing[index].astype(F32)
    return total


GROUP_SEMS = (pltpu.SemaphoreType.DMA((REP,)), pltpu.SemaphoreType.DMA((REP,)))


def keep_factor(ids):
    columns = lax.broadcasted_iota(jnp.int32, (1, WIDE), 1)
    mixed = ids * 73244475 + columns * 19349663 + 12345
    mixed = mixed ^ jnp.right_shift(mixed, 15)
    mixed = mixed * 40503
    mixed = mixed ^ jnp.right_shift(mixed, 13)
    return jnp.where(jnp.bitwise_and(mixed, 3) != 0, F32(4.0 / 3.0), F32(0.0))


def first_kernel(x, sections, send, chain_send, arrive):
    waits = greet_spread_sources()
    rep, blk = where_am_i()
    pl.semaphore_wait(pltpu.get_barrier_semaphore(), waits - jnp.where(rep == 0, 1, 0))
    spread(x, sections, send, chain_send, arrive)


def forward_kernel(place, count, tiles, sections, out, total):
    total[...] = jnp.zeros_like(total)
    for section in range(SEC):
        live = count[section]
        for group in range(SLOTS // 4):
            @pl.when(group * 4 < live)
            def _(section=section, group=group):
                for slot in range(group * 4, group * 4 + 4):
                    spot = place[section, slot]
                    row = spot // SLOTS
                    column = lax.rem(spot, SLOTS)
                    source = sections[section, lax.rem(column, 2), column // 2]
                    product = jnp.dot(
                        tiles[section, slot], source, preferred_element_type=F32
                    )
                    flag = jnp.where(slot < live, F32(1.0), F32(0.0))
                    total[row] = total[row] + product * flag
    out[...] = total[...].astype(out.dtype)


def backward_kernel(place, count, tiles, rows, out, total):
    total[...] = jnp.zeros_like(total)
    for section in range(SEC):
        live = count[section]
        for group in range(SLOTS // 4):
            @pl.when(group * 4 < live)
            def _(section=section, group=group):
                for slot in range(group * 4, group * 4 + 4):
                    spot = place[section, slot]
                    row = spot // SLOTS
                    column = lax.rem(spot, SLOTS)
                    product = lax.dot_general(
                        tiles[section, slot],
                        rows[row],
                        (((0,), (0,)), ((), ())),
                        preferred_element_type=F32,
                    )
                    flag = jnp.where(slot < live, F32(1.0), F32(0.0))
                    half = lax.rem(column, 2)
                    piece = column // 2
                    total[section, half, piece] = total[section, half, piece] + product * flag
    out[...] = total[...].astype(out.dtype)


def hidden_kernel(
    partial,
    ids,
    weight_in,
    weight_out,
    z_out,
    dropped_out,
    slope_factor,
    sections,
    landing,
    shard,
    group_sems_send,
    group_sems_arrive,
    send,
    chain_send,
    arrive,
):
    waits = greet_group() + greet_spread_sources()
    rep, blk = where_am_i()
    pl.semaphore_wait(pltpu.get_barrier_semaphore(), waits - jnp.where(rep == 0, 1, 0))
    group_send(partial, landing, group_sems_send, group_sems_arrive)
    group_wait(partial, landing, group_sems_send, group_sems_arrive)
    z_input = group_sum(partial, landing).astype(BF16)
    z_out[...] = z_input
    pre_act = jnp.dot(z_input, weight_in[...], preferred_element_type=F32)
    kept = keep_factor(ids[...])
    dropped = (jnp.maximum(pre_act, 0.0) * kept).astype(BF16)
    dropped_out[...] = dropped
    slope_factor[...] = jnp.where(pre_act > 0, kept, 0.0)
    mapped = jnp.dot(dropped, weight_out[...], preferred_element_type=F32).astype(BF16)
    shard[0] = mapped[:TILE]
    shard[1] = mapped[TILE:]
    spread(shard, sections, send, chain_send, arrive)


def class_kernel(
    scale,
    partial,
    labels,
    mask,
    bias,
    logits_out,
    slopes,
    landing,
    send,
    arrive,
    slope_send,
    slope_arrive,
):
    waits = greet_group()
    rep, blk = where_am_i()
    pl.semaphore_wait(pltpu.get_barrier_semaphore(), waits)
    group_send(partial, landing, send, arrive)
    group_wait(partial, landing, send, arrive)
    logits = group_sum(partial, landing) + bias[...]
    logits_out[...] = logits[:, :CLASSES]
    columns = lax.broadcasted_iota(jnp.int32, logits.shape, 1)
    real = columns < CLASSES
    top = jnp.max(jnp.where(real, logits, -jnp.inf), axis=1, keepdims=True)
    powers = jnp.where(real, jnp.exp(logits - top), 0.0)
    likelihood = powers / jnp.sum(powers, axis=1, keepdims=True)
    onehot = jnp.where(columns == labels[...], 1.0, 0.0)
    slope = (likelihood - onehot) * mask[...].astype(F32) * scale
    slopes[rep] = slope.astype(BF16)
    for step in range(1, REP):
        other = lax.rem(rep + step, REP)
        remote(
            slopes.at[rep], slopes.at[rep], slope_send.at[other], slope_arrive.at[rep], (other, blk)
        ).start()
    for step in range(1, REP):
        other = lax.rem(rep + step, REP)
        copy = remote(
            slopes.at[rep], slopes.at[other], slope_send.at[other], slope_arrive.at[other], (other, blk)
        )
        copy.wait_recv()
        copy.wait_send()


def blk_of(part, depth, core):
    return (part * (BLK // 4) + depth) * 2 + core


def last_kernel(
    parts,
    z_input,
    dropped,
    slope_factor,
    weight_out,
    grad_in,
    grad_out,
    low_in,
    high_in,
    low_out,
    high_out,
    final_out,
    final_in,
    mine,
    terms,
    landing,
    corner,
    corner_in,
    depth_in,
    full_corner,
    full,
    chain_send,
    chain_arrive,
    final_send,
    final_arrive,
    a_send,
    a_arrive,
    b_send,
    b_arrive,
    c_send,
    c_arrive,
    d_send,
    d_arrive,
    e_send,
    e_arrive,
):
    rep, blk = where_am_i()
    here = (rep, blk)
    core = lax.rem(blk, 2)
    depth = lax.rem(blk // 2, 8)
    part = blk // 16
    waits = greet_group() + greet_fold_sources()
    corner_me = part * 2 + core
    for step in range(1, 4):
        other = lax.rem(corner_me + step, 4)
        greet((rep, blk_of(other // 2, depth, lax.rem(other, 2))))
    for step in range(1, 8):
        greet((rep, blk_of(part, lax.rem(depth + step, 8), core)))
    waits = waits + 10
    pl.semaphore_wait(pltpu.get_barrier_semaphore(), waits - jnp.where(rep == 0, 1, 0))

    up = lax.rem(blk + 1, BLK)
    down = lax.rem(blk + BLK - 1, BLK)
    first = lax.rem(blk - SEC * rep + BLK, BLK)
    last = lax.rem(blk - SEC * rep - (SEC - 1) + 2 * BLK, BLK)

    def start(piece, carry):
        remote(
            parts.at[SEC - 1, 0, piece],
            low_in.at[SEC - 2, piece],
            chain_send.at[0, 0, piece],
            chain_arrive.at[0, SEC - 2, piece],
            (rep, down),
        ).start()
        remote(
            parts.at[0, 1, piece],
            high_in.at[0, piece],
            chain_send.at[1, 0, piece],
            chain_arrive.at[1, 0, piece],
            (rep, up),
        ).start()
        return carry

    lax.fori_loop(0, REP, start, 0)

    def hop(index, carry):
        step = index // REP
        piece = lax.rem(index, REP)
        low_section = SEC - 2 - step
        landed(
            low_in.at[low_section, piece],
            chain_send.at[0, 0, 0],
            chain_arrive.at[0, low_section, piece],
            here,
        )
        low_out[low_section, piece] = (
            low_in[low_section, piece].astype(F32) + parts[low_section, 0, piece].astype(F32)
        ).astype(BF16)
        remote(
            low_out.at[low_section, piece],
            low_in.at[low_section - 1, piece],
            chain_send.at[0, step + 1, piece],
            chain_arrive.at[0, low_section - 1, piece],
            (rep, down),
        ).start()
        landed(
            high_in.at[step, piece],
            chain_send.at[0, 0, 0],
            chain_arrive.at[1, step, piece],
            here,
        )
        high_out[step, piece] = (
            high_in[step, piece].astype(F32) + parts[step + 1, 1, piece].astype(F32)
        ).astype(BF16)
        remote(
            high_out.at[step, piece],
            high_in.at[step + 1, piece],
            chain_send.at[1, step + 1, piece],
            chain_arrive.at[1, step + 1, piece],
            (rep, up),
        ).start()
        return carry

    lax.fori_loop(0, (SEC - 2) * REP, hop, 0)

    def low_final(piece):
        return remote(
            final_out.at[0, piece],
            final_in.at[0, rep],
            final_send.at[0, piece],
            final_arrive.at[0, rep],
            (piece, first),
        )

    def high_final(piece):
        return remote(
            final_out.at[1, piece],
            final_in.at[1, rep],
            final_send.at[1, piece],
            final_arrive.at[1, rep],
            (piece, last),
        )

    def final(piece, carry):
        landed(
            low_in.at[0, piece], chain_send.at[0, 0, 0], chain_arrive.at[0, 0, piece], here
        )
        final_out[0, piece] = (
            low_in[0, piece].astype(F32) + parts[0, 0, piece].astype(F32)
        ).astype(BF16)
        self_piece = jnp.logical_and(rep == 0, piece == 0)

        @pl.when(self_piece)
        def _():
            final_in[0, 0] = final_out[0, 0]

        @pl.when(jnp.logical_not(self_piece))
        def _():
            low_final(piece).start()

        landed(
            high_in.at[SEC - 2, piece],
            chain_send.at[0, 0, 0],
            chain_arrive.at[1, SEC - 2, piece],
            here,
        )
        final_out[1, piece] = (
            high_in[SEC - 2, piece].astype(F32) + parts[SEC - 1, 1, piece].astype(F32)
        ).astype(BF16)
        high_final(piece).start()
        return carry

    lax.fori_loop(0, REP, final, 0)

    def gather_final(source, carry):
        @pl.when(jnp.logical_not(jnp.logical_and(rep == 0, source == 0)))
        def _():
            landed(
                final_in.at[0, source],
                chain_send.at[0, 0, 0],
                final_arrive.at[0, source],
                here,
            )

        landed(
            final_in.at[1, source], chain_send.at[0, 0, 0], final_arrive.at[1, source], here
        )
        return carry

    lax.fori_loop(0, REP, gather_final, 0)
    for half in range(2):
        total = final_in[half, 0].astype(F32)
        for source in range(1, REP):
            total = total + final_in[half, source].astype(F32)
        mine[pl.ds(half * TILE, TILE), :] = total.astype(BF16)

    back = mine[...]
    out_terms = lax.dot_general(
        dropped[...], back, (((0,), (0,)), ((), ())), preferred_element_type=F32
    )
    back_rows = lax.dot_general(
        back, weight_out[...], (((1,), (1,)), ((), ())), preferred_element_type=F32
    )
    pre_slope = (back_rows * slope_factor[...]).astype(BF16)
    in_terms = lax.dot_general(
        z_input[...], pre_slope, (((0,), (0,)), ((), ())), preferred_element_type=F32
    )
    in_rows = in_terms.shape[0]
    chunk = (in_rows + WIDE) // REP
    joined = jnp.concatenate([in_terms, out_terms], axis=0)
    for index in range(REP):
        terms[index] = joined[index * chunk : (index + 1) * chunk]
    group_send(terms, landing, a_send, a_arrive)
    group_wait(terms, landing, a_send, a_arrive)
    total = group_sum(terms, landing)
    for index in range(12):
        corner[index // 3, index % 3] = total[
            (index // 2) * 8 : (index // 2) * 8 + 8, (index % 2) * 128 : (index % 2) * 128 + 128
        ]

    def corner_device(index):
        return (rep, blk_of(index // 2, depth, lax.rem(index, 2)))

    for step in range(1, 4):
        other = lax.rem(corner_me + step, 4)
        remote(
            corner.at[other],
            corner_in.at[corner_me],
            b_send.at[other],
            b_arrive.at[corner_me],
            corner_device(other),
        ).start()
    for step in range(1, 4):
        other = lax.rem(corner_me + step, 4)
        copy = remote(
            corner.at[other],
            corner_in.at[other],
            b_send.at[other],
            b_arrive.at[other],
            corner_device(other),
        )
        copy.wait_recv()
        copy.wait_send()
    corner_in[corner_me] = corner[corner_me]
    total = corner_in[0] + corner_in[1] + corner_in[2] + corner_in[3]
    depth_in[depth] = total
    for step in range(1, 8):
        other = lax.rem(depth + step, 8)
        remote(
            depth_in.at[depth],
            depth_in.at[depth],
            c_send.at[other],
            c_arrive.at[depth],
            (rep, blk_of(part, other, core)),
        ).start()
    for step in range(1, 8):
        other = lax.rem(depth + step, 8)
        copy = remote(
            depth_in.at[depth],
            depth_in.at[other],
            c_send.at[other],
            c_arrive.at[other],
            (rep, blk_of(part, other, core)),
        )
        copy.wait_recv()
        copy.wait_send()
    total = depth_in[0]
    for index in range(1, 8):
        total = total + depth_in[index]
    full_corner[corner_me] = total
    for step in range(1, 4):
        other = lax.rem(corner_me + step, 4)
        remote(
            full_corner.at[corner_me],
            full_corner.at[corner_me],
            d_send.at[other],
            d_arrive.at[corner_me],
            corner_device(other),
        ).start()
    for step in range(1, 4):
        other = lax.rem(corner_me + step, 4)
        copy = remote(
            full_corner.at[corner_me],
            full_corner.at[other],
            d_send.at[other],
            d_arrive.at[other],
            corner_device(other),
        )
        copy.wait_recv()
        copy.wait_send()
    full[rep] = full_corner[...]
    for step in range(1, REP):
        other = lax.rem(rep + step, REP)
        remote(full.at[rep], full.at[rep], e_send.at[other], e_arrive.at[rep], (other, blk)).start()
    for step in range(1, REP):
        other = lax.rem(rep + step, REP)
        copy = remote(
            full.at[rep], full.at[other], e_send.at[other], e_arrive.at[other], (other, blk)
        )
        copy.wait_recv()
        copy.wait_send()
    for index in range(REP * 6):
        group, inner = index // 6, index % 6
        left, right = 2 * inner, 2 * inner + 1
        row = jnp.concatenate(
            [full[group, left // 3, left % 3], full[group, right // 3, right % 3]], axis=1
        )
        if index * 8 < in_rows:
            grad_in[index * 8 : index * 8 + 8, :] = row
        else:
            start_row = index * 8 - in_rows
            grad_out[start_row : start_row + 8, :] = row[:, :CLASSES]

    def drain(piece, carry):
        for direction in range(2):
            for step in range(SEC - 1):
                remote(
                    low_in.at[0, piece],
                    low_in.at[0, piece],
                    chain_send.at[direction, step, piece],
                    chain_arrive.at[0, 0, piece],
                    (rep, down),
                ).wait_send()
        @pl.when(jnp.logical_not(jnp.logical_and(rep == 0, piece == 0)))
        def _():
            low_final(piece).wait_send()

        high_final(piece).wait_send()
        return carry

    lax.fori_loop(0, REP, drain, 0)


def on_device(
    features,
    node_ids,
    labels,
    train_mask,
    tile_values,
    tile_place,
    tile_count,
    weight_in,
    weight_out,
    class_bias,
):
    width = features.shape[-1]
    own_rows = features.shape[1]
    scale = 1.0 / math.sqrt(own_rows * REP * BLK)
    tiles = tile_values[0, 0]
    place = tile_place[0, 0]
    count = tile_count[0, 0]
    shape = jax.ShapeDtypeStruct
    padded_out = jnp.pad(weight_out, ((0, 0), (0, WIDE - CLASSES)))
    padded_bias = jnp.pad(class_bias, (0, WIDE - CLASSES))[None, :]
    ids = node_ids.reshape(own_rows, 1)
    label_column = labels.reshape(own_rows, 1)
    mask_column = train_mask.reshape(own_rows, 1)

    sections = pl.pallas_call(
        first_kernel,
        out_shape=shape((SEC, 2, REP, TILE, width), BF16),
        in_specs=[whole()],
        out_specs=whole(),
        scratch_shapes=list(SPREAD_SEMS),
        compiler_params=params(0),
        name="spread_features",
    )(features.reshape(2, TILE, width))
    partial = pl.pallas_call(
        forward_kernel,
        out_shape=shape((2 * REP, TILE, width), F32),
        in_specs=[in_smem(), in_smem(), whole(), whole()],
        out_specs=whole(),
        scratch_shapes=[pltpu.VMEM((2 * REP, TILE, width), F32)],
        compiler_params=params(None),
        name="aggregate_features",
    )(place, count, tiles, sections)
    z_input, dropped, slope_factor, sections = pl.pallas_call(
        hidden_kernel,
        out_shape=(
            shape((own_rows, width), BF16),
            shape((own_rows, WIDE), BF16),
            shape((own_rows, WIDE), F32),
            shape((SEC, 2, REP, TILE, WIDE), BF16),
        ),
        in_specs=[whole()] * 4,
        out_specs=[whole()] * 4,
        scratch_shapes=[
            pltpu.VMEM((REP, own_rows, width), F32),
            pltpu.VMEM((2, TILE, WIDE), BF16),
            *GROUP_SEMS,
            *SPREAD_SEMS,
        ],
        compiler_params=params(1),
        name="hidden",
    )(partial.reshape(REP, own_rows, width), ids, weight_in, padded_out)
    partial = pl.pallas_call(
        forward_kernel,
        out_shape=shape((2 * REP, TILE, WIDE), BF16),
        in_specs=[in_smem(), in_smem(), whole(), whole()],
        out_specs=whole(),
        scratch_shapes=[pltpu.VMEM((2 * REP, TILE, WIDE), F32)],
        compiler_params=params(None),
        name="aggregate_hidden",
    )(place, count, tiles, sections)
    logits, slopes = pl.pallas_call(
        functools.partial(class_kernel, scale),
        out_shape=(
            shape((own_rows, CLASSES), F32),
            shape((REP, own_rows, WIDE), BF16),
        ),
        in_specs=[whole()] * 4,
        out_specs=[whole()] * 2,
        scratch_shapes=[
            pltpu.VMEM((REP, own_rows, WIDE), BF16),
            *GROUP_SEMS,
            *GROUP_SEMS,
        ],
        compiler_params=params(2),
        name="classes",
    )(partial.reshape(REP, own_rows, WIDE), label_column, mask_column, padded_bias)
    parts = pl.pallas_call(
        backward_kernel,
        out_shape=shape((SEC, 2, REP, TILE, WIDE), BF16),
        in_specs=[in_smem(), in_smem(), whole(), whole()],
        out_specs=whole(),
        scratch_shapes=[pltpu.VMEM((SEC, 2, REP, TILE, WIDE), F32)],
        compiler_params=params(None),
        name="aggregate_back",
    )(place, count, tiles, slopes.reshape(2 * REP, TILE, WIDE))
    chunk = (width + WIDE) // REP
    dma = pltpu.SemaphoreType.DMA
    grad_in, grad_out = pl.pallas_call(
        last_kernel,
        out_shape=(shape((width, WIDE), F32), shape((WIDE, CLASSES), F32)),
        in_specs=[whole()] * 5,
        out_specs=[whole()] * 2,
        scratch_shapes=[
            pltpu.VMEM((SEC - 1, REP, TILE, WIDE), BF16),
            pltpu.VMEM((SEC - 1, REP, TILE, WIDE), BF16),
            pltpu.VMEM((SEC - 1, REP, TILE, WIDE), BF16),
            pltpu.VMEM((SEC - 1, REP, TILE, WIDE), BF16),
            pltpu.VMEM((2, REP, TILE, WIDE), BF16),
            pltpu.VMEM((2, REP, TILE, WIDE), BF16),
            pltpu.VMEM((own_rows, WIDE), BF16),
            pltpu.VMEM((REP, chunk, WIDE), F32),
            pltpu.VMEM((REP, chunk, WIDE), F32),
            pltpu.VMEM((4, 3, 8, 128), F32),
            pltpu.VMEM((4, 3, 8, 128), F32),
            pltpu.VMEM((8, 3, 8, 128), F32),
            pltpu.VMEM((4, 3, 8, 128), F32),
            pltpu.VMEM((REP, 4, 3, 8, 128), F32),
            dma((2, SEC - 1, REP)),
            dma((2, SEC - 1, REP)),
            dma((2, REP)),
            dma((2, REP)),
            dma((REP,)),
            dma((REP,)),
            dma((4,)),
            dma((4,)),
            dma((8,)),
            dma((8,)),
            dma((4,)),
            dma((4,)),
            dma((REP,)),
            dma((REP,)),
        ],
        compiler_params=params(3),
        name="gradients",
    )(parts, z_input, dropped, slope_factor, padded_out)
    return (logits[None], grad_in, grad_out)


def solution(mesh):
    placed = (
        P("blk", "rep", None),
        P("blk", "rep"),
        P("blk", "rep"),
        P("blk", "rep"),
        P("blk", "rep", None, None, None, None),
        P("blk", "rep", None, None),
        P("blk", "rep", None),
        P(),
        P(),
        P(),
    )
    return jax.shard_map(
        on_device,
        mesh=mesh,
        in_specs=placed,
        out_specs=(P("blk", "rep", None), P(), P()),
        check_vma=False,
    )
```

time: 1090 us -> 282 us (0.26)
  waiting for transfers between devices: 771 us -> 0 us
  Pallas kernels: 0 us -> 272 us
  starting transfers between devices: 93.1 us -> 0 us
  other arithmetic: 74.4 us -> 0 us
  local copies, waits for them, and re-layouts: 65 us -> 8.82 us
  matrix products: 36.4 us -> 0 us
  blocking collectives: 25.7 us -> 0 us
  between operations: 14.8 us -> 0.69 us
    ppermute x18 -> x0, waiting for transfers between devices: 307 us -> none  [from_behind(): return lax.ppermute(value, axis, pairs)]
    pallas_call x0 -> x7, Pallas kernels: none -> 272 us  [the longest x1 118 us: on_device(): pl.pallas_call(last_kernel, out_shape=(shape((width, WIDE), F32), shape((...]
    psum x1 -> x0, waiting for transfers between devices: 253 us -> none  [on_device(): grad_in = lax.psum(in_terms, ('rep', 'blk'))]
    reduce_scatter x3 -> x0, waiting for transfers between devices: 131 us -> none  [the longest x1 48.7 us: on_device(): lax.psum_scatter(spread(hidden_block), 'rep', scatter_dimension=0, tiled=...]
    ppermute x18 -> x0, starting transfers between devices: 92.4 us -> none  [from_behind(): return lax.ppermute(value, axis, pairs)]
    all_gather x2 -> x0, waiting for transfers between devices: 80.2 us -> none  [the longest x1 42.5 us: on_device(): hidden_block = lax.all_gather(dropped, 'rep', axis=0, tiled=True)]
    scatter-add x12 -> x0, other arithmetic: 43.4 us -> none  [place_rows(): jnp.zeros((tile_side, tile_edge, feat_width), jnp.float32).at[target]]
    dot_general x17 -> x0, matrix products: 36.4 us -> none  [the longest x8 21.4 us: place_rows(): jnp.einsum('tij,tjf->tif', tile_group, gathered, preferred_element_type=j...]
  transfers between devices with their start and end apart: 24 -> 0, of which waited for: 21 -> 0; matrix products, arithmetic and copies ran while one was open for 10% -> 0% of each run, Pallas kernels for 0% -> 0%
where the time goes in v1:
time: 282 us; the launch traced here: 281 us
  Pallas kernels  272 us (96%)
  local copies, waits for them, and re-layouts  8.82 us (3%)
    pallas_call x1, Pallas kernels, on_device(): pl.pallas_call(last_kernel, out_shape=(shape((width, WIDE), F32), shape((...  118 us
    pallas_call x1, Pallas kernels, on_device(): pl.pallas_call(hidden_kernel, out_shape=(shape((own_rows, width), BF16),...  66.8 us
    pallas_call x1, Pallas kernels, on_device(): pl.pallas_call(first_kernel, out_shape=shape((SEC, 2, REP, TILE, width),...  39.1 us
    pallas_call x1, Pallas kernels, on_device(): pl.pallas_call(functools.partial(class_kernel, scale), out_shape=(shape((...  24 us
    pallas_call x1, Pallas kernels, on_device(): pl.pallas_call(backward_kernel, out_shape=shape((SEC, 2, REP, TILE, WIDE)...  8.96 us
    pallas_call x1, Pallas kernels, on_device(): pl.pallas_call(forward_kernel, out_shape=shape((2 * REP, TILE, WIDE), BF1...  7.88 us
    pallas_call x1, Pallas kernels, on_device(): pl.pallas_call(forward_kernel, out_shape=shape((2 * REP, TILE, width), F3...  6.57 us

profile of v1, /device:TPU:1, one launch (start us, length us, event | category | flops | bytes accessed | tf_op | source)
XLA Modules:
  0.0 281.2 jit_solution(14723067151027536621)
XLA Ops:
  0.6 0.0 copy-start.1
  0.6 0.0 copy-start
  0.7 39.1 %spread_features.1.sections = bf16[4,2,8,128,128]{4,3,2,1,0:T(8,128)(2,1)} custom-call(bf16[2,128,128]{2,1,0:T(8,128)(2,1)} %bitcast.19), custom_call_target="tpu_custom_call" | custom-call | tf_op jit(solution)/shard_map/spread_features/pallas_call | solution.py:753
  39.8 6.6 %aggregate_features.1 = f32[16,128,128]{2,1,0:T(8,128)} custom-call(s32[4,16]{1,0:T(4,128)} %bitcast.20, s32[4]{0:T(128)} %bitcast.23, bf16[4,16,128,128]{3,2,1,0:T(8,128)(2,1)} %bitcast.12, bf16[4,2,8,128,128]{4,3,2,1,0:T(8,128)(2,1)} %spread_features.1.sections), custom_call_target="tpu_custom_call" | custom-call | tf_op jit(solution)/shard_map/aggregate_features/pallas_call | solution.py:762
  46.3 0.0 copy-done.1
  46.4 0.8 copy.17.ids
  47.2 0.0 copy-done
  47.2 0.1 copy.16
  47.3 0.7 pad.8.weight_out
  47.9 0.0 copy-start.2
  47.9 0.0 copy-start.3
  47.9 0.0 copy-start.4
  47.9 66.8 %hidden.1 = (bf16[256,128]{1,0:T(8,128)(2,1)}, bf16[256,256]{1,0:T(8,128)(2,1)}, f32[256,256]{1,0:T(8,128)}, bf16[4,2,8,128,256]{4,3,2,1,0:T(8,128)(2,1)}) custom-call(f32[8,256,128]{2,1,0:T(8,128)} %bitcast.15, s32[256,1]{1,0:T(8,128)} %copy.17.ids, bf16[128,256]{1,0:T(8,128)(2,1)} %weight_in.1, bf16[256,256]{1,0:T(8,128)(2,1)} %pad.8.weight_out), custom_call_target="tpu_custom_call" | custom-call | tf_op jit(solution)/shard_map/hidden/pallas_call | solution.py:771
  114.8 7.9 %aggregate_hidden.1 = bf16[16,128,256]{2,1,0:T(8,128)(2,1)} custom-call(s32[4,16]{1,0:T(4,128)} %bitcast.21, s32[4]{0:T(128)} %bitcast.24, bf16[4,16,128,128]{3,2,1,0:T(8,128)(2,1)} %bitcast.13, bf16[4,2,8,128,256]{4,3,2,1,0:T(8,128)(2,1)} %get-tuple-element.11.sections), custom_call_target="tpu_custom_call" | custom-call | tf_op jit(solution)/shard_map/aggregate_hidden/pallas_call | solution.py:790
  122.7 0.0 copy-done.2
  122.7 0.8 copy.18.labels
  123.5 0.0 copy-done.3
  123.5 0.8 copy.19.mask
  124.3 0.0 copy-done.4
  124.3 0.6 pad.9
  124.8 24.0 %classes.1 = (f32[256,172]{1,0:T(8,128)}, bf16[8,256,256]{2,1,0:T(8,128)(2,1)}) custom-call(bf16[8,256,256]{2,1,0:T(8,128)(2,1)} %bitcast.16, s32[256,1]{1,0:T(8,128)} %copy.18.labels, s32[256,1]{1,0:T(8,128)} %copy.19.mask, f32[1,256]{1,0:T(1,128)} %bitcast.26), custom_call_target="tpu_custom_call" | custom-call | tf_op jit(solution)/shard_map/classes/pallas_call | solution.py:799
  148.9 1.7 copy.20
  150.6 9.0 %aggregate_back.1.parts = bf16[4,2,8,128,256]{4,3,2,1,0:T(8,128)(2,1)} custom-call(s32[4,16]{1,0:T(4,128)} %bitcast.22, s32[4]{0:T(128)} %bitcast.25, bf16[4,16,128,128]{3,2,1,0:T(8,128)(2,1)} %bitcast.14, bf16[16,128,256]{2,1,0:T(8,128)(2,1)} %bitcast.17), custom_call_target="tpu_custom_call" | custom-call | tf_op jit(solution)/shard_map/aggregate_back/pallas_call | solution.py:815
  159.6 118.3 %gradients.1 = (f32[128,256]{1,0:T(8,128)}, f32[256,172]{1,0:T(8,128)}) custom-call(bf16[4,2,8,128,256]{4,3,2,1,0:T(8,128)(2,1)} %aggregate_back.1.parts, bf16[256,128]{1,0:T(8,128)(2,1)} %get-tuple-element.14.z_input, bf16[256,256]{1,0:T(8,128)(2,1)} %get-tuple-element.15.dropped, f32[256,256]{1,0:T(8,128)} %get-tuple-element.16.slope_factor, ...), custom_call_target="tpu_custom_call" | custom-call | tf_op jit(solution)/shard_map/gradients/pallas_call | solution.py:826
  277.9 1.7 copy.21
  279.7 1.6 copy.23
Async XLA Ops:
  0.6 45.7 %copy-start.1 = (s32[1,256]{1,0:T(1,128)S(1)}, s32[1,256]{1,0:T(1,128)}, u32[]{:S(2)}) copy-start(s32[1,256]{1,0:T(1,128)} %param.11) | copy-start | bytes 3076
  0.6 46.5 %copy-start = (bf16[256,172]{0,1:T(8,128)(2,1)S(1)}, bf16[256,172]{0,1:T(8,128)(2,1)}, u32[]{:S(2)}) copy-start(bf16[256,172]{0,1:T(8,128)(2,1)} %param.18) | copy-start | bytes 264196
  47.9 74.7 %copy-start.2 = (s32[1,256]{1,0:T(1,128)S(1)}, s32[1,256]{1,0:T(1,128)}, u32[]{:S(2)}) copy-start(s32[1,256]{1,0:T(1,128)} %param.12) | copy-start | bytes 3076
  47.9 75.5 %copy-start.3 = (s32[1,256]{1,0:T(1,128)S(1)}, s32[1,256]{1,0:T(1,128)}, u32[]{:S(2)}) copy-start(s32[1,256]{1,0:T(1,128)} %param.13) | copy-start | bytes 3076
  47.9 76.3 %copy-start.4 = (f32[172]{0:T(256)S(1)}, f32[172]{0:T(256)}, u32[]{:S(2)}) copy-start(f32[172]{0:T(256)} %param.19) | copy-start | bytes 2068

commit v2 on v1

v2 whole, which is shorter than its diff:
```python
import functools
import math

import jax
import jax.numpy as jnp
from jax import lax
from jax.experimental import pallas as pl
from jax.experimental.pallas import tpu as pltpu
from jax.sharding import PartitionSpec as P

MESH = pl.DeviceIdType.MESH
F32 = jnp.float32
BF16 = jnp.bfloat16
REP = 8
BLK = 32
SEC = 4
TILE = 128
SLOTS = 16
WIDE = 256
CLASSES = 172
LANES = 128
PACKED = 192
DEPTH = 8
VMEM_LIMIT = 56 << 20


def whole():
    return pl.BlockSpec(memory_space=pltpu.VMEM)


def in_smem():
    return pl.BlockSpec(memory_space=pltpu.SMEM)


def params(collective):
    if collective is None:
        return pltpu.CompilerParams(vmem_limit_bytes=VMEM_LIMIT)
    return pltpu.CompilerParams(
        collective_id=collective, has_side_effects=True, vmem_limit_bytes=VMEM_LIMIT
    )


def where_am_i():
    return lax.axis_index("rep"), lax.axis_index("blk")


def remote(source, target, send, arrive, device):
    return pltpu.make_async_remote_copy(
        src_ref=source,
        dst_ref=target,
        send_sem=send,
        recv_sem=arrive,
        device_id=device,
        device_id_type=MESH,
    )


def landed(target, send, arrive, device):
    remote(target, target, send, arrive, device).wait_recv()


def greet(device):
    pl.semaphore_signal(
        pltpu.get_barrier_semaphore(), inc=1, device_id=device, device_id_type=MESH
    )


def greet_group():
    rep, blk = where_am_i()
    for step in range(1, REP):
        greet((lax.rem(rep + step, REP), blk))
    return REP - 1


def blk_of(part, depth, core):
    return (part * (BLK // 4) + depth) * 2 + core


class Spot:
    def __init__(self):
        self.rep = lax.axis_index("rep")
        self.blk = lax.axis_index("blk")
        self.core = lax.rem(self.blk, 2)
        self.depth = lax.rem(self.blk // 2, DEPTH)
        self.part = self.blk // 16
        self.here = (self.rep, self.blk)
        self.up = (self.rep, lax.rem(self.blk + 1, BLK))
        self.down = (self.rep, lax.rem(self.blk + BLK - 1, BLK))
        low_block = lax.rem(self.blk - SEC * self.rep + BLK, BLK)
        high_block = lax.rem(self.blk - SEC * self.rep - (SEC - 1) + 2 * BLK, BLK)
        self.low_relay = (low_block // 16) * 16 + lax.rem(self.blk, 16)
        self.high_relay = blk_of(high_block // 16, self.depth, 1 - self.core)
        self.own_relay = self.low_relay == self.blk

    def line(self, step):
        return (self.rep, blk_of(self.part, lax.rem(self.depth + step + DEPTH, DEPTH), self.core))

    def local(self, piece):
        return jnp.logical_and(self.own_relay, piece == self.rep)

    def targets(self, half, slot):
        offset = 2 * slot + half * (1 + self.core)
        source = blk_of(self.part, lax.rem(self.depth - offset + 2 * DEPTH, DEPTH), self.core)
        for other in (slot, slot + 4):
            yield other, (other, lax.rem(source + (SEC - 1) * half + SEC * other, BLK))


def greet_line(spot):
    for step in (-2, -1, 1, 2):
        greet(spot.line(step))
    return 4


def greet_spread(spot):
    for other in range(REP):
        @pl.when(jnp.logical_not(spot.local(other)))
        def _(other=other):
            greet((other, spot.low_relay))
        greet((other, spot.high_relay))
    greet(spot.up)
    greet(spot.down)
    return greet_line(spot) + 2 * REP + 2 - jnp.where(spot.own_relay, 1, 0)


def greet_fold(spot):
    for slot in range(4):
        for half in range(2):
            for other, device in spot.targets(half, slot):
                if half == 0:
                    same = jnp.logical_and(other == spot.rep, device[1] == spot.blk)

                    @pl.when(jnp.logical_not(same))
                    def _(device=device):
                        greet(device)
                else:
                    greet(device)
    greet(spot.up)
    greet(spot.down)
    return greet_line(spot) + 2 * REP + 2 - jnp.where(spot.own_relay, 1, 0)


def spread(spot, shard, sections, relay, line_send, line_arrive, send, chain_send, arrive):
    rep, blk, core, here = spot.rep, spot.blk, spot.core, spot.here
    dummy = chain_send.at[0, 0, 0]

    def line_copy(half, source, slot, step):
        return remote(
            source,
            relay.at[half, slot],
            line_send.at[half, slot],
            line_arrive.at[half, slot],
            spot.line(step),
        )

    def line_wait(half, slot):
        landed(relay.at[half, slot], dummy, line_arrive.at[half, slot], here)

    def hand_on(half, slot, source):
        section = (SEC - 1) * half
        for other, device in spot.targets(half, slot):
            copy = remote(
                source,
                sections.at[section, half, rep],
                send.at[half, other],
                arrive.at[section, half, rep],
                device,
            )
            if half == 0:
                same = jnp.logical_and(other == rep, device[1] == blk)

                @pl.when(same)
                def _(source=source):
                    sections[0, 0, rep] = source[...]

                @pl.when(jnp.logical_not(same))
                def _(copy=copy):
                    copy.start()
            else:
                copy.start()

    direct = [
        line_copy(0, shard.at[0], 1, 2),
        line_copy(0, shard.at[0], 3, -2),
        line_copy(1, shard.at[1], 0, 1 + core),
        line_copy(1, shard.at[1], 3 - core, -1 - core),
    ]
    for copy in direct:
        copy.start()
    hand_on(0, 0, shard.at[0])

    @pl.when(core == 1)
    def _():
        hand_on(1, 3, shard.at[1])

    line_wait(1, 3 - core)
    back = line_copy(1, relay.at[1, 3 - core], 2 - core, -2)
    back.start()
    line_wait(1, 0)
    forth = line_copy(1, relay.at[1, 0], 1, 2)

    @pl.when(core == 0)
    def _():
        forth.start()

    line_wait(0, 1)
    onward = line_copy(0, relay.at[0, 1], 2, 2)
    onward.start()
    hand_on(1, 0, relay.at[1, 0])
    hand_on(1, 3 - core, relay.at[1, 3 - core])
    hand_on(0, 1, relay.at[0, 1])
    line_wait(0, 3)
    hand_on(0, 3, relay.at[0, 3])
    line_wait(1, 2 - core)
    hand_on(1, 2 - core, relay.at[1, 2 - core])

    @pl.when(core == 0)
    def _():
        line_wait(1, 1)
        hand_on(1, 1, relay.at[1, 1])

    line_wait(0, 2)
    hand_on(0, 2, relay.at[0, 2])

    def hop(index, carry):
        section = index // REP
        step = lax.rem(index, REP)
        piece = lax.rem(rep + REP - step, REP)
        other_section = SEC - 1 - section

        @pl.when(jnp.logical_not(jnp.logical_and(spot.local(piece), section == 0)))
        def _():
            landed(
                sections.at[section, 0, piece], dummy, arrive.at[section, 0, piece], here
            )

        remote(
            sections.at[section, 0, piece],
            sections.at[section + 1, 0, piece],
            chain_send.at[0, section, piece],
            arrive.at[section + 1, 0, piece],
            spot.up,
        ).start()
        landed(
            sections.at[other_section, 1, piece],
            dummy,
            arrive.at[other_section, 1, piece],
            here,
        )
        remote(
            sections.at[other_section, 1, piece],
            sections.at[other_section - 1, 1, piece],
            chain_send.at[1, section, piece],
            arrive.at[other_section - 1, 1, piece],
            spot.down,
        ).start()
        return carry

    lax.fori_loop(0, (SEC - 1) * REP, hop, 0)

    def finish(piece, carry):
        landed(
            sections.at[SEC - 1, 0, piece], dummy, arrive.at[SEC - 1, 0, piece], here
        )
        landed(sections.at[0, 1, piece], dummy, arrive.at[0, 1, piece], here)
        for direction in range(2):
            for section in range(SEC - 1):
                remote(
                    sections.at[0, 1, piece],
                    sections.at[0, 1, piece],
                    chain_send.at[direction, section, piece],
                    arrive.at[0, 1, piece],
                    here,
                ).wait_send()
        return carry

    lax.fori_loop(0, REP, finish, 0)
    for copy in direct:
        copy.wait_send()
    back.wait_send()
    onward.wait_send()

    @pl.when(core == 0)
    def _():
        forth.wait_send()

    for other in range(REP):
        for half in range(2):
            done = remote(
                shard.at[half], shard.at[half], send.at[half, other], arrive.at[0, 0, 0], here
            )
            if half == 0:
                @pl.when(jnp.logical_not(spot.local(other)))
                def _(done=done):
                    done.wait_send()
            else:
                done.wait_send()


def spread_scratch(height):
    dma = pltpu.SemaphoreType.DMA
    return [
        pltpu.VMEM((2, 4, height, LANES), BF16),
        dma((2, 4)),
        dma((2, 4)),
        dma((2, REP)),
        dma((2, SEC - 1, REP)),
        dma((SEC, 2, REP)),
    ]


def fold(
    spot,
    parts,
    low_in,
    high_in,
    low_out,
    high_out,
    final_out,
    final_in,
    line_out,
    line_in,
    chain_send,
    chain_arrive,
    final_send,
    final_arrive,
    line_send,
    line_arrive,
):
    rep, blk, core, here = spot.rep, spot.blk, spot.core, spot.here
    dummy = chain_send.at[0, 0, 0]

    def start(piece, carry):
        remote(
            parts.at[SEC - 1, 0, piece],
            low_in.at[SEC - 2, piece],
            chain_send.at[0, 0, piece],
            chain_arrive.at[0, SEC - 2, piece],
            spot.down,
        ).start()
        remote(
            parts.at[0, 1, piece],
            high_in.at[0, piece],
            chain_send.at[1, 0, piece],
            chain_arrive.at[1, 0, piece],
            spot.up,
        ).start()
        return carry

    lax.fori_loop(0, REP, start, 0)

    def hop(index, carry):
        step = index // REP
        piece = lax.rem(index, REP)
        low_section = SEC - 2 - step
        landed(low_in.at[low_section, piece], dummy, chain_arrive.at[0, low_section, piece], here)
        low_out[low_section, piece] = (
            low_in[low_section, piece].astype(F32) + parts[low_section, 0, piece].astype(F32)
        ).astype(BF16)
        remote(
            low_out.at[low_section, piece],
            low_in.at[low_section - 1, piece],
            chain_send.at[0, step + 1, piece],
            chain_arrive.at[0, low_section - 1, piece],
            spot.down,
        ).start()
        landed(high_in.at[step, piece], dummy, chain_arrive.at[1, step, piece], here)
        high_out[step, piece] = (
            high_in[step, piece].astype(F32) + parts[step + 1, 1, piece].astype(F32)
        ).astype(BF16)
        remote(
            high_out.at[step, piece],
            high_in.at[step + 1, piece],
            chain_send.at[1, step + 1, piece],
            chain_arrive.at[1, step + 1, piece],
            spot.up,
        ).start()
        return carry

    lax.fori_loop(0, (SEC - 2) * REP, hop, 0)

    def final_copy(half, piece):
        return remote(
            final_out.at[half, piece],
            final_in.at[half, rep],
            final_send.at[half, piece],
            final_arrive.at[half, rep],
            (piece, spot.low_relay if half == 0 else spot.high_relay),
        )

    def final(index, carry):
        piece = lax.rem(index + rep, REP)
        landed(low_in.at[0, piece], dummy, chain_arrive.at[0, 0, piece], here)
        final_out[0, piece] = (
            low_in[0, piece].astype(F32) + parts[0, 0, piece].astype(F32)
        ).astype(BF16)

        @pl.when(spot.local(piece))
        def _():
            final_in[0, rep] = final_out[0, piece]

        @pl.when(jnp.logical_not(spot.local(piece)))
        def _():
            final_copy(0, piece).start()

        landed(high_in.at[SEC - 2, piece], dummy, chain_arrive.at[1, SEC - 2, piece], here)
        final_out[1, piece] = (
            high_in[SEC - 2, piece].astype(F32) + parts[SEC - 1, 1, piece].astype(F32)
        ).astype(BF16)
        final_copy(1, piece).start()
        return carry

    lax.fori_loop(0, REP, final, 0)

    def pair(half, slot):
        for other in (slot, slot + 4):
            if half == 0:
                @pl.when(jnp.logical_not(spot.local(other)))
                def _(other=other):
                    landed(
                        final_in.at[0, other], dummy, final_arrive.at[0, other], here
                    )
            else:
                landed(final_in.at[1, other], dummy, final_arrive.at[1, other], here)
        return final_in[half, slot].astype(F32) + final_in[half, slot + 4].astype(F32)

    def line_copy(half, index, step):
        return remote(
            line_out.at[half, index],
            line_in.at[half, index],
            line_send.at[half, index],
            line_arrive.at[half, index],
            spot.line(step),
        )

    def line_wait(half, index):
        landed(line_in.at[half, index], dummy, line_arrive.at[half, index], here)
        return line_in[half, index].astype(F32)

    low_far = line_copy(0, 0, -2)
    line_out[0, 0] = pair(0, 2).astype(BF16)
    low_far.start()
    high_far = line_copy(1, 0, 2)
    line_out[1, 0] = pair(1, 2 - core).astype(BF16)
    high_far.start()
    high_side = line_copy(1, 1, -2)

    @pl.when(core == 0)
    def _():
        line_out[1, 1] = pair(1, 1).astype(BF16)
        high_side.start()

    low_back = line_copy(0, 1, 2)
    line_out[0, 1] = pair(0, 3).astype(BF16)
    low_back.start()
    low_near = line_copy(0, 2, -2)
    line_out[0, 2] = (pair(0, 1) + line_wait(0, 0)).astype(BF16)
    low_near.start()
    high_up = line_copy(1, 2, 1 + core)
    line_out[1, 2] = (pair(1, 3 - core) + line_wait(1, 0)).astype(BF16)
    high_up.start()
    high_down = line_copy(1, 3, -1 - core)

    @pl.when(core == 0)
    def _():
        line_out[1, 3] = (pair(1, 0) + line_wait(1, 1)).astype(BF16)

    @pl.when(core == 1)
    def _():
        line_out[1, 3] = pair(1, 0).astype(BF16)
        line_in[1, 1] = pair(1, 3).astype(BF16)

    high_down.start()
    low = pair(0, 0) + line_wait(0, 1) + line_wait(0, 2)
    high = line_wait(1, 2) + line_wait(1, 3)
    high = high + jnp.where(core == 1, line_in[1, 1].astype(F32), 0.0)

    def drain(piece, carry):
        for direction in range(2):
            for step in range(SEC - 1):
                remote(
                    low_in.at[0, piece],
                    low_in.at[0, piece],
                    chain_send.at[direction, step, piece],
                    dummy,
                    here,
                ).wait_send()

        @pl.when(jnp.logical_not(spot.local(piece)))
        def _():
            final_copy(0, piece).wait_send()

        final_copy(1, piece).wait_send()
        return carry

    lax.fori_loop(0, REP, drain, 0)
    for copy in (low_far, high_far, low_back, low_near, high_up, high_down):
        copy.wait_send()

    @pl.when(core == 0)
    def _():
        high_side.wait_send()

    return low, high


def fold_scratch(height):
    dma = pltpu.SemaphoreType.DMA
    chain = pltpu.VMEM((SEC - 1, REP, height, LANES), BF16)
    final = pltpu.VMEM((2, REP, height, LANES), BF16)
    line = pltpu.VMEM((2, 4, height, LANES), BF16)
    return [
        chain,
        chain,
        chain,
        chain,
        final,
        final,
        line,
        line,
        dma((2, SEC - 1, REP)),
        dma((2, SEC - 1, REP)),
        dma((2, REP)),
        dma((2, REP)),
        dma((2, 4)),
        dma((2, 4)),
    ]


def pack(values):
    half = TILE // 2
    lanes = lax.broadcasted_iota(jnp.int32, (half, LANES), 1)
    rest = jnp.where(
        lanes < half,
        values[:half, LANES:],
        pltpu.roll(values[half:, LANES:], half, 1),
    )
    return jnp.concatenate([values[:, :LANES], rest], axis=0).astype(BF16)


def unpack(packed):
    half = TILE // 2
    rest = packed[TILE:]
    turned = jnp.concatenate([rest[:, half:], rest[:, :half]], axis=1)
    return jnp.concatenate(
        [packed[:TILE], jnp.concatenate([rest, turned], axis=0)], axis=1
    )


def group_send(pieces, landing, send, arrive):
    rep, blk = where_am_i()
    for step in range(1, REP):
        other = lax.rem(rep + step, REP)
        remote(
            pieces.at[other], landing.at[rep], send.at[other], arrive.at[rep], (other, blk)
        ).start()


def group_wait(pieces, landing, send, arrive):
    rep, blk = where_am_i()
    for step in range(1, REP):
        other = lax.rem(rep + step, REP)
        copy = remote(
            pieces.at[other], landing.at[other], send.at[other], arrive.at[other], (other, blk)
        )
        copy.wait_recv()
        copy.wait_send()


def group_sum(pieces, landing):
    rep, blk = where_am_i()
    landing[rep] = pieces[rep]
    total = landing[0].astype(F32)
    for index in range(1, REP):
        total = total + landing[index].astype(F32)
    return total


GROUP_SEMS = (pltpu.SemaphoreType.DMA((REP,)), pltpu.SemaphoreType.DMA((REP,)))


def keep_factor(ids):
    columns = lax.broadcasted_iota(jnp.int32, (1, WIDE), 1)
    mixed = ids * 73244475 + columns * 19349663 + 12345
    mixed = mixed ^ jnp.right_shift(mixed, 15)
    mixed = mixed * 40503
    mixed = mixed ^ jnp.right_shift(mixed, 13)
    return jnp.where(jnp.bitwise_and(mixed, 3) != 0, F32(4.0 / 3.0), F32(0.0))


def first_kernel(x, sections, *spread_refs):
    spot = Spot()
    waits = greet_spread(spot)
    pl.semaphore_wait(pltpu.get_barrier_semaphore(), waits)
    spread(spot, x, sections, *spread_refs)


def forward_kernel(place, count, tiles, sections, out, total):
    total[...] = jnp.zeros_like(total)
    for section in range(SEC):
        live = count[section]
        for group in range(SLOTS // 4):
            @pl.when(group * 4 < live)
            def _(section=section, group=group):
                for slot in range(group * 4, group * 4 + 4):
                    spot = place[section, slot]
                    row = spot // SLOTS
                    column = lax.rem(spot, SLOTS)
                    source = sections[section, lax.rem(column, 2), column // 2]
                    if source.shape[0] == PACKED:
                        source = unpack(source)
                    product = jnp.dot(
                        tiles[section, slot], source, preferred_element_type=F32
                    )
                    flag = jnp.where(slot < live, F32(1.0), F32(0.0))
                    total[row] = total[row] + product * flag
    if out.shape[1] == PACKED:
        for row in range(out.shape[0]):
            out[row] = pack(total[row])
    else:
        out[...] = total[...]


def backward_kernel(place, count, tiles, rows, out, total):
    total[...] = jnp.zeros_like(total)
    for section in range(SEC):
        live = count[section]
        for group in range(SLOTS // 4):
            @pl.when(group * 4 < live)
            def _(section=section, group=group):
                for slot in range(group * 4, group * 4 + 4):
                    spot = place[section, slot]
                    row = spot // SLOTS
                    column = lax.rem(spot, SLOTS)
                    product = lax.dot_general(
                        tiles[section, slot],
                        unpack(rows[row]),
                        (((0,), (0,)), ((), ())),
                        preferred_element_type=F32,
                    )
                    flag = jnp.where(slot < live, F32(1.0), F32(0.0))
                    half = lax.rem(column, 2)
                    piece = column // 2
                    total[section, half, piece] = total[section, half, piece] + product * flag
    for section in range(SEC):
        for piece in range(REP):
            for half in range(2):
                out[section, half, piece] = pack(total[section, half, piece])


def hidden_kernel(
    partial,
    ids,
    weight_in,
    weight_out,
    z_out,
    dropped_out,
    slope_factor,
    sections,
    landing,
    shard,
    group_sems_send,
    group_sems_arrive,
    *spread_refs,
):
    spot = Spot()
    waits = greet_group() + greet_spread(spot)
    pl.semaphore_wait(pltpu.get_barrier_semaphore(), waits)
    group_send(partial, landing, group_sems_send, group_sems_arrive)
    group_wait(partial, landing, group_sems_send, group_sems_arrive)
    z_input = group_sum(partial, landing).astype(BF16)
    z_out[...] = z_input
    pre_act = jnp.dot(z_input, weight_in[...], preferred_element_type=F32)
    kept = keep_factor(ids[...])
    dropped = (jnp.maximum(pre_act, 0.0) * kept).astype(BF16)
    dropped_out[...] = dropped
    slope_factor[...] = jnp.where(pre_act > 0, kept, 0.0)
    mapped = jnp.dot(dropped, weight_out[...], preferred_element_type=F32)
    shard[0] = pack(mapped[:TILE])
    shard[1] = pack(mapped[TILE:])
    spread(spot, shard, sections, *spread_refs)


def class_kernel(
    scale,
    partial,
    labels,
    mask,
    bias,
    logits_out,
    slopes,
    landing,
    send,
    arrive,
    slope_send,
    slope_arrive,
):
    waits = greet_group()
    rep, blk = where_am_i()
    pl.semaphore_wait(pltpu.get_barrier_semaphore(), waits)
    group_send(partial, landing, send, arrive)
    group_wait(partial, landing, send, arrive)
    summed = group_sum(partial, landing)
    logits = jnp.concatenate([unpack(summed[:PACKED]), unpack(summed[PACKED:])], axis=0) + bias[...]
    logits_out[...] = logits[:, :CLASSES]
    columns = lax.broadcasted_iota(jnp.int32, logits.shape, 1)
    real = columns < CLASSES
    top = jnp.max(jnp.where(real, logits, -jnp.inf), axis=1, keepdims=True)
    powers = jnp.where(real, jnp.exp(logits - top), 0.0)
    likelihood = powers / jnp.sum(powers, axis=1, keepdims=True)
    onehot = jnp.where(columns == labels[...], 1.0, 0.0)
    slope = (likelihood - onehot) * mask[...].astype(F32) * scale
    slopes[rep] = jnp.concatenate([pack(slope[:TILE]), pack(slope[TILE:])], axis=0)
    for step in range(1, REP):
        other = lax.rem(rep + step, REP)
        remote(
            slopes.at[rep], slopes.at[rep], slope_send.at[other], slope_arrive.at[rep], (other, blk)
        ).start()
    for step in range(1, REP):
        other = lax.rem(rep + step, REP)
        copy = remote(
            slopes.at[rep], slopes.at[other], slope_send.at[other], slope_arrive.at[other], (other, blk)
        )
        copy.wait_recv()
        copy.wait_send()


def last_kernel(
    parts,
    z_input,
    dropped,
    slope_factor,
    weight_out,
    grad_in,
    grad_out,
    terms,
    landing,
    corner,
    corner_in,
    depth_in,
    full_corner,
    full,
    a_send,
    a_arrive,
    b_send,
    b_arrive,
    c_send,
    c_arrive,
    d_send,
    d_arrive,
    e_send,
    e_arrive,
    *fold_refs,
):
    spot = Spot()
    rep, blk, core, depth, part = spot.rep, spot.blk, spot.core, spot.depth, spot.part
    waits = greet_group() + greet_fold(spot)
    corner_me = part * 2 + core
    for step in range(1, 4):
        other = lax.rem(corner_me + step, 4)
        greet((rep, blk_of(other // 2, depth, lax.rem(other, 2))))
    for step in range(1, 8):
        greet((rep, blk_of(part, lax.rem(depth + step, 8), core)))
    pl.semaphore_wait(pltpu.get_barrier_semaphore(), waits + 10)

    low, high = fold(spot, parts, *fold_refs)
    back = jnp.concatenate([unpack(low.astype(BF16)), unpack(high.astype(BF16))], axis=0)
    out_terms = lax.dot_general(
        dropped[...], back, (((0,), (0,)), ((), ())), preferred_element_type=F32
    )
    back_rows = lax.dot_general(
        back, weight_out[...], (((1,), (1,)), ((), ())), preferred_element_type=F32
    )
    pre_slope = (back_rows * slope_factor[...]).astype(BF16)
    in_terms = lax.dot_general(
        z_input[...], pre_slope, (((0,), (0,)), ((), ())), preferred_element_type=F32
    )
    in_rows = in_terms.shape[0]
    chunk = (in_rows + WIDE) // REP
    joined = jnp.concatenate([in_terms, out_terms], axis=0)
    for index in range(REP):
        terms[index] = joined[index * chunk : (index + 1) * chunk]
    group_send(terms, landing, a_send, a_arrive)
    group_wait(terms, landing, a_send, a_arrive)
    total = group_sum(terms, landing)
    for index in range(12):
        corner[index // 3, index % 3] = total[
            (index // 2) * 8 : (index // 2) * 8 + 8, (index % 2) * 128 : (index % 2) * 128 + 128
        ]

    def corner_device(index):
        return (rep, blk_of(index // 2, depth, lax.rem(index, 2)))

    for step in range(1, 4):
        other = lax.rem(corner_me + step, 4)
        remote(
            corner.at[other],
            corner_in.at[corner_me],
            b_send.at[other],
            b_arrive.at[corner_me],
            corner_device(other),
        ).start()
    for step in range(1, 4):
        other = lax.rem(corner_me + step, 4)
        copy = remote(
            corner.at[other],
            corner_in.at[other],
            b_send.at[other],
            b_arrive.at[other],
            corner_device(other),
        )
        copy.wait_recv()
        copy.wait_send()
    corner_in[corner_me] = corner[corner_me]
    total = corner_in[0] + corner_in[1] + corner_in[2] + corner_in[3]
    depth_in[depth] = total
    for step in range(1, 8):
        other = lax.rem(depth + step, 8)
        remote(
            depth_in.at[depth],
            depth_in.at[depth],
            c_send.at[other],
            c_arrive.at[depth],
            (rep, blk_of(part, other, core)),
        ).start()
    for step in range(1, 8):
        other = lax.rem(depth + step, 8)
        copy = remote(
            depth_in.at[depth],
            depth_in.at[other],
            c_send.at[other],
            c_arrive.at[other],
            (rep, blk_of(part, other, core)),
        )
        copy.wait_recv()
        copy.wait_send()
    total = depth_in[0]
    for index in range(1, 8):
        total = total + depth_in[index]
    full_corner[corner_me] = total
    for step in range(1, 4):
        other = lax.rem(corner_me + step, 4)
        remote(
            full_corner.at[corner_me],
            full_corner.at[corner_me],
            d_send.at[other],
            d_arrive.at[corner_me],
            corner_device(other),
        ).start()
    for step in range(1, 4):
        other = lax.rem(corner_me + step, 4)
        copy = remote(
            full_corner.at[corner_me],
            full_corner.at[other],
            d_send.at[other],
            d_arrive.at[other],
            corner_device(other),
        )
        copy.wait_recv()
        copy.wait_send()
    full[rep] = full_corner[...]
    for step in range(1, REP):
        other = lax.rem(rep + step, REP)
        remote(full.at[rep], full.at[rep], e_send.at[other], e_arrive.at[rep], (other, blk)).start()
    for step in range(1, REP):
        other = lax.rem(rep + step, REP)
        copy = remote(
            full.at[rep], full.at[other], e_send.at[other], e_arrive.at[other], (other, blk)
        )
        copy.wait_recv()
        copy.wait_send()
    for index in range(REP * 6):
        group, inner = index // 6, index % 6
        left, right = 2 * inner, 2 * inner + 1
        row = jnp.concatenate(
            [full[group, left // 3, left % 3], full[group, right // 3, right % 3]], axis=1
        )
        if index * 8 < in_rows:
            grad_in[index * 8 : index * 8 + 8, :] = row
        else:
            start_row = index * 8 - in_rows
            grad_out[start_row : start_row + 8, :] = row[:, :CLASSES]


def on_device(
    features,
    node_ids,
    labels,
    train_mask,
    tile_values,
    tile_place,
    tile_count,
    weight_in,
    weight_out,
    class_bias,
):
    width = features.shape[-1]
    own_rows = features.shape[1]
    scale = 1.0 / math.sqrt(own_rows * REP * BLK)
    tiles = tile_values[0, 0]
    place = tile_place[0, 0]
    count = tile_count[0, 0]
    shape = jax.ShapeDtypeStruct
    padded_out = jnp.pad(weight_out, ((0, 0), (0, WIDE - CLASSES)))
    padded_bias = jnp.pad(class_bias, (0, WIDE - CLASSES))[None, :]
    ids = node_ids.reshape(own_rows, 1)
    label_column = labels.reshape(own_rows, 1)
    mask_column = train_mask.reshape(own_rows, 1)

    sections = pl.pallas_call(
        first_kernel,
        out_shape=shape((SEC, 2, REP, TILE, width), BF16),
        in_specs=[whole()],
        out_specs=whole(),
        scratch_shapes=spread_scratch(TILE),
        compiler_params=params(0),
        name="spread_features",
    )(features.reshape(2, TILE, width))
    partial = pl.pallas_call(
        forward_kernel,
        out_shape=shape((2 * REP, TILE, width), F32),
        in_specs=[in_smem(), in_smem(), whole(), whole()],
        out_specs=whole(),
        scratch_shapes=[pltpu.VMEM((2 * REP, TILE, width), F32)],
        compiler_params=params(None),
        name="aggregate_features",
    )(place, count, tiles, sections)
    z_input, dropped, slope_factor, sections = pl.pallas_call(
        hidden_kernel,
        out_shape=(
            shape((own_rows, width), BF16),
            shape((own_rows, WIDE), BF16),
            shape((own_rows, WIDE), F32),
            shape((SEC, 2, REP, PACKED, LANES), BF16),
        ),
        in_specs=[whole()] * 4,
        out_specs=[whole()] * 4,
        scratch_shapes=[
            pltpu.VMEM((REP, own_rows, width), F32),
            pltpu.VMEM((2, PACKED, LANES), BF16),
            *GROUP_SEMS,
            *spread_scratch(PACKED),
        ],
        compiler_params=params(1),
        name="hidden",
    )(partial.reshape(REP, own_rows, width), ids, weight_in, padded_out)
    partial = pl.pallas_call(
        forward_kernel,
        out_shape=shape((2 * REP, PACKED, LANES), BF16),
        in_specs=[in_smem(), in_smem(), whole(), whole()],
        out_specs=whole(),
        scratch_shapes=[pltpu.VMEM((2 * REP, TILE, WIDE), F32)],
        compiler_params=params(None),
        name="aggregate_hidden",
    )(place, count, tiles, sections)
    logits, slopes = pl.pallas_call(
        functools.partial(class_kernel, scale),
        out_shape=(
            shape((own_rows, CLASSES), F32),
            shape((REP, 2 * PACKED, LANES), BF16),
        ),
        in_specs=[whole()] * 4,
        out_specs=[whole()] * 2,
        scratch_shapes=[
            pltpu.VMEM((REP, 2 * PACKED, LANES), BF16),
            *GROUP_SEMS,
            *GROUP_SEMS,
        ],
        compiler_params=params(2),
        name="classes",
    )(partial.reshape(REP, 2 * PACKED, LANES), label_column, mask_column, padded_bias)
    parts = pl.pallas_call(
        backward_kernel,
        out_shape=shape((SEC, 2, REP, PACKED, LANES), BF16),
        in_specs=[in_smem(), in_smem(), whole(), whole()],
        out_specs=whole(),
        scratch_shapes=[pltpu.VMEM((SEC, 2, REP, TILE, WIDE), F32)],
        compiler_params=params(None),
        name="aggregate_back",
    )(place, count, tiles, slopes.reshape(2 * REP, PACKED, LANES))
    chunk = (width + WIDE) // REP
    dma = pltpu.SemaphoreType.DMA
    grad_in, grad_out = pl.pallas_call(
        last_kernel,
        out_shape=(shape((width, WIDE), F32), shape((WIDE, CLASSES), F32)),
        in_specs=[whole()] * 5,
        out_specs=[whole()] * 2,
        scratch_shapes=[
            pltpu.VMEM((REP, chunk, WIDE), F32),
            pltpu.VMEM((REP, chunk, WIDE), F32),
            pltpu.VMEM((4, 3, 8, 128), F32),
            pltpu.VMEM((4, 3, 8, 128), F32),
            pltpu.VMEM((8, 3, 8, 128), F32),
            pltpu.VMEM((4, 3, 8, 128), F32),
            pltpu.VMEM((REP, 4, 3, 8, 128), F32),
            dma((REP,)),
            dma((REP,)),
            dma((4,)),
            dma((4,)),
            dma((8,)),
            dma((8,)),
            dma((4,)),
            dma((4,)),
            dma((REP,)),
            dma((REP,)),
            *fold_scratch(PACKED),
        ],
        compiler_params=params(3),
        name="gradients",
    )(parts, z_input, dropped, slope_factor, padded_out)
    return (logits[None], grad_in, grad_out)


def solution(mesh):
    placed = (
        P("blk", "rep", None),
        P("blk", "rep"),
        P("blk", "rep"),
        P("blk", "rep"),
        P("blk", "rep", None, None, None, None),
        P("blk", "rep", None, None),
        P("blk", "rep", None),
        P(),
        P(),
        P(),
    )
    return jax.shard_map(
        on_device,
        mesh=mesh,
        in_specs=placed,
        out_specs=(P("blk", "rep", None), P(), P()),
        check_vma=False,
    )
```

time: 282 us -> 238 us (0.84)
  Pallas kernels: 272 us -> 229 us
    pallas_call x1, Pallas kernels: 118 us -> 83.4 us  [on_device(): pl.pallas_call(last_kernel, out_shape=(shape((width, WIDE), F32), shape((...]
    pallas_call x1, Pallas kernels: 24 us -> 35 us  [on_device(): pl.pallas_call(functools.partial(class_kernel, scale), out_shape=(shape((...]
    pallas_call x1, Pallas kernels: 66.8 us -> 57.7 us  [on_device(): pl.pallas_call(hidden_kernel, out_shape=(shape((own_rows, width), BF16),...]
    pallas_call x2, Pallas kernels: 16.8 us -> 12.7 us  [the longest x1 6.84 us: on_device(): pl.pallas_call(backward_kernel, out_shape=shape((SEC, 2, REP, PACKED, LAN...]
    pallas_call x1, Pallas kernels: 39.1 us -> 35.3 us  [on_device(): pl.pallas_call(first_kernel, out_shape=shape((SEC, 2, REP, TILE, width),...]
where the time goes in v2:
time: 238 us
  Pallas kernels  229 us (96%)
  local copies, waits for them, and re-layouts  7.87 us (3%)
    pallas_call x1, Pallas kernels, on_device(): pl.pallas_call(last_kernel, out_shape=(shape((width, WIDE), F32), shape((...  83.4 us
    pallas_call x1, Pallas kernels, on_device(): pl.pallas_call(hidden_kernel, out_shape=(shape((own_rows, width), BF16),...  57.7 us
    pallas_call x1, Pallas kernels, on_device(): pl.pallas_call(first_kernel, out_shape=shape((SEC, 2, REP, TILE, width),...  35.3 us
    pallas_call x1, Pallas kernels, on_device(): pl.pallas_call(functools.partial(class_kernel, scale), out_shape=(shape((...  35 us
    pallas_call x1, Pallas kernels, on_device(): pl.pallas_call(backward_kernel, out_shape=shape((SEC, 2, REP, PACKED, LAN...  6.84 us
    pallas_call x1, Pallas kernels, on_device(): pl.pallas_call(forward_kernel, out_shape=shape((2 * REP, PACKED, LANES),...  5.85 us
    pallas_call x1, Pallas kernels, on_device(): pl.pallas_call(forward_kernel, out_shape=shape((2 * REP, TILE, width), F3...  4.83 us

profile of v2, /device:TPU:1, one launch (start us, length us, event | category | flops | bytes accessed | tf_op | source)
XLA Modules:
  0.0 237.5 jit_solution(7191287187400186838)
XLA Ops:
  0.6 35.3 %spread_features.1.sections = bf16[4,2,8,128,128]{4,3,2,1,0:T(8,128)(2,1)} custom-call(bf16[2,128,128]{2,1,0:T(8,128)(2,1)} %bitcast.19), custom_call_target="tpu_custom_call" | custom-call | tf_op jit(solution)/shard_map/spread_features/pallas_call | solution.py:909
  35.9 0.0 copy-start.1
  36.0 0.0 copy-start.2
  36.0 4.8 %aggregate_features.1 = f32[16,128,128]{2,1,0:T(8,128)} custom-call(s32[4,16]{1,0:T(4,128)} %bitcast.20, s32[4]{0:T(128)} %bitcast.23, bf16[4,16,128,128]{3,2,1,0:T(8,128)(2,1)} %bitcast.12, bf16[4,2,8,128,128]{4,3,2,1,0:T(8,128)(2,1)} %spread_features.1.sections), custom_call_target="tpu_custom_call" | custom-call | tf_op jit(solution)/shard_map/aggregate_features/pallas_call | solution.py:918
  40.8 0.0 copy-done.1
  40.8 0.1 copy.16
  40.9 0.7 pad.8.weight_out
  41.6 0.0 copy-done.2
  41.6 0.8 copy.17.ids
  42.4 57.7 %hidden.1 = (bf16[256,128]{1,0:T(8,128)(2,1)}, bf16[256,256]{1,0:T(8,128)(2,1)}, f32[256,256]{1,0:T(8,128)}, bf16[4,2,8,192,128]{4,3,2,1,0:T(8,128)(2,1)}) custom-call(f32[8,256,128]{2,1,0:T(8,128)} %bitcast.15, s32[256,1]{1,0:T(8,128)} %copy.17.ids, bf16[128,256]{1,0:T(8,128)(2,1)} %weight_in.1, bf16[256,256]{1,0:T(8,128)(2,1)} %pad.8.weight_out), custom_call_target="tpu_custom_call" | custom-call | tf_op jit(solution)/shard_map/hidden/pallas_call | solution.py:927
  100.1 0.0 copy-start.3
  100.1 0.0 copy-start.4
  100.1 0.0 copy-start.5
  100.1 5.8 %aggregate_hidden.1 = bf16[16,192,128]{2,1,0:T(8,128)(2,1)} custom-call(s32[4,16]{1,0:T(4,128)} %bitcast.21, s32[4]{0:T(128)} %bitcast.24, bf16[4,16,128,128]{3,2,1,0:T(8,128)(2,1)} %bitcast.13, bf16[4,2,8,192,128]{4,3,2,1,0:T(8,128)(2,1)} %get-tuple-element.11.sections), custom_call_target="tpu_custom_call" | custom-call | tf_op jit(solution)/shard_map/aggregate_hidden/pallas_call | solution.py:946
  106.0 0.0 copy-done.3
  106.0 0.8 copy.18.labels
  106.8 0.0 copy-done.4
  106.8 0.8 copy.19.mask
  107.6 0.0 copy-done.5
  107.6 0.6 pad.9
  108.2 35.0 %classes.1 = (f32[256,172]{1,0:T(8,128)}, bf16[8,384,128]{2,1,0:T(8,128)(2,1)}) custom-call(bf16[8,384,128]{2,1,0:T(8,128)(2,1)} %bitcast.16, s32[256,1]{1,0:T(8,128)} %copy.18.labels, s32[256,1]{1,0:T(8,128)} %copy.19.mask, f32[1,256]{1,0:T(1,128)} %bitcast.26), custom_call_target="tpu_custom_call" | custom-call | tf_op jit(solution)/shard_map/classes/pallas_call | solution.py:955
  143.2 6.8 %aggregate_back.1.parts = bf16[4,2,8,192,128]{4,3,2,1,0:T(8,128)(2,1)} custom-call(s32[4,16]{1,0:T(4,128)} %bitcast.22, s32[4]{0:T(128)} %bitcast.25, bf16[4,16,128,128]{3,2,1,0:T(8,128)(2,1)} %bitcast.14, bf16[16,192,128]{2,1,0:T(8,128)(2,1)} %bitcast.17), custom_call_target="tpu_custom_call" | custom-call | tf_op jit(solution)/shard_map/aggregate_back/pallas_call | solution.py:971
  150.0 0.0 copy-start
  150.0 83.4 %gradients.1 = (f32[128,256]{1,0:T(8,128)}, f32[256,172]{1,0:T(8,128)}) custom-call(bf16[4,2,8,192,128]{4,3,2,1,0:T(8,128)(2,1)} %aggregate_back.1.parts, bf16[256,128]{1,0:T(8,128)(2,1)} %get-tuple-element.14.z_input, bf16[256,256]{1,0:T(8,128)(2,1)} %get-tuple-element.15.dropped, f32[256,256]{1,0:T(8,128)} %get-tuple-element.16.slope_factor, ...), custom_call_target="tpu_custom_call" | custom-call | tf_op jit(solution)/shard_map/gradients/pallas_call | solution.py:982
  233.4 1.7 copy.21
  235.2 0.0 copy-done
  235.2 0.8 copy.20
  236.0 1.6 copy.23
Async XLA Ops:
  35.9 4.9 %copy-start.1 = (bf16[256,172]{0,1:T(8,128)(2,1)S(1)}, bf16[256,172]{0,1:T(8,128)(2,1)}, u32[]{:S(2)}) copy-start(bf16[256,172]{0,1:T(8,128)(2,1)} %param.18) | copy-start | bytes 264196
  36.0 5.6 %copy-start.2 = (s32[1,256]{1,0:T(1,128)S(1)}, s32[1,256]{1,0:T(1,128)}, u32[]{:S(2)}) copy-start(s32[1,256]{1,0:T(1,128)} %param.11) | copy-start | bytes 3076
  100.1 5.9 %copy-start.3 = (s32[1,256]{1,0:T(1,128)S(1)}, s32[1,256]{1,0:T(1,128)}, u32[]{:S(2)}) copy-start(s32[1,256]{1,0:T(1,128)} %param.12) | copy-start | bytes 3076
  100.1 6.7 %copy-start.4 = (s32[1,256]{1,0:T(1,128)S(1)}, s32[1,256]{1,0:T(1,128)}, u32[]{:S(2)}) copy-start(s32[1,256]{1,0:T(1,128)} %param.13) | copy-start | bytes 3076
  100.1 7.5 %copy-start.5 = (f32[172]{0:T(256)S(1)}, f32[172]{0:T(256)}, u32[]{:S(2)}) copy-start(f32[172]{0:T(256)} %param.19) | copy-start | bytes 2068
  150.0 85.1 %copy-start = (f32[256,172]{1,0:T(8,128)S(1)}, f32[256,172]{1,0:T(8,128)}, u32[]{:S(2)}) copy-start(f32[256,172]{1,0:T(8,128)} %get-tuple-element.12) | copy-start | bytes 528388

commit v3 on v0

v3 whole, which is shorter than its diff:
```python
import math

import jax
import jax.numpy as jnp
from jax import lax
from jax.experimental import pallas as pl
from jax.experimental.pallas import tpu as pltpu
from jax.sharding import PartitionSpec as P

MESH = pl.DeviceIdType.MESH
F32 = jnp.float32
BF16 = jnp.bfloat16
REP = 8
BLK = 32
SEC = 4
TILE = 128
SLOTS = 16
WIDE = 256
CLASSES = 172
LANES = 128
PACKED = 192
DEPTH = 8
NONE = SEC * SLOTS
FORWARD_ORDER = (1, 2, 0, 3)
BACKWARD_ORDER = (3, 0, 2, 1)
VMEM_LIMIT = 60 << 20


def whole():
    return pl.BlockSpec(memory_space=pltpu.VMEM)


def remote(source, target, send, arrive, device):
    return pltpu.make_async_remote_copy(
        src_ref=source,
        dst_ref=target,
        send_sem=send,
        recv_sem=arrive,
        device_id=device,
        device_id_type=MESH,
    )


def landed(target, send, arrive, device):
    remote(target, target, send, arrive, device).wait_recv()


def greet(device):
    pl.semaphore_signal(
        pltpu.get_barrier_semaphore(), inc=1, device_id=device, device_id_type=MESH
    )


def blk_of(part, depth, core):
    return (part * (BLK // 4) + depth) * 2 + core


class Spot:
    def __init__(self):
        self.rep = lax.axis_index("rep")
        self.blk = lax.axis_index("blk")
        self.core = lax.rem(self.blk, 2)
        self.depth = lax.rem(self.blk // 2, DEPTH)
        self.part = self.blk // 16
        self.here = (self.rep, self.blk)
        self.up = (self.rep, lax.rem(self.blk + 1, BLK))
        self.down = (self.rep, lax.rem(self.blk + BLK - 1, BLK))
        low_block = lax.rem(self.blk - SEC * self.rep + BLK, BLK)
        high_block = lax.rem(self.blk - SEC * self.rep - (SEC - 1) + 2 * BLK, BLK)
        self.low_relay = (low_block // 16) * 16 + lax.rem(self.blk, 16)
        self.high_relay = blk_of(high_block // 16, self.depth, 1 - self.core)
        self.own_relay = self.low_relay == self.blk
        self.corner = self.part * 2 + self.core

    def line(self, step):
        return (self.rep, blk_of(self.part, lax.rem(self.depth + step + DEPTH, DEPTH), self.core))

    def corner_device(self, index):
        return (self.rep, blk_of(index // 2, self.depth, lax.rem(index, 2)))

    def local(self, piece):
        return jnp.logical_and(self.own_relay, piece == self.rep)

    def targets(self, half, slot):
        offset = 2 * slot + half * (1 + self.core)
        source = blk_of(self.part, lax.rem(self.depth - offset + 2 * DEPTH, DEPTH), self.core)
        for other in (slot, slot + 4):
            yield other, (other, lax.rem(source + (SEC - 1) * half + SEC * other, BLK))


def greet_everyone(spot):
    for step in range(1, REP):
        greet((lax.rem(spot.rep + step, REP), spot.blk))
    for step in range(1, DEPTH):
        greet(spot.line(step))
    for step in range(1, 4):
        greet(spot.corner_device(lax.rem(spot.corner + step, 4)))
    for other in range(REP):
        @pl.when(jnp.logical_not(spot.local(other)))
        def _(other=other):
            greet((other, spot.low_relay))

        greet((other, spot.high_relay))
    for slot in range(4):
        for half in range(2):
            for other, device in spot.targets(half, slot):
                if half == 0:
                    same = jnp.logical_and(other == spot.rep, device[1] == spot.blk)

                    @pl.when(jnp.logical_not(same))
                    def _(device=device):
                        greet(device)
                else:
                    greet(device)
    greet(spot.up)
    greet(spot.down)
    count = (REP - 1) + (DEPTH - 1) + 3 + 4 * REP + 2
    return count - jnp.where(spot.own_relay, 2, 0)


class Spread:
    def __init__(self, spot, shard, sections, relay, line_send, line_arrive, send, chain_send, arrive):
        self.spot, self.shard, self.sections, self.relay = spot, shard, sections, relay
        self.line_send, self.line_arrive, self.send = line_send, line_arrive, send
        self.chain_send, self.arrive = chain_send, arrive
        self.dummy = chain_send.at[0, 0, 0]

    def line_copy(self, half, source, slot, step):
        return remote(
            source,
            self.relay.at[half, slot],
            self.line_send.at[half, slot],
            self.line_arrive.at[half, slot],
            self.spot.line(step),
        )

    def line_wait(self, half, slot):
        landed(
            self.relay.at[half, slot], self.dummy, self.line_arrive.at[half, slot], self.spot.here
        )

    def hand_on(self, half, slot, source):
        spot = self.spot
        section = (SEC - 1) * half
        for other, device in spot.targets(half, slot):
            copy = remote(
                source,
                self.sections[section].at[half * REP + spot.rep],
                self.send.at[half, other],
                self.arrive.at[section, half, spot.rep],
                device,
            )
            if half == 0:
                same = jnp.logical_and(other == spot.rep, device[1] == spot.blk)

                @pl.when(same)
                def _(source=source):
                    self.sections[0][spot.rep] = source[...]

                @pl.when(jnp.logical_not(same))
                def _(copy=copy):
                    copy.start()
            else:
                copy.start()

    def start_low(self):
        self.low = [
            self.line_copy(0, self.shard.at[0], 1, 2),
            self.line_copy(0, self.shard.at[0], 3, -2),
        ]
        for copy in self.low:
            copy.start()
        self.hand_on(0, 0, self.shard.at[0])

    def start_high(self):
        core = self.spot.core
        self.high = [
            self.line_copy(1, self.shard.at[1], 0, 1 + core),
            self.line_copy(1, self.shard.at[1], 3 - core, -1 - core),
        ]
        for copy in self.high:
            copy.start()

        @pl.when(core == 1)
        def _():
            self.hand_on(1, 3, self.shard.at[1])

    def pass_on(self):
        core, relay = self.spot.core, self.relay
        self.line_wait(0, 1)
        self.onward = self.line_copy(0, relay.at[0, 1], 2, 2)
        self.onward.start()
        self.hand_on(0, 1, relay.at[0, 1])
        self.line_wait(0, 3)
        self.hand_on(0, 3, relay.at[0, 3])
        self.line_wait(1, 3 - core)
        self.back = self.line_copy(1, relay.at[1, 3 - core], 2 - core, -2)
        self.back.start()
        self.line_wait(1, 0)
        self.forth = self.line_copy(1, relay.at[1, 0], 1, 2)

        @pl.when(core == 0)
        def _():
            self.forth.start()

        self.hand_on(1, 0, relay.at[1, 0])
        self.hand_on(1, 3 - core, relay.at[1, 3 - core])
        self.line_wait(0, 2)
        self.hand_on(0, 2, relay.at[0, 2])
        self.line_wait(1, 2 - core)
        self.hand_on(1, 2 - core, relay.at[1, 2 - core])

        @pl.when(core == 0)
        def _():
            self.line_wait(1, 1)
            self.hand_on(1, 1, relay.at[1, 1])

    def arrived(self, section, half, piece):
        landed(
            self.sections[section].at[half * REP + piece],
            self.dummy,
            self.arrive.at[section, half, piece],
            self.spot.here,
        )

    def chains(self):
        spot = self.spot
        for section in range(SEC - 1):
            other_section = SEC - 1 - section

            def hop(step, carry, section=section, other_section=other_section):
                piece = lax.rem(spot.rep + REP - step, REP)
                if section == 0:
                    @pl.when(jnp.logical_not(spot.local(piece)))
                    def _():
                        self.arrived(section, 0, piece)
                else:
                    self.arrived(section, 0, piece)
                remote(
                    self.sections[section].at[piece],
                    self.sections[section + 1].at[piece],
                    self.chain_send.at[0, section, piece],
                    self.arrive.at[section + 1, 0, piece],
                    spot.up,
                ).start()
                self.arrived(other_section, 1, piece)
                remote(
                    self.sections[other_section].at[REP + piece],
                    self.sections[other_section - 1].at[REP + piece],
                    self.chain_send.at[1, section, piece],
                    self.arrive.at[other_section - 1, 1, piece],
                    spot.down,
                ).start()
                return carry

            lax.fori_loop(0, REP, hop, 0)

    def last_arrivals(self):
        def finish(piece, carry):
            self.arrived(SEC - 1, 0, piece)
            self.arrived(0, 1, piece)
            return carry

        lax.fori_loop(0, REP, finish, 0)

    def drain(self):
        spot = self.spot
        sample = self.shard.at[0]

        def sent(semaphore):
            remote(sample, sample, semaphore, self.arrive.at[0, 0, 0], spot.here).wait_send()

        def body(piece, carry):
            for direction in range(2):
                for section in range(SEC - 1):
                    sent(self.chain_send.at[direction, section, piece])

            @pl.when(jnp.logical_not(spot.local(piece)))
            def _():
                sent(self.send.at[0, piece])

            sent(self.send.at[1, piece])
            return carry

        lax.fori_loop(0, REP, body, 0)
        for copy in (*self.low, *self.high, self.back, self.onward):
            copy.wait_send()

        @pl.when(spot.core == 0)
        def _():
            self.forth.wait_send()


def spread_scratch(height):
    dma = pltpu.SemaphoreType.DMA
    return [
        *[pltpu.VMEM((2 * REP, height, LANES), BF16)] * SEC,
        pltpu.VMEM((2, 4, height, LANES), BF16),
        dma((2, 4)),
        dma((2, 4)),
        dma((2, REP)),
        dma((2, SEC - 1, REP)),
        dma((SEC, 2, REP)),
    ]


class Scatter:
    def __init__(self, spot, pieces, landing, send, arrive):
        self.spot, self.pieces, self.landing = spot, pieces, landing
        self.send, self.arrive = send, arrive

    def copy(self, half, other, lands):
        return remote(
            self.pieces.at[half, other],
            self.landing.at[half, lands],
            self.send.at[half, other],
            self.arrive.at[half, lands],
            (other, self.spot.blk),
        )

    def put(self, half, make):
        rep = self.spot.rep

        def one(step, carry):
            other = lax.rem(rep + 1 + step, REP)
            self.pieces[half, other] = make(other)
            self.copy(half, other, rep).start()
            return carry

        lax.fori_loop(0, REP - 1, one, 0)
        self.landing[half, rep] = make(rep)

    def total(self, half):
        rep = self.spot.rep

        def one(step, carry):
            other = lax.rem(rep + 1 + step, REP)
            self.copy(half, other, other).wait_recv()
            return carry

        lax.fori_loop(0, REP - 1, one, 0)
        total = self.landing[half, 0].astype(F32)
        for index in range(1, REP):
            total = total + self.landing[half, index].astype(F32)
        return total

    def drain(self):
        def one(step, carry):
            other = lax.rem(self.spot.rep + 1 + step, REP)
            for half in range(self.pieces.shape[0]):
                self.copy(half, other, other).wait_send()
            return carry

        lax.fori_loop(0, REP - 1, one, 0)


def scatter_scratch(halves, height, width, dtype):
    dma = pltpu.SemaphoreType.DMA
    return [
        pltpu.VMEM((halves, REP, height, width), dtype),
        pltpu.VMEM((halves, REP, height, width), dtype),
        dma((halves, REP)),
        dma((halves, REP)),
    ]


def fold(
    spot,
    fill,
    parts,
    low_in,
    high_in,
    low_out,
    high_out,
    final_out,
    final_in,
    line_out,
    line_in,
    chain_send,
    chain_arrive,
    final_send,
    final_arrive,
    line_send,
    line_arrive,
):
    rep, blk, core, here = spot.rep, spot.blk, spot.core, spot.here
    dummy = chain_send.at[0, 0, 0]

    def send_low(piece):
        remote(
            parts[SEC - 1].at[piece],
            low_in.at[SEC - 2, piece],
            chain_send.at[0, 0, piece],
            chain_arrive.at[0, SEC - 2, piece],
            spot.down,
        ).start()

    def send_high(piece):
        remote(
            parts[0].at[REP + piece],
            high_in.at[0, piece],
            chain_send.at[1, 0, piece],
            chain_arrive.at[1, 0, piece],
            spot.up,
        ).start()

    fill(SEC - 1, send_low, None)
    fill(0, None, send_high)
    fill(SEC - 2, None, None)
    fill(1, None, None)

    for step in range(SEC - 2):
        low_section = SEC - 2 - step

        def hop(piece, carry, step=step, low_section=low_section):
            landed(
                low_in.at[low_section, piece], dummy, chain_arrive.at[0, low_section, piece], here
            )
            low_out[low_section, piece] = (
                low_in[low_section, piece].astype(F32) + parts[low_section][piece].astype(F32)
            ).astype(BF16)
            remote(
                low_out.at[low_section, piece],
                low_in.at[low_section - 1, piece],
                chain_send.at[0, step + 1, piece],
                chain_arrive.at[0, low_section - 1, piece],
                spot.down,
            ).start()
            landed(high_in.at[step, piece], dummy, chain_arrive.at[1, step, piece], here)
            high_out[step, piece] = (
                high_in[step, piece].astype(F32) + parts[step + 1][REP + piece].astype(F32)
            ).astype(BF16)
            remote(
                high_out.at[step, piece],
                high_in.at[step + 1, piece],
                chain_send.at[1, step + 1, piece],
                chain_arrive.at[1, step + 1, piece],
                spot.up,
            ).start()
            return carry

        lax.fori_loop(0, REP, hop, 0)

    def final_copy(half, piece):
        return remote(
            final_out.at[half, piece],
            final_in.at[half, rep],
            final_send.at[half, piece],
            final_arrive.at[half, rep],
            (piece, spot.low_relay if half == 0 else spot.high_relay),
        )

    def final(index, carry):
        piece = lax.rem(index + rep, REP)
        landed(low_in.at[0, piece], dummy, chain_arrive.at[0, 0, piece], here)
        final_out[0, piece] = (
            low_in[0, piece].astype(F32) + parts[0][piece].astype(F32)
        ).astype(BF16)

        @pl.when(spot.local(piece))
        def _():
            final_in[0, rep] = final_out[0, piece]

        @pl.when(jnp.logical_not(spot.local(piece)))
        def _():
            final_copy(0, piece).start()

        landed(high_in.at[SEC - 2, piece], dummy, chain_arrive.at[1, SEC - 2, piece], here)
        final_out[1, piece] = (
            high_in[SEC - 2, piece].astype(F32) + parts[SEC - 1][REP + piece].astype(F32)
        ).astype(BF16)
        final_copy(1, piece).start()
        return carry

    lax.fori_loop(0, REP, final, 0)

    def pair(half, slot):
        for other in (slot, slot + 4):
            if half == 0:
                @pl.when(jnp.logical_not(spot.local(other)))
                def _(other=other):
                    landed(
                        final_in.at[0, other], dummy, final_arrive.at[0, other], here
                    )
            else:
                landed(final_in.at[1, other], dummy, final_arrive.at[1, other], here)
        return final_in[half, slot].astype(F32) + final_in[half, slot + 4].astype(F32)

    def line_copy(half, index, step):
        return remote(
            line_out.at[half, index],
            line_in.at[half, index],
            line_send.at[half, index],
            line_arrive.at[half, index],
            spot.line(step),
        )

    def line_wait(half, index):
        landed(line_in.at[half, index], dummy, line_arrive.at[half, index], here)
        return line_in[half, index].astype(F32)

    low_far = line_copy(0, 0, -2)
    line_out[0, 0] = pair(0, 2).astype(BF16)
    low_far.start()
    high_far = line_copy(1, 0, 2)
    line_out[1, 0] = pair(1, 2 - core).astype(BF16)
    high_far.start()
    high_side = line_copy(1, 1, -2)

    @pl.when(core == 0)
    def _():
        line_out[1, 1] = pair(1, 1).astype(BF16)
        high_side.start()

    low_back = line_copy(0, 1, 2)
    line_out[0, 1] = pair(0, 3).astype(BF16)
    low_back.start()
    low_near = line_copy(0, 2, -2)
    line_out[0, 2] = (pair(0, 1) + line_wait(0, 0)).astype(BF16)
    low_near.start()
    high_up = line_copy(1, 2, 1 + core)
    line_out[1, 2] = (pair(1, 3 - core) + line_wait(1, 0)).astype(BF16)
    high_up.start()
    high_down = line_copy(1, 3, -1 - core)

    @pl.when(core == 0)
    def _():
        line_out[1, 3] = (pair(1, 0) + line_wait(1, 1)).astype(BF16)

    @pl.when(core == 1)
    def _():
        line_out[1, 3] = pair(1, 0).astype(BF16)
        line_in[1, 1] = pair(1, 3).astype(BF16)

    high_down.start()
    low = pair(0, 0) + line_wait(0, 1) + line_wait(0, 2)
    high = line_wait(1, 2) + line_wait(1, 3)
    high = high + jnp.where(core == 1, line_in[1, 1].astype(F32), 0.0)

    def drain_all():
        def drain(piece, carry):
            for direction in range(2):
                for step in range(SEC - 1):
                    remote(
                        low_in.at[0, piece],
                        low_in.at[0, piece],
                        chain_send.at[direction, step, piece],
                        dummy,
                        here,
                    ).wait_send()

            @pl.when(jnp.logical_not(spot.local(piece)))
            def _():
                final_copy(0, piece).wait_send()

            final_copy(1, piece).wait_send()
            return carry

        lax.fori_loop(0, REP, drain, 0)
        for copy in (low_far, high_far, low_back, low_near, high_up, high_down):
            copy.wait_send()

        @pl.when(core == 0)
        def _():
            high_side.wait_send()

    return low, high, drain_all


def fold_scratch(height):
    dma = pltpu.SemaphoreType.DMA
    chain = pltpu.VMEM((SEC - 1, REP, height, LANES), BF16)
    final = pltpu.VMEM((2, REP, height, LANES), BF16)
    line = pltpu.VMEM((2, 4, height, LANES), BF16)
    return [
        *[pltpu.VMEM((2 * REP, height, LANES), BF16)] * SEC,
        chain,
        chain,
        chain,
        chain,
        final,
        final,
        line,
        line,
        dma((2, SEC - 1, REP)),
        dma((2, SEC - 1, REP)),
        dma((2, REP)),
        dma((2, REP)),
        dma((2, 4)),
        dma((2, 4)),
    ]


def pack(values):
    half = TILE // 2
    lanes = lax.broadcasted_iota(jnp.int32, (half, LANES), 1)
    rest = jnp.where(
        lanes < half,
        values[:half, LANES:],
        pltpu.roll(values[half:, LANES:], half, 1),
    )
    return jnp.concatenate([values[:, :LANES], rest], axis=0).astype(BF16)


def unpack(packed):
    half = TILE // 2
    rest = packed[TILE:]
    turned = jnp.concatenate([rest[:, half:], rest[:, :half]], axis=1)
    return jnp.concatenate(
        [packed[:TILE], jnp.concatenate([rest, turned], axis=0)], axis=1
    )


def keep_factor(ids):
    columns = lax.broadcasted_iota(jnp.int32, (1, WIDE), 1)
    mixed = ids * 73244475 + columns * 19349663 + 12345
    mixed = mixed ^ jnp.right_shift(mixed, 15)
    mixed = mixed * 40503
    mixed = mixed ^ jnp.right_shift(mixed, 13)
    return jnp.where(jnp.bitwise_and(mixed, 3) != 0, F32(4.0 / 3.0), F32(0.0))


def column_of(row):
    lanes = lax.broadcasted_iota(jnp.int32, (TILE, LANES), 1)
    rows = lax.broadcasted_iota(jnp.int32, (TILE, LANES), 0)
    spread_out = jnp.broadcast_to(row.astype(F32), (TILE, LANES))
    return jnp.sum(jnp.where(lanes == rows, spread_out, 0.0), axis=1, keepdims=True)


def step_kernel(
    scale,
    tables,
    x,
    ids,
    labels,
    mask,
    tiles,
    weight_in,
    weight_out,
    bias,
    logits_out,
    grad_in,
    grad_out,
    wide_out,
    wide_bias,
    running,
    shard,
    z_input,
    dropped,
    slope_factor,
    slopes,
    slope_send,
    slope_arrive,
    corner,
    corner_in,
    depth_in,
    full_corner,
    full,
    b_send,
    b_arrive,
    c_send,
    c_arrive,
    d_send,
    d_arrive,
    e_send,
    e_arrive,
    *rest,
):
    rest = list(rest)

    def take(count):
        taken = rest[:count]
        del rest[:count]
        return taken

    spot = Spot()
    rep, blk = spot.rep, spot.blk
    first_sections = take(SEC)
    first_spread = Spread(spot, x, first_sections, *take(6))
    second_sections = take(SEC)
    second_spread = Spread(spot, shard, second_sections, *take(6))
    first_scatter = Scatter(spot, *take(4))
    second_scatter = Scatter(spot, *take(4))
    term_scatter = Scatter(spot, *take(4))
    parts = take(SEC)
    fold_refs = take(14)

    waits = greet_everyone(spot)
    running[NONE] = jnp.zeros((TILE, WIDE), F32)
    wide_out[...] = jnp.zeros_like(wide_out)
    wide_out[:, :CLASSES] = weight_out[...]
    wide_bias[...] = jnp.zeros_like(wide_bias)
    wide_bias[:, :CLASSES] = bias[...]
    pl.semaphore_wait(pltpu.get_barrier_semaphore(), waits)

    def products(sections, section, width):
        place = FORWARD_ORDER.index(section)

        def some(group, carry):
            made = []
            for inner in range(4):
                slot = group * 4 + inner
                entry = place * SLOTS + slot
                source = sections[section][tables[0, entry]]
                if width == WIDE:
                    source = unpack(source)
                made.append(
                    jnp.dot(
                        tiles[section * SLOTS + slot], source, preferred_element_type=F32
                    )
                )
            for inner in range(4):
                entry = place * SLOTS + group * 4 + inner
                running[entry, :, :width] = (
                    made[inner] + running[tables[1, entry], :, :width]
                )
            return carry

        lax.fori_loop(0, SLOTS // 4, some, 0)

    def first_sum(half):
        return lambda other: running[tables[2, 2 * other + half], :, :LANES]

    def second_sum(half):
        return lambda other: pack(running[tables[2, 2 * other + half]])

    first_spread.start_low()
    first_spread.start_high()
    first_spread.pass_on()
    first_spread.chains()
    products(first_sections, 1, LANES)
    products(first_sections, 2, LANES)
    first_spread.last_arrivals()
    products(first_sections, 0, LANES)
    products(first_sections, 3, LANES)
    first_scatter.put(0, first_sum(0))
    first_scatter.put(1, first_sum(1))
    first_spread.drain()

    def hidden(half):
        rows = pl.ds(half * TILE, TILE)
        z_half = first_scatter.total(half).astype(BF16)
        z_input[rows, :] = z_half
        pre_act = jnp.dot(z_half, weight_in[...], preferred_element_type=F32)
        kept = keep_factor(column_of(ids[half : half + 1, :]).astype(jnp.int32))
        active = (jnp.maximum(pre_act, 0.0) * kept).astype(BF16)
        dropped[rows, :] = active
        slope_factor[rows, :] = jnp.where(pre_act > 0, kept, 0.0)
        shard[half] = pack(jnp.dot(active, wide_out[...], preferred_element_type=F32))

    hidden(0)
    second_spread.start_low()
    hidden(1)
    second_spread.start_high()
    second_spread.pass_on()
    second_spread.chains()
    products(second_sections, 1, WIDE)
    products(second_sections, 2, WIDE)
    second_spread.last_arrivals()
    products(second_sections, 0, WIDE)
    products(second_sections, 3, WIDE)
    second_scatter.put(0, second_sum(0))
    second_scatter.put(1, second_sum(1))
    second_spread.drain()
    first_scatter.drain()

    def slope_copy(half, other, lands):
        return remote(
            slopes.at[2 * rep + half],
            slopes.at[2 * lands + half],
            slope_send.at[half, other],
            slope_arrive.at[half, lands],
            (other, blk),
        )

    def classes(half):
        logits = unpack(second_scatter.total(half)) + wide_bias[...]
        logits_out[half * TILE : (half + 1) * TILE, :] = logits[:, :CLASSES]
        columns = lax.broadcasted_iota(jnp.int32, logits.shape, 1)
        real = columns < CLASSES
        top = jnp.max(jnp.where(real, logits, -jnp.inf), axis=1, keepdims=True)
        powers = jnp.where(real, jnp.exp(jnp.where(real, logits - top, 0.0)), 0.0)
        likelihood = powers / jnp.sum(powers, axis=1, keepdims=True)
        label = column_of(labels[half : half + 1, :]).astype(jnp.int32)
        onehot = jnp.where(columns == label, 1.0, 0.0)
        chosen = column_of(mask[half : half + 1, :]) * scale
        slopes[2 * rep + half] = pack((likelihood - onehot) * chosen)
        for step in range(1, REP):
            slope_copy(half, lax.rem(rep + step, REP), rep).start()

    classes(0)
    classes(1)
    second_scatter.drain()

    def slope_waits(step, carry):
        other = lax.rem(rep + step, REP)
        for half in range(2):
            copy = remote(
                slopes.at[2 * rep + half],
                slopes.at[2 * other + half],
                slope_send.at[half, other],
                slope_arrive.at[half, other],
                (other, blk),
            )
            copy.wait_recv()
            copy.wait_send()
        return carry

    lax.fori_loop(1, REP, slope_waits, 0)

    def fill(section, send_low, send_high):
        def some(group, carry):
            made = []
            for inner in range(4):
                entry = section * SLOTS + group * 4 + inner
                made.append(
                    lax.dot_general(
                        tiles[entry],
                        unpack(slopes[tables[3, entry]]),
                        (((0,), (0,)), ((), ())),
                        preferred_element_type=F32,
                    )
                )
            for inner in range(4):
                entry = section * SLOTS + group * 4 + inner
                running[entry] = made[inner] + running[tables[4, entry]]
            return carry

        lax.fori_loop(0, SLOTS // 4, some, 0)

        def gather(piece, carry):
            order = ((0, send_low), (1, send_high))
            for half, send in order:
                column = 2 * piece + half
                parts[section][half * REP + piece] = pack(
                    running[tables[5, section * SLOTS + column]]
                )
                if send is not None:
                    send(piece)
            return carry

        lax.fori_loop(0, REP, gather, 0)

    low, high, fold_drain = fold(spot, fill, parts, *fold_refs)
    back = jnp.concatenate([unpack(low.astype(BF16)), unpack(high.astype(BF16))], axis=0)
    out_terms = lax.dot_general(
        dropped[...], back, (((0,), (0,)), ((), ())), preferred_element_type=F32
    )
    back_rows = lax.dot_general(
        back, wide_out[...], (((1,), (1,)), ((), ())), preferred_element_type=F32
    )
    pre_slope = (back_rows * slope_factor[...]).astype(BF16)
    in_terms = lax.dot_general(
        z_input[...], pre_slope, (((0,), (0,)), ((), ())), preferred_element_type=F32
    )
    in_rows = in_terms.shape[0]
    chunk = (in_rows + WIDE) // REP
    joined = jnp.concatenate([in_terms, out_terms], axis=0).astype(BF16)
    for index in range(REP):
        term_scatter.pieces[0, index] = joined[index * chunk : (index + 1) * chunk]
    for step in range(1, REP):
        term_scatter.copy(0, lax.rem(rep + step, REP), rep).start()
    term_scatter.landing[0, rep] = term_scatter.pieces[0, rep]
    fold_drain()
    total = term_scatter.total(0)
    term_scatter.drain()
    for index in range(12):
        corner[index // 3, index % 3] = total[
            (index // 2) * 8 : (index // 2) * 8 + 8, (index % 2) * LANES : (index % 2 + 1) * LANES
        ]
    me = spot.corner
    for step in range(1, 4):
        other = lax.rem(me + step, 4)
        remote(
            corner.at[other],
            corner_in.at[me],
            b_send.at[other],
            b_arrive.at[me],
            spot.corner_device(other),
        ).start()
    for step in range(1, 4):
        other = lax.rem(me + step, 4)
        copy = remote(
            corner.at[other],
            corner_in.at[other],
            b_send.at[other],
            b_arrive.at[other],
            spot.corner_device(other),
        )
        copy.wait_recv()
        copy.wait_send()
    corner_in[me] = corner[me]
    depth = spot.depth
    depth_in[depth] = corner_in[0] + corner_in[1] + corner_in[2] + corner_in[3]
    for step in range(1, DEPTH):
        remote(
            depth_in.at[depth],
            depth_in.at[depth],
            c_send.at[step],
            c_arrive.at[depth],
            spot.line(step),
        ).start()
    for step in range(1, DEPTH):
        other = lax.rem(depth + step, DEPTH)
        copy = remote(
            depth_in.at[depth],
            depth_in.at[other],
            c_send.at[step],
            c_arrive.at[other],
            spot.line(step),
        )
        copy.wait_recv()
        copy.wait_send()
    total = depth_in[0]
    for index in range(1, DEPTH):
        total = total + depth_in[index]
    full_corner[me] = total
    for step in range(1, 4):
        other = lax.rem(me + step, 4)
        remote(
            full_corner.at[me],
            full_corner.at[me],
            d_send.at[other],
            d_arrive.at[me],
            spot.corner_device(other),
        ).start()
    for step in range(1, 4):
        other = lax.rem(me + step, 4)
        copy = remote(
            full_corner.at[me],
            full_corner.at[other],
            d_send.at[other],
            d_arrive.at[other],
            spot.corner_device(other),
        )
        copy.wait_recv()
        copy.wait_send()
    full[rep] = jnp.concatenate(
        [
            jnp.concatenate(
                [
                    full_corner[(2 * row) // 3, (2 * row) % 3],
                    full_corner[(2 * row + 1) // 3, (2 * row + 1) % 3],
                ],
                axis=1,
            )
            for row in range(6)
        ],
        axis=0,
    ).astype(BF16)
    for step in range(1, REP):
        other = lax.rem(rep + step, REP)
        remote(full.at[rep], full.at[rep], e_send.at[other], e_arrive.at[rep], (other, blk)).start()
    for step in range(1, REP):
        other = lax.rem(rep + step, REP)
        copy = remote(
            full.at[rep], full.at[other], e_send.at[other], e_arrive.at[other], (other, blk)
        )
        copy.wait_recv()
        copy.wait_send()
    joined = jnp.concatenate([full[index] for index in range(REP)], axis=0).astype(F32)
    grad_in[...] = joined[:in_rows]
    grad_out[...] = joined[in_rows:, :CLASSES]


def index_tables(tile_place, tile_count):
    entries = jnp.arange(NONE, dtype=jnp.int32)
    live = (jnp.arange(SLOTS, dtype=jnp.int32)[None, :] < tile_count[:, None]).astype(jnp.int32)
    forward = list(FORWARD_ORDER)
    place_f = jnp.concatenate([tile_place[index] for index in forward])
    live_f = jnp.concatenate([live[index] for index in forward])
    place_b = tile_place.reshape(-1)
    live_b = live.reshape(-1)
    row_f, column_f = place_f // SLOTS, place_f % SLOTS
    row_b, column_b = place_b // SLOTS, place_b % SLOTS
    source_f = (column_f % 2) * REP + column_f // 2
    group = entries // SLOTS

    def latest(keys, wanted, before, live_now):
        match = (keys[None, :] == wanted[:, None]) & (live_now[None, :] > 0)
        match = match & (entries[None, :] < before[:, None])
        found = jnp.max(jnp.where(match, entries[None, :], -1), axis=1)
        return jnp.where(found < 0, NONE, found)

    everything = jnp.full((NONE,), NONE, jnp.int32)
    key_b = group * SLOTS + column_b
    return jnp.stack(
        [
            source_f,
            latest(row_f, row_f, entries, live_f),
            latest(row_f, entries, everything, live_f),
            row_b,
            latest(key_b, key_b, entries, live_b),
            latest(key_b, entries, everything, live_b),
        ]
    )


def on_device(
    features,
    node_ids,
    labels,
    train_mask,
    tile_values,
    tile_place,
    tile_count,
    weight_in,
    weight_out,
    class_bias,
):
    width = features.shape[-1]
    own_rows = features.shape[1]
    scale = 1.0 / math.sqrt(own_rows * REP * BLK)
    shape = jax.ShapeDtypeStruct
    dma = pltpu.SemaphoreType.DMA
    vmem = pltpu.VMEM
    chunk = (width + WIDE) // REP
    tables = index_tables(tile_place[0, 0], tile_count[0, 0])
    logits, grad_in, grad_out = pl.pallas_call(
        lambda *refs: step_kernel(scale, *refs),
        out_shape=(
            shape((own_rows, CLASSES), F32),
            shape((width, WIDE), F32),
            shape((WIDE, CLASSES), F32),
        ),
        in_specs=[pl.BlockSpec(memory_space=pltpu.SMEM)] + [whole()] * 8,
        out_specs=[whole()] * 3,
        scratch_shapes=[
            vmem((WIDE, WIDE), BF16),
            vmem((1, WIDE), F32),
            vmem((NONE + 1, TILE, WIDE), F32),
            vmem((2, PACKED, LANES), BF16),
            vmem((own_rows, width), BF16),
            vmem((own_rows, WIDE), BF16),
            vmem((own_rows, WIDE), F32),
            vmem((2 * REP, PACKED, LANES), BF16),
            dma((2, REP)),
            dma((2, REP)),
            vmem((4, 3, 8, LANES), F32),
            vmem((4, 3, 8, LANES), F32),
            vmem((DEPTH, 3, 8, LANES), F32),
            vmem((4, 3, 8, LANES), F32),
            vmem((REP, chunk, WIDE), BF16),
            dma((4,)),
            dma((4,)),
            dma((DEPTH,)),
            dma((DEPTH,)),
            dma((4,)),
            dma((4,)),
            dma((REP,)),
            dma((REP,)),
            *spread_scratch(TILE),
            *spread_scratch(PACKED),
            *scatter_scratch(2, TILE, LANES, F32),
            *scatter_scratch(2, PACKED, LANES, BF16),
            *scatter_scratch(1, chunk, WIDE, BF16),
            *fold_scratch(PACKED),
        ],
        compiler_params=pltpu.CompilerParams(
            collective_id=0, has_side_effects=True, vmem_limit_bytes=VMEM_LIMIT
        ),
        name="training_step",
    )(
        tables,
        features.reshape(2, TILE, width),
        node_ids.reshape(2, TILE),
        labels.reshape(2, TILE),
        train_mask.reshape(2, TILE),
        tile_values.reshape(NONE, TILE, TILE),
        weight_in,
        weight_out,
        class_bias.reshape(1, CLASSES),
    )
    return (logits[None], grad_in, grad_out)


def solution(mesh):
    placed = (
        P("blk", "rep", None),
        P("blk", "rep"),
        P("blk", "rep"),
        P("blk", "rep"),
        P("blk", "rep", None, None, None, None),
        P("blk", "rep", None, None),
        P("blk", "rep", None),
        P(),
        P(),
        P(),
    )
    return jax.shard_map(
        on_device,
        mesh=mesh,
        in_specs=placed,
        out_specs=(P("blk", "rep", None), P(), P()),
        check_vma=False,
    )
```

time: 1090 us -> 198 us (0.18)
  waiting for transfers between devices: 771 us -> 0 us
  Pallas kernels: 0 us -> 186 us
  starting transfers between devices: 93.1 us -> 0 us
  other arithmetic: 74.4 us -> 1.25 us
  local copies, waits for them, and re-layouts: 65 us -> 9.76 us
  matrix products: 36.4 us -> 0 us
  blocking collectives: 25.7 us -> 0 us
  between operations: 14.8 us -> 0.66 us
    ppermute x18 -> x0, waiting for transfers between devices: 307 us -> none  [from_behind(): return lax.ppermute(value, axis, pairs)]
    psum x1 -> x0, waiting for transfers between devices: 253 us -> none  [on_device(): grad_in = lax.psum(in_terms, ('rep', 'blk'))]
    pallas_call x0 -> x1, Pallas kernels: none -> 186 us  [on_device(): pl.pallas_call(lambda *refs: step_kernel(scale, *refs), out_shape=(shape(...]
    reduce_scatter x3 -> x0, waiting for transfers between devices: 131 us -> none  [the longest x1 48.7 us: on_device(): lax.psum_scatter(spread(hidden_block), 'rep', scatter_dimension=0, tiled=...]
    ppermute x18 -> x0, starting transfers between devices: 92.4 us -> none  [from_behind(): return lax.ppermute(value, axis, pairs)]
    all_gather x2 -> x0, waiting for transfers between devices: 80.2 us -> none  [the longest x1 42.5 us: on_device(): hidden_block = lax.all_gather(dropped, 'rep', axis=0, tiled=True)]
    scatter-add x12 -> x0, other arithmetic: 43.4 us -> none  [place_rows(): jnp.zeros((tile_side, tile_edge, feat_width), jnp.float32).at[target]]
    dot_general x17 -> x0, matrix products: 36.4 us -> none  [the longest x8 21.4 us: place_rows(): jnp.einsum('tij,tjf->tif', tile_group, gathered, preferred_element_type=j...]
  transfers between devices with their start and end apart: 24 -> 0, of which waited for: 21 -> 0; matrix products, arithmetic and copies ran while one was open for 10% -> 0% of each run, Pallas kernels for 0% -> 0%
where the time goes in v3:
time: 198 us
  Pallas kernels  186 us (94%)
  local copies, waits for them, and re-layouts  9.76 us (5%)
    pallas_call x1, Pallas kernels, on_device(): pl.pallas_call(lambda *refs: step_kernel(scale, *refs), out_shape=(shape(...  186 us
    unnamed x4, local copies, waits for them, and re-layouts  6.69 us

profile of v3, /device:TPU:1, one launch (start us, length us, event | category | flops | bytes accessed | tf_op | source)
XLA Modules:
  0.0 197.9 jit_solution(16555086958326188721)
XLA Ops:
  0.6 0.8 reshape_squeeze.6
  1.4 0.8 reshape_squeeze.5
  2.2 0.7 fusion.6
  2.9 0.1 add_compare_fusion
  3.0 0.1 gt.23
  3.1 0.8 slice_bitcast_fusion.10
  3.9 0.1 and_select_fusion.3
  4.0 0.2 select_reduce_fusion
  4.2 0.1 and_select_fusion.2
  4.4 0.6 stack.2.refs_0_
  5.0 1.6 copy.16.refs_7_
  6.6 186.3 %training_step.1 = (f32[256,172]{1,0:T(8,128)}, f32[128,256]{1,0:T(8,128)}, f32[256,172]{1,0:T(8,128)}) custom-call(s32[6,64]{1,0:T(8,128)} %stack.2.refs_0_, bf16[2,128,128]{2,1,0:T(8,128)(2,1)} %bitcast.42, s32[2,128]{1,0:T(2,128)} %bitcast.43, s32[2,128]{1,0:T(2,128)} %bitcast.44, s32[2,128]{1,0:T(2,128)} %bitcast.45, bf16[64,128,128]{2,1,0:T(8,128)(2,1)} %bitcast.40, ...), custom_call_target="tpu_custom_call" | custom-call | tf_op jit(solution)/shard_map/training_step/pallas_call | solution.py:1019
  192.9 1.7 copy.17
  194.6 1.7 copy.18
  196.4 1.6 copy.20
  (5 shorter events, 0.0 us)

commit v4 on v3

--- a/solution.py
+++ b/solution.py
@@ -22,7 +22,8 @@
 DEPTH = 8
 NONE = SEC * SLOTS
 FORWARD_ORDER = (1, 2, 0, 3)
-BACKWARD_ORDER = (3, 0, 2, 1)
+CODED = 144
+KEEP = 4.0 / 3.0
 VMEM_LIMIT = 60 << 20
 
 
@@ -101,21 +102,10 @@
             greet((other, spot.low_relay))
 
         greet((other, spot.high_relay))
-    for slot in range(4):
-        for half in range(2):
-            for other, device in spot.targets(half, slot):
-                if half == 0:
-                    same = jnp.logical_and(other == spot.rep, device[1] == spot.blk)
-
-                    @pl.when(jnp.logical_not(same))
-                    def _(device=device):
-                        greet(device)
-                else:
-                    greet(device)
     greet(spot.up)
     greet(spot.down)
-    count = (REP - 1) + (DEPTH - 1) + 3 + 4 * REP + 2
-    return count - jnp.where(spot.own_relay, 2, 0)
+    count = (REP - 1) + (DEPTH - 1) + 3 + 2 * REP + 2
+    return count - jnp.where(spot.own_relay, 1, 0)
 
 
 class Spread:
@@ -364,233 +354,6 @@
     ]
 
 
-def fold(
-    spot,
-    fill,
-    parts,
-    low_in,
-    high_in,
-    low_out,
-    high_out,
-    final_out,
-    final_in,
-    line_out,
-    line_in,
-    chain_send,
-    chain_arrive,
-    final_send,
-    final_arrive,
-    line_send,
-    line_arrive,
-):
-    rep, blk, core, here = spot.rep, spot.blk, spot.core, spot.here
-    dummy = chain_send.at[0, 0, 0]
-
-    def send_low(piece):
-        remote(
-            parts[SEC - 1].at[piece],
-            low_in.at[SEC - 2, piece],
-            chain_send.at[0, 0, piece],
-            chain_arrive.at[0, SEC - 2, piece],
-            spot.down,
-        ).start()
-
-    def send_high(piece):
-        remote(
-            parts[0].at[REP + piece],
-            high_in.at[0, piece],
-            chain_send.at[1, 0, piece],
-            chain_arrive.at[1, 0, piece],
-            spot.up,
-        ).start()
-
-    fill(SEC - 1, send_low, None)
-    fill(0, None, send_high)
-    fill(SEC - 2, None, None)
-    fill(1, None, None)
-
-    for step in range(SEC - 2):
-        low_section = SEC - 2 - step
-
-        def hop(piece, carry, step=step, low_section=low_section):
-            landed(
-                low_in.at[low_section, piece], dummy, chain_arrive.at[0, low_section, piece], here
-            )
-            low_out[low_section, piece] = (
-                low_in[low_section, piece].astype(F32) + parts[low_section][piece].astype(F32)
-            ).astype(BF16)
-            remote(
-                low_out.at[low_section, piece],
-                low_in.at[low_section - 1, piece],
-                chain_send.at[0, step + 1, piece],
-                chain_arrive.at[0, low_section - 1, piece],
-                spot.down,
-            ).start()
-            landed(high_in.at[step, piece], dummy, chain_arrive.at[1, step, piece], here)
-            high_out[step, piece] = (
-                high_in[step, piece].astype(F32) + parts[step + 1][REP + piece].astype(F32)
-            ).astype(BF16)
-            remote(
-                high_out.at[step, piece],
-                high_in.at[step + 1, piece],
-                chain_send.at[1, step + 1, piece],
-                chain_arrive.at[1, step + 1, piece],
-                spot.up,
-            ).start()
-            return carry
-
-        lax.fori_loop(0, REP, hop, 0)
-
-    def final_copy(half, piece):
-        return remote(
-            final_out.at[half, piece],
-            final_in.at[half, rep],
-            final_send.at[half, piece],
-            final_arrive.at[half, rep],
-            (piece, spot.low_relay if half == 0 else spot.high_relay),
-        )
-
-    def final(index, carry):
-        piece = lax.rem(index + rep, REP)
-        landed(low_in.at[0, piece], dummy, chain_arrive.at[0, 0, piece], here)
-        final_out[0, piece] = (
-            low_in[0, piece].astype(F32) + parts[0][piece].astype(F32)
-        ).astype(BF16)
-
-        @pl.when(spot.local(piece))
-        def _():
-            final_in[0, rep] = final_out[0, piece]
-
-        @pl.when(jnp.logical_not(spot.local(piece)))
-        def _():
-            final_copy(0, piece).start()
-
-        landed(high_in.at[SEC - 2, piece], dummy, chain_arrive.at[1, SEC - 2, piece], here)
-        final_out[1, piece] = (
-            high_in[SEC - 2, piece].astype(F32) + parts[SEC - 1][REP + piece].astype(F32)
-        ).astype(BF16)
-        final_copy(1, piece).start()
-        return carry
-
-    lax.fori_loop(0, REP, final, 0)
-
-    def pair(half, slot):
-        for other in (slot, slot + 4):
-            if half == 0:
-                @pl.when(jnp.logical_not(spot.local(other)))
-                def _(other=other):
-                    landed(
-                        final_in.at[0, other], dummy, final_arrive.at[0, other], here
-                    )
-            else:
-                landed(final_in.at[1, other], dummy, final_arrive.at[1, other], here)
-        return final_in[half, slot].astype(F32) + final_in[half, slot + 4].astype(F32)
-
-    def line_copy(half, index, step):
-        return remote(
-            line_out.at[half, index],
-            line_in.at[half, index],
-            line_send.at[half, index],
-            line_arrive.at[half, index],
-            spot.line(step),
-        )
-
-    def line_wait(half, index):
-        landed(line_in.at[half, index], dummy, line_arrive.at[half, index], here)
-        return line_in[half, index].astype(F32)
-
-    low_far = line_copy(0, 0, -2)
-    line_out[0, 0] = pair(0, 2).astype(BF16)
-    low_far.start()
-    high_far = line_copy(1, 0, 2)
-    line_out[1, 0] = pair(1, 2 - core).astype(BF16)
-    high_far.start()
-    high_side = line_copy(1, 1, -2)
-
-    @pl.when(core == 0)
-    def _():
-        line_out[1, 1] = pair(1, 1).astype(BF16)
-        high_side.start()
-
-    low_back = line_copy(0, 1, 2)
-    line_out[0, 1] = pair(0, 3).astype(BF16)
-    low_back.start()
-    low_near = line_copy(0, 2, -2)
-    line_out[0, 2] = (pair(0, 1) + line_wait(0, 0)).astype(BF16)
-    low_near.start()
-    high_up = line_copy(1, 2, 1 + core)
-    line_out[1, 2] = (pair(1, 3 - core) + line_wait(1, 0)).astype(BF16)
-    high_up.start()
-    high_down = line_copy(1, 3, -1 - core)
-
-    @pl.when(core == 0)
-    def _():
-        line_out[1, 3] = (pair(1, 0) + line_wait(1, 1)).astype(BF16)
-
-    @pl.when(core == 1)
-    def _():
-        line_out[1, 3] = pair(1, 0).astype(BF16)
-        line_in[1, 1] = pair(1, 3).astype(BF16)
-
-    high_down.start()
-    low = pair(0, 0) + line_wait(0, 1) + line_wait(0, 2)
-    high = line_wait(1, 2) + line_wait(1, 3)
-    high = high + jnp.where(core == 1, line_in[1, 1].astype(F32), 0.0)
-
-    def drain_all():
-        def drain(piece, carry):
-            for direction in range(2):
-                for step in range(SEC - 1):
-                    remote(
-                        low_in.at[0, piece],
-                        low_in.at[0, piece],
-                        chain_send.at[direction, step, piece],
-                        dummy,
-                        here,
-                    ).wait_send()
-
-            @pl.when(jnp.logical_not(spot.local(piece)))
-            def _():
-                final_copy(0, piece).wait_send()
-
-            final_copy(1, piece).wait_send()
-            return carry
-
-        lax.fori_loop(0, REP, drain, 0)
-        for copy in (low_far, high_far, low_back, low_near, high_up, high_down):
-            copy.wait_send()
-
-        @pl.when(core == 0)
-        def _():
-            high_side.wait_send()
-
-    return low, high, drain_all
-
-
-def fold_scratch(height):
-    dma = pltpu.SemaphoreType.DMA
-    chain = pltpu.VMEM((SEC - 1, REP, height, LANES), BF16)
-    final = pltpu.VMEM((2, REP, height, LANES), BF16)
-    line = pltpu.VMEM((2, 4, height, LANES), BF16)
-    return [
-        *[pltpu.VMEM((2 * REP, height, LANES), BF16)] * SEC,
-        chain,
-        chain,
-        chain,
-        chain,
-        final,
-        final,
-        line,
-        line,
-        dma((2, SEC - 1, REP)),
-        dma((2, SEC - 1, REP)),
-        dma((2, REP)),
-        dma((2, REP)),
-        dma((2, 4)),
-        dma((2, 4)),
-    ]
-
-
 def pack(values):
     half = TILE // 2
     lanes = lax.broadcasted_iota(jnp.int32, (half, LANES), 1)
@@ -617,7 +380,7 @@
     mixed = mixed ^ jnp.right_shift(mixed, 15)
     mixed = mixed * 40503
     mixed = mixed ^ jnp.right_shift(mixed, 13)
-    return jnp.where(jnp.bitwise_and(mixed, 3) != 0, F32(4.0 / 3.0), F32(0.0))
+    return jnp.bitwise_and(mixed, 3) != 0
 
 
 def column_of(row):
@@ -629,7 +392,12 @@
 
 def step_kernel(
     scale,
-    tables,
+    source_table,
+    previous_table,
+    last_table,
+    row_table,
+    back_previous_table,
+    back_last_table,
     x,
     ids,
     labels,
@@ -644,10 +412,13 @@
     wide_out,
     wide_bias,
     running,
+    coded,
     shard,
-    z_input,
-    dropped,
-    slope_factor,
+    kept,
+    dense,
+    back_rows,
+    in_sum,
+    out_sum,
     slopes,
     slope_send,
     slope_arrive,
@@ -676,91 +447,135 @@
     spot = Spot()
     rep, blk = spot.rep, spot.blk
     first_sections = take(SEC)
-    first_spread = Spread(spot, x, first_sections, *take(6))
+    first_spread = Spread(spot, coded, first_sections, *take(6))
     second_sections = take(SEC)
     second_spread = Spread(spot, shard, second_sections, *take(6))
     first_scatter = Scatter(spot, *take(4))
     second_scatter = Scatter(spot, *take(4))
     term_scatter = Scatter(spot, *take(4))
-    parts = take(SEC)
-    fold_refs = take(14)
-
     waits = greet_everyone(spot)
     running[NONE] = jnp.zeros((TILE, WIDE), F32)
     wide_out[...] = jnp.zeros_like(wide_out)
-    wide_out[:, :CLASSES] = weight_out[...]
+    wide_out[:CLASSES, :] = weight_out[...]
     wide_bias[...] = jnp.zeros_like(wide_bias)
     wide_bias[:, :CLASSES] = bias[...]
+    code_rows = lax.broadcasted_iota(jnp.int32, (CODED - TILE, LANES), 0)
+    for half in range(2):
+        coded[half, :TILE] = x[half]
+        number = ids[half : half + 1, :]
+        code = jnp.zeros((CODED - TILE, LANES), F32)
+        for byte in range(3):
+            value = jnp.bitwise_and(jnp.right_shift(number, 8 * byte), 255).astype(F32)
+            code = jnp.where(code_rows == byte, jnp.broadcast_to(value, code.shape), code)
+        coded[half, TILE:] = code.astype(BF16)
     pl.semaphore_wait(pltpu.get_barrier_semaphore(), waits)
 
-    def products(sections, section, width):
+    def products(section, width, source_of):
         place = FORWARD_ORDER.index(section)
 
         def some(group, carry):
             made = []
             for inner in range(4):
                 slot = group * 4 + inner
-                entry = place * SLOTS + slot
-                source = sections[section][tables[0, entry]]
-                if width == WIDE:
-                    source = unpack(source)
                 made.append(
                     jnp.dot(
-                        tiles[section * SLOTS + slot], source, preferred_element_type=F32
+                        tiles[section * SLOTS + slot],
+                        source_of(source_table[section, slot]),
+                        preferred_element_type=F32,
                     )
                 )
             for inner in range(4):
-                entry = place * SLOTS + group * 4 + inner
-                running[entry, :, :width] = (
-                    made[inner] + running[tables[1, entry], :, :width]
+                slot = group * 4 + inner
+                running[place * SLOTS + slot, :, :width] = (
+                    made[inner] + running[previous_table[section, slot], :, :width]
                 )
             return carry
 
         lax.fori_loop(0, SLOTS // 4, some, 0)
 
+    def first_products(section):
+        products(section, LANES, lambda index: first_sections[section][index, :TILE])
+
+    def second_products(section):
+        products(section, WIDE, lambda index: dense[section * SLOTS + index])
+
     def first_sum(half):
-        return lambda other: running[tables[2, 2 * other + half], :, :LANES]
+        return lambda other: running[last_table[2 * other + half], :, :LANES]
 
     def second_sum(half):
-        return lambda other: pack(running[tables[2, 2 * other + half]])
+        def one(other):
+            part = running[last_table[2 * other + half]].astype(BF16)
+            return pack(
+                lax.dot_general(
+                    part, wide_out[...], (((1,), (1,)), ((), ())), preferred_element_type=F32
+                )
+            )
+
+        return one
+
+    def find_kept(section):
+        lanes = lax.broadcasted_iota(jnp.int32, (TILE, LANES), 1)
+        rows = lax.broadcasted_iota(jnp.int32, (TILE, LANES), 0)
+        unit = jnp.where(lanes == rows, 1.0, 0.0).astype(BF16)
+
+        def one(index, carry):
+            code = lax.dot_general(
+                unit,
+                first_sections[section][index, TILE:],
+                (((1,), (1,)), ((), ())),
+                preferred_element_type=F32,
+            )
+            number = code[:, 0:1] + 256.0 * code[:, 1:2] + 65536.0 * code[:, 2:3]
+            kept[section * SLOTS + index] = jnp.where(
+                keep_factor(number.astype(jnp.int32)), 1.0, 0.0
+            ).astype(BF16)
+            return carry
+
+        lax.fori_loop(0, SLOTS, one, 0)
+
+    def activate(section):
+        def one(index, carry):
+            pre_act = jnp.dot(
+                second_sections[section][index], weight_in[...], preferred_element_type=F32
+            )
+            active = jnp.maximum(pre_act, 0.0) * F32(KEEP)
+            flag = kept[section * SLOTS + index].astype(F32)
+            dense[section * SLOTS + index] = jnp.where(flag > 0.0, active, 0.0).astype(BF16)
+            return carry
+
+        lax.fori_loop(0, SLOTS, one, 0)
 
     first_spread.start_low()
     first_spread.start_high()
     first_spread.pass_on()
     first_spread.chains()
-    products(first_sections, 1, LANES)
-    products(first_sections, 2, LANES)
+    first_products(1)
+    first_products(2)
     first_spread.last_arrivals()
-    products(first_sections, 0, LANES)
-    products(first_sections, 3, LANES)
+    first_products(0)
+    first_products(3)
     first_scatter.put(0, first_sum(0))
     first_scatter.put(1, first_sum(1))
-    first_spread.drain()
-
-    def hidden(half):
-        rows = pl.ds(half * TILE, TILE)
-        z_half = first_scatter.total(half).astype(BF16)
-        z_input[rows, :] = z_half
-        pre_act = jnp.dot(z_half, weight_in[...], preferred_element_type=F32)
-        kept = keep_factor(column_of(ids[half : half + 1, :]).astype(jnp.int32))
-        active = (jnp.maximum(pre_act, 0.0) * kept).astype(BF16)
-        dropped[rows, :] = active
-        slope_factor[rows, :] = jnp.where(pre_act > 0, kept, 0.0)
-        shard[half] = pack(jnp.dot(active, wide_out[...], preferred_element_type=F32))
-
-    hidden(0)
+    for section in range(SEC):
+        find_kept(section)
+    shard[0] = first_scatter.total(0).astype(BF16)
     second_spread.start_low()
-    hidden(1)
+    shard[1] = first_scatter.total(1).astype(BF16)
     second_spread.start_high()
     second_spread.pass_on()
     second_spread.chains()
-    products(second_sections, 1, WIDE)
-    products(second_sections, 2, WIDE)
+    activate(1)
+    activate(2)
+    second_products(1)
+    second_products(2)
     second_spread.last_arrivals()
-    products(second_sections, 0, WIDE)
-    products(second_sections, 3, WIDE)
+    activate(0)
+    activate(3)
+    second_products(0)
+    second_products(3)
     second_scatter.put(0, second_sum(0))
     second_scatter.put(1, second_sum(1))
+    first_spread.drain()
     second_spread.drain()
     first_scatter.drain()
 
@@ -808,60 +623,70 @@
 
     lax.fori_loop(1, REP, slope_waits, 0)
 
-    def fill(section, send_low, send_high):
+    def back_products(section):
         def some(group, carry):
             made = []
             for inner in range(4):
-                entry = section * SLOTS + group * 4 + inner
+                slot = group * 4 + inner
                 made.append(
                     lax.dot_general(
-                        tiles[entry],
-                        unpack(slopes[tables[3, entry]]),
+                        tiles[section * SLOTS + slot],
+                        unpack(slopes[row_table[section, slot]]),
                         (((0,), (0,)), ((), ())),
                         preferred_element_type=F32,
                     )
                 )
             for inner in range(4):
-                entry = section * SLOTS + group * 4 + inner
-                running[entry] = made[inner] + running[tables[4, entry]]
+                slot = group * 4 + inner
+                running[section * SLOTS + slot] = (
+                    made[inner] + running[back_previous_table[section, slot]]
+                )
             return carry
 
         lax.fori_loop(0, SLOTS // 4, some, 0)
 
         def gather(piece, carry):
-            order = ((0, send_low), (1, send_high))
-            for half, send in order:
-                column = 2 * piece + half
-                parts[section][half * REP + piece] = pack(
-                    running[tables[5, section * SLOTS + column]]
-                )
-                if send is not None:
-                    send(piece)
+            for half in range(2):
+                back_rows[section * SLOTS + half * REP + piece] = running[
+                    back_last_table[section, 2 * piece + half]
+                ].astype(BF16)
             return carry
 
         lax.fori_loop(0, REP, gather, 0)
 
-    low, high, fold_drain = fold(spot, fill, parts, *fold_refs)
-    back = jnp.concatenate([unpack(low.astype(BF16)), unpack(high.astype(BF16))], axis=0)
-    out_terms = lax.dot_general(
-        dropped[...], back, (((0,), (0,)), ((), ())), preferred_element_type=F32
-    )
-    back_rows = lax.dot_general(
-        back, wide_out[...], (((1,), (1,)), ((), ())), preferred_element_type=F32
-    )
-    pre_slope = (back_rows * slope_factor[...]).astype(BF16)
-    in_terms = lax.dot_general(
-        z_input[...], pre_slope, (((0,), (0,)), ((), ())), preferred_element_type=F32
-    )
-    in_rows = in_terms.shape[0]
+    in_sum[...] = jnp.zeros_like(in_sum)
+    out_sum[...] = jnp.zeros_like(out_sum)
+
+    def terms(section):
+        for half in range(2):
+            inside = pl.ds(section * SLOTS + half * REP, REP)
+            back = back_rows[inside].reshape(REP * TILE, WIDE)
+            active = dense[inside].reshape(REP * TILE, WIDE)
+            z_rows = second_sections[section][half * REP : (half + 1) * REP].reshape(
+                REP * TILE, LANES
+            )
+            out_sum[...] += lax.dot_general(
+                back, active, (((0,), (0,)), ((), ())), preferred_element_type=F32
+            )
+            hidden_rows = jnp.dot(back, wide_out[...], preferred_element_type=F32)
+            pre_slope = jnp.where(
+                active.astype(F32) > 0.0, hidden_rows * F32(KEEP), 0.0
+            ).astype(BF16)
+            in_sum[...] += lax.dot_general(
+                z_rows, pre_slope, (((0,), (0,)), ((), ())), preferred_element_type=F32
+            )
+
+    for section in range(SEC):
+        back_products(section)
+        terms(section)
+    in_rows = in_sum.shape[0]
     chunk = (in_rows + WIDE) // REP
-    joined = jnp.concatenate([in_terms, out_terms], axis=0).astype(BF16)
+    joined = jnp.concatenate([in_sum[...], out_sum[...]], axis=0).astype(BF16)
     for index in range(REP):
         term_scatter.pieces[0, index] = joined[index * chunk : (index + 1) * chunk]
     for step in range(1, REP):
         term_scatter.copy(0, lax.rem(rep + step, REP), rep).start()
     term_scatter.landing[0, rep] = term_scatter.pieces[0, rep]
-    fold_drain()
     total = term_scatter.total(0)
     term_scatter.drain()
     for index in range(12):
@@ -960,40 +785,37 @@
         copy.wait_send()
     joined = jnp.concatenate([full[index] for index in range(REP)], axis=0).astype(F32)
     grad_in[...] = joined[:in_rows]
-    grad_out[...] = joined[in_rows:, :CLASSES]
-
-
-def index_tables(tile_place, tile_count):
-    entries = jnp.arange(NONE, dtype=jnp.int32)
-    live = (jnp.arange(SLOTS, dtype=jnp.int32)[None, :] < tile_count[:, None]).astype(jnp.int32)
-    forward = list(FORWARD_ORDER)
-    place_f = jnp.concatenate([tile_place[index] for index in forward])
-    live_f = jnp.concatenate([live[index] for index in forward])
-    place_b = tile_place.reshape(-1)
-    live_b = live.reshape(-1)
-    row_f, column_f = place_f // SLOTS, place_f % SLOTS
-    row_b, column_b = place_b // SLOTS, place_b % SLOTS
-    source_f = (column_f % 2) * REP + column_f // 2
-    group = entries // SLOTS
-
-    def latest(keys, wanted, before, live_now):
-        match = (keys[None, :] == wanted[:, None]) & (live_now[None, :] > 0)
-        match = match & (entries[None, :] < before[:, None])
-        found = jnp.max(jnp.where(match, entries[None, :], -1), axis=1)
-        return jnp.where(found < 0, NONE, found)
-
-    everything = jnp.full((NONE,), NONE, jnp.int32)
-    key_b = group * SLOTS + column_b
-    return jnp.stack(
-        [
-            source_f,
-            latest(row_f, row_f, entries, live_f),
-            latest(row_f, entries, everything, live_f),
-            row_b,
-            latest(key_b, key_b, entries, live_b),
-            latest(key_b, entries, everything, live_b),
-        ]
+    grad_out[...] = joined[in_rows : in_rows + CLASSES]
+
+
+def index_tables(place, count):
+    section = lax.broadcasted_iota(jnp.int32, (SEC, SLOTS), 0)
+    slot = lax.broadcasted_iota(jnp.int32, (SEC, SLOTS), 1)
+    live = slot < count[:, None]
+    row, column = place // SLOTS, place % SLOTS
+    turn = jnp.where(section == SEC - 1, SEC - 1, (section + 2) % (SEC - 1))
+    entry = turn * SLOTS + slot
+    back_entry = section * SLOTS + slot
+
+    def found(match, entries, axes):
+        latest = jnp.max(jnp.where(match, entries, -1), axis=axes)
+        return jnp.where(latest < 0, NONE, latest)
+
+    entries = entry[None, None]
+    same_row = (row[None, None] == row[:, :, None, None]) & live[None, None]
+    previous = found(same_row & (entries < entry[:, :, None, None]), entries, (2, 3))
+    numbers = jnp.arange(SLOTS, dtype=jnp.int32)
+    of_row = (row[None] == numbers[:, None, None]) & live[None]
+    last = found(of_row, entry[None], (1, 2))
+    back_entries = back_entry[:, None, :]
+    same_column = (column[:, None, :] == column[:, :, None]) & live[:, None, :]
+    back_previous = found(
+        same_column & (back_entries < back_entry[:, :, None]), back_entries, 2
     )
+    of_column = (column[:, None, :] == numbers[None, :, None]) & live[:, None, :]
+    back_last = found(of_column, back_entries, 2)
+    source = (column % 2) * REP + column // 2
+    return source, previous, last, row, back_previous, back_last
 
 
 def on_device(
@@ -1021,18 +843,21 @@
         out_shape=(
             shape((own_rows, CLASSES), F32),
             shape((width, WIDE), F32),
-            shape((WIDE, CLASSES), F32),
+            shape((CLASSES, WIDE), F32),
         ),
-        in_specs=[pl.BlockSpec(memory_space=pltpu.SMEM)] + [whole()] * 8,
+        in_specs=[pl.BlockSpec(memory_space=pltpu.SMEM)] * 6 + [whole()] * 8,
         out_specs=[whole()] * 3,
         scratch_shapes=[
             vmem((WIDE, WIDE), BF16),
             vmem((1, WIDE), F32),
             vmem((NONE + 1, TILE, WIDE), F32),
-            vmem((2, PACKED, LANES), BF16),
-            vmem((own_rows, width), BF16),
-            vmem((own_rows, WIDE), BF16),
-            vmem((own_rows, WIDE), F32),
+            vmem((2, CODED, LANES), BF16),
+            vmem((2, TILE, LANES), BF16),
+            vmem((NONE, TILE, WIDE), BF16),
+            vmem((NONE, TILE, WIDE), BF16),
+            vmem((NONE, TILE, WIDE), BF16),
+            vmem((width, WIDE), F32),
+            vmem((WIDE, WIDE), F32),
             vmem((2 * REP, PACKED, LANES), BF16),
             dma((2, REP)),
             dma((2, REP)),
@@ -1049,29 +874,28 @@
             dma((4,)),
             dma((REP,)),
             dma((REP,)),
+            *spread_scratch(CODED),
             *spread_scratch(TILE),
-            *spread_scratch(PACKED),
             *scatter_scratch(2, TILE, LANES, F32),
             *scatter_scratch(2, PACKED, LANES, BF16),
             *scatter_scratch(1, chunk, WIDE, BF16),
-            *fold_scratch(PACKED),
         ],
         compiler_params=pltpu.CompilerParams(
             collective_id=0, has_side_effects=True, vmem_limit_bytes=VMEM_LIMIT
         ),
         name="training_step",
     )(
-        tables,
+        *tables,
         features.reshape(2, TILE, width),
         node_ids.reshape(2, TILE),
         labels.reshape(2, TILE),
         train_mask.reshape(2, TILE),
         tile_values.reshape(NONE, TILE, TILE),
         weight_in,
-        weight_out,
+        weight_out.T,
         class_bias.reshape(1, CLASSES),
     )
-    return (logits[None], grad_in, grad_out)
+    return (logits[None], grad_in, grad_out.T)
 
 
 def solution(mesh):

time: 198 us -> 163 us (0.82)
  Pallas kernels: 186 us -> 152 us
  local copies, waits for them, and re-layouts: 9.76 us -> 4.92 us
  other arithmetic: 1.25 us -> 5.25 us
    pallas_call x1, Pallas kernels: 186 us -> 152 us  [on_device(): pl.pallas_call(lambda *refs: step_kernel(scale, *refs), out_shape=(shape(...]
    another operation x3 -> x0, local copies, waits for them, and re-layouts: 2.14 us -> none  [the longest x2 1.53 us: index_tables(): place_b = tile_place.reshape(-1)]
    unnamed x4 -> x5, local copies, waits for them, and re-layouts: 6.69 us -> 4.92 us
where the time goes in v4:
time: 163 us
  Pallas kernels  152 us (93%)
  other arithmetic  5.25 us (3%)
  local copies, waits for them, and re-layouts  4.92 us (3%)
    pallas_call x1, Pallas kernels, on_device(): pl.pallas_call(lambda *refs: step_kernel(scale, *refs), out_shape=(shape(...  152 us
    unnamed x5, local copies, waits for them, and re-layouts  4.92 us

profile of v4, /device:TPU:1, one launch (start us, length us, event | category | flops | bytes accessed | tf_op | source)
XLA Modules:
  0.0 162.7 jit_solution(9737576157120234158)
XLA Ops:
  0.6 0.7 iota_compare_fusion.2
  1.4 0.1 iota_add_fusion.1
  1.5 0.1 iota_add_fusion
  1.5 0.7 fusion.5
  2.2 1.3 fusion.3
  3.5 0.0 copy-start
  3.5 0.2 select_reduce_fusion
  3.8 0.1 select_reduce_fusion.3
  3.9 0.6 compare_select_fusion.3.refs_2_
  4.5 0.6 compare_select_fusion.2.refs_1_
  5.0 0.2 select_reduce_fusion.1
  5.3 0.6 compare_select_fusion
  5.9 0.0 copy-done
  5.9 151.9 %training_step.1 = (f32[256,172]{1,0:T(8,128)}, f32[128,256]{1,0:T(8,128)}, f32[172,256]{1,0:T(8,128)}) custom-call(s32[4,16]{1,0:T(4,128)} %get-tuple-element.17.refs_0_, s32[4,16]{1,0:T(4,128)} %compare_select_fusion.2.refs_1_, s32[16]{0:T(128)} %compare_select_fusion.3.refs_2_, s32[4,16]{1,0:T(4,128)} %copy-done, s32[4,16]{1,0:T(4,128)} %get-tuple-element.25.refs_4_, ...), custom_call_target="tpu_custom_call" | custom-call | tf_op jit(solution)/shard_map/training_step/pallas_call | solution.py:841
  157.8 1.7 %copy.14 = f32[1,256,172]{1,0,2:T(1,128)} copy(f32[1,256,172]{2,1,0:T(8,128)} %bitcast.36) | data formatting | bytes 352256
  159.5 1.6 copy.17
  161.1 1.6 copy.18
  (3 shorter events, 0.0 us)
Async XLA Ops:
  3.5 2.4 %copy-start = (s32[4,16]{1,0:T(4,128)}, s32[4,16]{1,0:T(4,128)S(1)}, u32[]{:S(2)}) copy-start(s32[4,16]{1,0:T(4,128)S(1)} %get-tuple-element.19.refs_3_) | copy-start | bytes 772

commit v5 on v4

--- a/solution.py
+++ b/solution.py
@@ -24,6 +24,7 @@
 FORWARD_ORDER = (1, 2, 0, 3)
 CODED = 144
 KEEP = 4.0 / 3.0
+SOURCE, PREVIOUS, ROW, BACK_PREVIOUS, BACK_LAST, LAST = 0, 4, 8, 12, 16, 20
 VMEM_LIMIT = 60 << 20
 
 
@@ -374,11 +375,10 @@
     )
 
 
-def keep_factor(ids):
+def is_kept(ids):
     columns = lax.broadcasted_iota(jnp.int32, (1, WIDE), 1)
-    mixed = ids * 73244475 + columns * 19349663 + 12345
-    mixed = mixed ^ jnp.right_shift(mixed, 15)
-    mixed = mixed * 40503
+    mixed = (ids * 73244475 + 12345) + columns * 19349663
+    mixed = jnp.bitwise_and(mixed ^ jnp.right_shift(mixed, 15), 32767) * (40503 % 32768)
     mixed = mixed ^ jnp.right_shift(mixed, 13)
     return jnp.bitwise_and(mixed, 3) != 0
 
@@ -392,23 +392,25 @@
 
 def step_kernel(
     scale,
-    source_table,
-    previous_table,
-    last_table,
-    row_table,
-    back_previous_table,
-    back_last_table,
-    x,
+    count,
+    place,
+    x_hbm,
     ids,
     labels,
     mask,
+    tiles_hbm,
+    weight_in_hbm,
+    weight_out_hbm,
+    bias,
+    logits_out,
+    full,
+    x,
     tiles,
     weight_in,
     weight_out,
-    bias,
-    logits_out,
-    grad_in,
-    grad_out,
+    input_sems,
+    table_values,
+    table,
     wide_out,
     wide_bias,
     running,
@@ -426,7 +428,6 @@
     corner_in,
     depth_in,
     full_corner,
-    full,
     b_send,
     b_arrive,
     c_send,
@@ -454,11 +455,29 @@
     second_scatter = Scatter(spot, *take(4))
     term_scatter = Scatter(spot, *take(4))
     waits = greet_everyone(spot)
+    input_copies = [
+        pltpu.make_async_copy(source, target, input_sems.at[index])
+        for index, (source, target) in enumerate(
+            (
+                (x_hbm, x),
+                (weight_out_hbm, weight_out),
+                (weight_in_hbm, weight_in),
+                (tiles_hbm, tiles),
+            )
+        )
+    ]
+    for copy in input_copies:
+        copy.start()
+    fill_tables(place, count, table_values)
+    table_copy = pltpu.make_async_copy(table_values, table, input_sems.at[len(input_copies)])
+    table_copy.start()
     running[NONE] = jnp.zeros((TILE, WIDE), F32)
     wide_out[...] = jnp.zeros_like(wide_out)
-    wide_out[:CLASSES, :] = weight_out[...]
     wide_bias[...] = jnp.zeros_like(wide_bias)
     wide_bias[:, :CLASSES] = bias[...]
+    input_copies[0].wait()
+    input_copies[1].wait()
+    wide_out[:CLASSES, :] = weight_out[...]
     code_rows = lax.broadcasted_iota(jnp.int32, (CODED - TILE, LANES), 0)
     for half in range(2):
         coded[half, :TILE] = x[half]
@@ -480,14 +499,14 @@
                 made.append(
                     jnp.dot(
                         tiles[section * SLOTS + slot],
-                        source_of(source_table[section, slot]),
+                        source_of(table[SOURCE + section, slot]),
                         preferred_element_type=F32,
                     )
                 )
             for inner in range(4):
                 slot = group * 4 + inner
                 running[place * SLOTS + slot, :, :width] = (
-                    made[inner] + running[previous_table[section, slot], :, :width]
+                    made[inner] + running[table[PREVIOUS + section, slot], :, :width]
                 )
             return carry
 
@@ -500,11 +519,11 @@
         products(section, WIDE, lambda index: dense[section * SLOTS + index])
 
     def first_sum(half):
-        return lambda other: running[last_table[2 * other + half], :, :LANES]
+        return lambda other: running[table[LAST, 2 * other + half], :, :LANES]
 
     def second_sum(half):
         def one(other):
-            part = running[last_table[2 * other + half]].astype(BF16)
+            part = running[table[LAST, 2 * other + half]].astype(BF16)
             return pack(
                 lax.dot_general(
                     part, wide_out[...], (((1,), (1,)), ((), ())), preferred_element_type=F32
@@ -527,11 +546,11 @@
             )
             number = code[:, 0:1] + 256.0 * code[:, 1:2] + 65536.0 * code[:, 2:3]
             kept[section * SLOTS + index] = jnp.where(
-                keep_factor(number.astype(jnp.int32)), 1.0, 0.0
+                is_kept(number.astype(jnp.int32)), 1.0, 0.0
             ).astype(BF16)
             return carry
 
-        lax.fori_loop(0, SLOTS, one, 0)
+        lax.fori_loop(0, SLOTS, one, 0, unroll=4)
 
     def activate(section):
         def one(index, carry):
@@ -543,12 +562,15 @@
             dense[section * SLOTS + index] = jnp.where(flag > 0.0, active, 0.0).astype(BF16)
             return carry
 
-        lax.fori_loop(0, SLOTS, one, 0)
+        lax.fori_loop(0, SLOTS, one, 0, unroll=4)
 
     first_spread.start_low()
     first_spread.start_high()
     first_spread.pass_on()
     first_spread.chains()
+    input_copies[2].wait()
+    input_copies[3].wait()
+    table_copy.wait()
     first_products(1)
     first_products(2)
     first_spread.last_arrivals()
@@ -590,7 +612,6 @@
 
     def classes(half):
         logits = unpack(second_scatter.total(half)) + wide_bias[...]
-        logits_out[half * TILE : (half + 1) * TILE, :] = logits[:, :CLASSES]
         columns = lax.broadcasted_iota(jnp.int32, logits.shape, 1)
         real = columns < CLASSES
         top = jnp.max(jnp.where(real, logits, -jnp.inf), axis=1, keepdims=True)
@@ -602,9 +623,12 @@
         slopes[2 * rep + half] = pack((likelihood - onehot) * chosen)
         for step in range(1, REP):
             slope_copy(half, lax.rem(rep + step, REP), rep).start()
-
-    classes(0)
-    classes(1)
+        return logits
+
+    low_logits = classes(0)
+    high_logits = classes(1)
+    logits_out[:, :TILE] = low_logits.T[:CLASSES]
+    logits_out[:, TILE:] = high_logits.T[:CLASSES]
     second_scatter.drain()
 
     def slope_waits(step, carry):
@@ -631,7 +655,7 @@
                 made.append(
                     lax.dot_general(
                         tiles[section * SLOTS + slot],
-                        unpack(slopes[row_table[section, slot]]),
+                        unpack(slopes[table[ROW + section, slot]]),
                         (((0,), (0,)), ((), ())),
                         preferred_element_type=F32,
                     )
@@ -639,7 +663,7 @@
             for inner in range(4):
                 slot = group * 4 + inner
                 running[section * SLOTS + slot] = (
-                    made[inner] + running[back_previous_table[section, slot]]
+                    made[inner] + running[table[BACK_PREVIOUS + section, slot]]
                 )
             return carry
 
@@ -648,11 +672,11 @@
         def gather(piece, carry):
             for half in range(2):
                 back_rows[section * SLOTS + half * REP + piece] = running[
-                    back_last_table[section, 2 * piece + half]
+                    table[BACK_LAST + section, 2 * piece + half]
                 ].astype(BF16)
             return carry
 
-        lax.fori_loop(0, REP, gather, 0)
+        lax.fori_loop(0, REP, gather, 0, unroll=2)
 
     in_sum[...] = jnp.zeros_like(in_sum)
     out_sum[...] = jnp.zeros_like(out_sum)
@@ -783,39 +807,65 @@
         )
         copy.wait_recv()
         copy.wait_send()
+
+
+def result_kernel(in_rows, logits, full, logits_out, grad_in, grad_out):
+    logits_out[:, 0, :] = logits[...]
     joined = jnp.concatenate([full[index] for index in range(REP)], axis=0).astype(F32)
     grad_in[...] = joined[:in_rows]
     grad_out[...] = joined[in_rows : in_rows + CLASSES]
 
 
-def index_tables(place, count):
-    section = lax.broadcasted_iota(jnp.int32, (SEC, SLOTS), 0)
-    slot = lax.broadcasted_iota(jnp.int32, (SEC, SLOTS), 1)
-    live = slot < count[:, None]
-    row, column = place // SLOTS, place % SLOTS
-    turn = jnp.where(section == SEC - 1, SEC - 1, (section + 2) % (SEC - 1))
-    entry = turn * SLOTS + slot
-    back_entry = section * SLOTS + slot
-
-    def found(match, entries, axes):
-        latest = jnp.max(jnp.where(match, entries, -1), axis=axes)
-        return jnp.where(latest < 0, NONE, latest)
-
-    entries = entry[None, None]
-    same_row = (row[None, None] == row[:, :, None, None]) & live[None, None]
-    previous = found(same_row & (entries < entry[:, :, None, None]), entries, (2, 3))
-    numbers = jnp.arange(SLOTS, dtype=jnp.int32)
-    of_row = (row[None] == numbers[:, None, None]) & live[None]
-    last = found(of_row, entry[None], (1, 2))
-    back_entries = back_entry[:, None, :]
-    same_column = (column[:, None, :] == column[:, :, None]) & live[:, None, :]
-    back_previous = found(
-        same_column & (back_entries < back_entry[:, :, None]), back_entries, 2
-    )
-    of_column = (column[:, None, :] == numbers[None, :, None]) & live[:, None, :]
-    back_last = found(of_column, back_entries, 2)
-    source = (column % 2) * REP + column // 2
-    return source, previous, last, row, back_previous, back_last
+def fill_tables(place, count, out):
+    slots = lax.broadcasted_iota(jnp.int32, (SLOTS, SLOTS), 1)
+    others = lax.broadcasted_iota(jnp.int32, (SLOTS, SLOTS), 0)
+    before = others < slots
+
+    def turned(line):
+        flat = jnp.broadcast_to(line.astype(F32), (SLOTS, SLOTS))
+        column = jnp.sum(jnp.where(slots == others, flat, 0.0), axis=1, keepdims=True)
+        return column.astype(jnp.int32)
+
+    def top(match, entries):
+        return jnp.max(jnp.where(match, entries, -1), axis=0, keepdims=True)
+
+    def put(row, values):
+        out[row : row + 1, :SLOTS] = values
+
+    def settled(values):
+        return jnp.where(values < 0, NONE, values)
+
+    rows, columns, row_turned, column_turned, live = [], [], [], [], []
+    for section in range(SEC):
+        line = place[section : section + 1, :]
+        rows.append(jnp.right_shift(line, 4))
+        columns.append(jnp.bitwise_and(line, SLOTS - 1))
+        row_turned.append(turned(rows[section]))
+        column_turned.append(turned(columns[section]))
+        live.append(others < count[section])
+    numbers = slots[:1]
+    last = jnp.full((1, SLOTS), -1, jnp.int32)
+    for section in range(SEC):
+        turn = FORWARD_ORDER.index(section)
+        entries = others + turn * SLOTS
+        latest = jnp.full((1, SLOTS), -1, jnp.int32)
+        for earlier in FORWARD_ORDER[: turn + 1]:
+            match = (row_turned[earlier] == rows[section]) & live[earlier]
+            if earlier == section:
+                match = match & before
+            latest = jnp.maximum(
+                latest, top(match, others + FORWARD_ORDER.index(earlier) * SLOTS)
+            )
+        last = jnp.maximum(last, top((row_turned[section] == numbers) & live[section], entries))
+        put(SOURCE + section, jnp.bitwise_and(columns[section], 1) * REP + jnp.right_shift(columns[section], 1))
+        put(PREVIOUS + section, settled(latest))
+        put(ROW + section, rows[section])
+        own = others + section * SLOTS
+        match = (column_turned[section] == columns[section]) & live[section]
+        put(BACK_PREVIOUS + section, settled(top(match & before, own)))
+        match = (column_turned[section] == numbers) & live[section]
+        put(BACK_LAST + section, settled(top(match, own)))
+    put(LAST, settled(last))
 
 
 def on_device(
@@ -837,17 +887,31 @@
     dma = pltpu.SemaphoreType.DMA
     vmem = pltpu.VMEM
     chunk = (width + WIDE) // REP
-    tables = index_tables(tile_place[0, 0], tile_count[0, 0])
-    logits, grad_in, grad_out = pl.pallas_call(
+    anywhere = pl.BlockSpec(memory_space=pl.ANY)
+    logits, full = pl.pallas_call(
         lambda *refs: step_kernel(scale, *refs),
-        out_shape=(
-            shape((own_rows, CLASSES), F32),
-            shape((width, WIDE), F32),
-            shape((CLASSES, WIDE), F32),
-        ),
-        in_specs=[pl.BlockSpec(memory_space=pltpu.SMEM)] * 6 + [whole()] * 8,
-        out_specs=[whole()] * 3,
+        out_shape=(shape((CLASSES, own_rows), F32), shape((REP, chunk, WIDE), BF16)),
+        in_specs=[
+            pl.BlockSpec(memory_space=pltpu.SMEM),
+            whole(),
+            anywhere,
+            whole(),
+            whole(),
+            whole(),
+            anywhere,
+            anywhere,
+            anywhere,
+            whole(),
+        ],
+        out_specs=[whole()] * 2,
         scratch_shapes=[
+            vmem((2, TILE, width), BF16),
+            vmem((NONE, TILE, TILE), BF16),
+            vmem((width, WIDE), BF16),
+            vmem((CLASSES, WIDE), BF16),
+            dma((5,)),
+            vmem((24, LANES), jnp.int32),
+            pltpu.SMEM((24, LANES), jnp.int32),
             vmem((WIDE, WIDE), BF16),
             vmem((1, WIDE), F32),
             vmem((NONE + 1, TILE, WIDE), F32),
@@ -865,7 +929,6 @@
             vmem((4, 3, 8, LANES), F32),
             vmem((DEPTH, 3, 8, LANES), F32),
             vmem((4, 3, 8, LANES), F32),
-            vmem((REP, chunk, WIDE), BF16),
             dma((4,)),
             dma((4,)),
             dma((DEPTH,)),
@@ -885,7 +948,8 @@
         ),
         name="training_step",
     )(
-        *tables,
+        tile_count.reshape(SEC),
+        tile_place.reshape(SEC, SLOTS),
         features.reshape(2, TILE, width),
         node_ids.reshape(2, TILE),
         labels.reshape(2, TILE),
@@ -895,7 +959,18 @@
         weight_out.T,
         class_bias.reshape(1, CLASSES),
     )
-    return (logits[None], grad_in, grad_out.T)
+    logits, grad_in, grad_out = pl.pallas_call(
+        lambda *refs: result_kernel(width, *refs),
+        out_shape=(
+            shape((CLASSES, 1, own_rows), F32),
+            shape((width, WIDE), F32),
+            shape((CLASSES, WIDE), F32),
+        ),
+        in_specs=[whole()] * 2,
+        out_specs=[whole()] * 3,
+        name="results",
+    )(logits, full)
+    return (logits.transpose(1, 2, 0), grad_in, grad_out.T)
 
 
 def solution(mesh):

time: 163 us -> 138 us (0.85)
  Pallas kernels: 152 us -> 138 us
  other arithmetic: 5.25 us -> 0 us
  local copies, waits for them, and re-layouts: 4.92 us -> 0 us
    pallas_call x1, Pallas kernels: 152 us -> 136 us  [on_device(): pl.pallas_call(lambda *refs: step_kernel(scale, *refs), out_shape=(shape(...]
    unnamed x5 -> x0, local copies, waits for them, and re-layouts: 4.92 us -> none
    pallas_call x0 -> x1, Pallas kernels: none -> 1.8 us  [on_device(): pl.pallas_call(lambda *refs: result_kernel(width, *refs), out_shape=(shap...]
    select_n x3 -> x0, other arithmetic: 1.77 us -> none  [found(): return jnp.where(latest < 0, NONE, latest)]
where the time goes in v5:
time: 138 us
  Pallas kernels  138 us (100%)
    pallas_call x1, Pallas kernels, on_device(): pl.pallas_call(lambda *refs: step_kernel(scale, *refs), out_shape=(shape(...  136 us

profile of v5, /device:TPU:1, one launch (start us, length us, event | category | flops | bytes accessed | tf_op | source)
XLA Modules:
  0.0 138.2 jit_solution(5002886754666666297)
XLA Ops:
  0.6 135.8 %training_step.1 = (f32[172,256]{1,0:T(8,128)}, bf16[8,48,256]{2,1,0:T(8,128)(2,1)}) custom-call(s32[4]{0:T(128)} %bitcast.19, s32[4,16]{1,0:T(4,128)} %bitcast.14, bf16[2,128,128]{2,1,0:T(8,128)(2,1)} %bitcast.13, s32[2,128]{1,0:T(2,128)} %bitcast.15, s32[2,128]{1,0:T(2,128)} %bitcast.16, s32[2,128]{1,0:T(2,128)} %bitcast.17, ...), custom_call_target="tpu_custom_call" | custom-call | tf_op jit(solution)/shard_map/training_step/pallas_call | solution.py:891
  136.4 1.8 %results.1 = (f32[172,1,256]{2,1,0:T(1,128)}, f32[128,256]{1,0:T(8,128)}, f32[172,256]{1,0:T(8,128)}) custom-call(f32[172,256]{1,0:T(8,128)} %get-tuple-element.8.refs_0_, bf16[8,48,256]{2,1,0:T(8,128)(2,1)} %get-tuple-element.9.refs_1_), custom_call_target="tpu_custom_call" | custom-call | tf_op jit(solution)/shard_map/results/pallas_call | solution.py:962

commit v6 on v5

--- a/solution.py
+++ b/solution.py
@@ -23,7 +23,9 @@
 NONE = SEC * SLOTS
 FORWARD_ORDER = (1, 2, 0, 3)
 CODED = 144
+CREW = 32
 KEEP = 4.0 / 3.0
+CHUNK = 24
 SOURCE, PREVIOUS, ROW, BACK_PREVIOUS, BACK_LAST, LAST = 0, 4, 8, 12, 16, 20
 VMEM_LIMIT = 60 << 20
 
@@ -72,13 +74,14 @@
         self.low_relay = (low_block // 16) * 16 + lax.rem(self.blk, 16)
         self.high_relay = blk_of(high_block // 16, self.depth, 1 - self.core)
         self.own_relay = self.low_relay == self.blk
-        self.corner = self.part * 2 + self.core
+        self.member = self.rep * 4 + self.part * 2 + self.core
 
     def line(self, step):
         return (self.rep, blk_of(self.part, lax.rem(self.depth + step + DEPTH, DEPTH), self.core))
 
-    def corner_device(self, index):
-        return (self.rep, blk_of(index // 2, self.depth, lax.rem(index, 2)))
+    def crew(self, index):
+        corner = lax.rem(index, 4)
+        return (index // 4, blk_of(corner // 2, self.depth, lax.rem(corner, 2)))
 
     def local(self, piece):
         return jnp.logical_and(self.own_relay, piece == self.rep)
@@ -91,12 +94,10 @@
 
 
 def greet_everyone(spot):
-    for step in range(1, REP):
-        greet((lax.rem(spot.rep + step, REP), spot.blk))
+    for step in range(1, CREW):
+        greet(spot.crew(lax.rem(spot.member + step, CREW)))
     for step in range(1, DEPTH):
         greet(spot.line(step))
-    for step in range(1, 4):
-        greet(spot.corner_device(lax.rem(spot.corner + step, 4)))
     for other in range(REP):
         @pl.when(jnp.logical_not(spot.local(other)))
         def _(other=other):
@@ -105,7 +106,7 @@
         greet((other, spot.high_relay))
     greet(spot.up)
     greet(spot.down)
-    count = (REP - 1) + (DEPTH - 1) + 3 + 2 * REP + 2
+    count = (CREW - 1) + (DEPTH - 1) + 2 * REP + 2
     return count - jnp.where(spot.own_relay, 1, 0)
 
 
@@ -214,7 +215,7 @@
             self.spot.here,
         )
 
-    def chains(self):
+    def chains(self, meanwhile=None):
         spot = self.spot
         for section in range(SEC - 1):
             other_section = SEC - 1 - section
@@ -245,6 +246,8 @@
                 return carry
 
             lax.fori_loop(0, REP, hop, 0)
+            if meanwhile is not None:
+                meanwhile(section)
 
     def last_arrivals(self):
         def finish(piece, carry):
@@ -424,18 +427,15 @@
     slopes,
     slope_send,
     slope_arrive,
-    corner,
-    corner_in,
     depth_in,
-    full_corner,
+    pieces,
+    pieces_in,
     b_send,
     b_arrive,
     c_send,
     c_arrive,
     d_send,
     d_arrive,
-    e_send,
-    e_arrive,
     *rest,
 ):
     rest = list(rest)
@@ -453,7 +453,6 @@
     second_spread = Spread(spot, shard, second_sections, *take(6))
     first_scatter = Scatter(spot, *take(4))
     second_scatter = Scatter(spot, *take(4))
-    term_scatter = Scatter(spot, *take(4))
     waits = greet_everyone(spot)
     input_copies = [
         pltpu.make_async_copy(source, target, input_sems.at[index])
@@ -552,7 +551,7 @@
 
         lax.fori_loop(0, SLOTS, one, 0, unroll=4)
 
-    def activate(section):
+    def activate(section, half):
         def one(index, carry):
             pre_act = jnp.dot(
                 second_sections[section][index], weight_in[...], preferred_element_type=F32
@@ -562,7 +561,11 @@
             dense[section * SLOTS + index] = jnp.where(flag > 0.0, active, 0.0).astype(BF16)
             return carry
 
-        lax.fori_loop(0, SLOTS, one, 0, unroll=4)
+        lax.fori_loop(half * REP, (half + 1) * REP, one, 0, unroll=4)
+
+    def activate_arrived(section):
+        activate(section, 0)
+        activate(SEC - 1 - section, 1)
 
     first_spread.start_low()
     first_spread.start_high()
@@ -585,14 +588,11 @@
     shard[1] = first_scatter.total(1).astype(BF16)
     second_spread.start_high()
     second_spread.pass_on()
-    second_spread.chains()
-    activate(1)
-    activate(2)
+    second_spread.chains(activate_arrived)
     second_products(1)
     second_products(2)
     second_spread.last_arrivals()
-    activate(0)
-    activate(3)
+    activate_arrived(SEC - 1)
     second_products(0)
     second_products(3)
     second_scatter.put(0, second_sum(0))
@@ -703,44 +703,51 @@
     for section in range(SEC):
         back_products(section)
         terms(section)
-    in_rows = in_sum.shape[0]
-    chunk = (in_rows + WIDE) // REP
-    joined = jnp.concatenate([in_sum[...], out_sum[...]], axis=0).astype(BF16)
-    for index in range(REP):
-        term_scatter.pieces[0, index] = joined[index * chunk : (index + 1) * chunk]
-    for step in range(1, REP):
-        term_scatter.copy(0, lax.rem(rep + step, REP), rep).start()
-    term_scatter.landing[0, rep] = term_scatter.pieces[0, rep]
-    total = term_scatter.total(0)
-    term_scatter.drain()
-    for index in range(12):
-        corner[index // 3, index % 3] = total[
-            (index // 2) * 8 : (index // 2) * 8 + 8, (index % 2) * LANES : (index % 2 + 1) * LANES
-        ]
-    me = spot.corner
-    for step in range(1, 4):
-        other = lax.rem(me + step, 4)
-        remote(
-            corner.at[other],
-            corner_in.at[me],
+    joined = jnp.concatenate([in_sum[...], out_sum[...]], axis=0)
+    for index in range(CREW):
+        row = index % (CREW // 2) * CHUNK
+        lane = index // (CREW // 2) * LANES
+        pieces[index] = joined[row : row + CHUNK, lane : lane + LANES].astype(BF16)
+    me, depth = spot.member, spot.depth
+
+    def reduce_copy(other, lands):
+        return remote(
+            pieces.at[other],
+            pieces_in.at[lands],
             b_send.at[other],
-            b_arrive.at[me],
-            spot.corner_device(other),
-        ).start()
-    for step in range(1, 4):
-        other = lax.rem(me + step, 4)
-        copy = remote(
-            corner.at[other],
-            corner_in.at[other],
-            b_send.at[other],
-            b_arrive.at[other],
-            spot.corner_device(other),
+            b_arrive.at[lands],
+            spot.crew(other),
         )
-        copy.wait_recv()
-        copy.wait_send()
-    corner_in[me] = corner[me]
-    depth = spot.depth
-    depth_in[depth] = corner_in[0] + corner_in[1] + corner_in[2] + corner_in[3]
+
+    def gather_copy(other, lands):
+        return remote(
+            full.at[me], full.at[lands], d_send.at[other], d_arrive.at[lands], spot.crew(other)
+        )
+
+    def start_all(copy):
+        def one(step, carry):
+            copy(lax.rem(me + step, CREW), me).start()
+            return carry
+
+        lax.fori_loop(1, CREW, one, 0)
+
+    def wait_all(copy):
+        def one(step, carry):
+            other = lax.rem(me + step, CREW)
+            both = copy(other, other)
+            both.wait_recv()
+            both.wait_send()
+            return carry
+
+        lax.fori_loop(1, CREW, one, 0)
+
+    start_all(reduce_copy)
+    pieces_in[me] = pieces[me]
+    wait_all(reduce_copy)
+    total = pieces_in[0].astype(F32)
+    for index in range(1, CREW):
+        total = total + pieces_in[index].astype(F32)
+    depth_in[depth] = total
     for step in range(1, DEPTH):
         remote(
             depth_in.at[depth],
@@ -763,55 +770,22 @@
     total = depth_in[0]
     for index in range(1, DEPTH):
         total = total + depth_in[index]
-    full_corner[me] = total
-    for step in range(1, 4):
-        other = lax.rem(me + step, 4)
-        remote(
-            full_corner.at[me],
-            full_corner.at[me],
-            d_send.at[other],
-            d_arrive.at[me],
-            spot.corner_device(other),
-        ).start()
-    for step in range(1, 4):
-        other = lax.rem(me + step, 4)
-        copy = remote(
-            full_corner.at[me],
-            full_corner.at[other],
-            d_send.at[other],
-            d_arrive.at[other],
-            spot.corner_device(other),
-        )
-        copy.wait_recv()
-        copy.wait_send()
-    full[rep] = jnp.concatenate(
+    full[me] = total.astype(BF16)
+    start_all(gather_copy)
+    wait_all(gather_copy)
+
+
+def result_kernel(in_rows, logits, full, logits_out, grad_in, grad_out):
+    logits_out[:, 0, :] = logits[...]
+    joined = jnp.concatenate(
         [
             jnp.concatenate(
-                [
-                    full_corner[(2 * row) // 3, (2 * row) % 3],
-                    full_corner[(2 * row + 1) // 3, (2 * row + 1) % 3],
-                ],
-                axis=1,
-            )
-            for row in range(6)
+                [full[start + index].astype(F32) for index in range(CREW // 2)], axis=0
+            )
+            for start in (0, CREW // 2)
         ],
-        axis=0,
-    ).astype(BF16)
-    for step in range(1, REP):
-        other = lax.rem(rep + step, REP)
-        remote(full.at[rep], full.at[rep], e_send.at[other], e_arrive.at[rep], (other, blk)).start()
-    for step in range(1, REP):
-        other = lax.rem(rep + step, REP)
-        copy = remote(
-            full.at[rep], full.at[other], e_send.at[other], e_arrive.at[other], (other, blk)
-        )
-        copy.wait_recv()
-        copy.wait_send()
-
-
-def result_kernel(in_rows, logits, full, logits_out, grad_in, grad_out):
-    logits_out[:, 0, :] = logits[...]
-    joined = jnp.concatenate([full[index] for index in range(REP)], axis=0).astype(F32)
+        axis=1,
+    )
     grad_in[...] = joined[:in_rows]
     grad_out[...] = joined[in_rows : in_rows + CLASSES]
 
@@ -886,11 +860,10 @@
     shape = jax.ShapeDtypeStruct
     dma = pltpu.SemaphoreType.DMA
     vmem = pltpu.VMEM
-    chunk = (width + WIDE) // REP
     anywhere = pl.BlockSpec(memory_space=pl.ANY)
     logits, full = pl.pallas_call(
         lambda *refs: step_kernel(scale, *refs),
-        out_shape=(shape((CLASSES, own_rows), F32), shape((REP, chunk, WIDE), BF16)),
+        out_shape=(shape((CLASSES, own_rows), F32), shape((CREW, CHUNK, LANES), BF16)),
         in_specs=[
             pl.BlockSpec(memory_space=pltpu.SMEM),
             whole(),
@@ -925,23 +898,19 @@
             vmem((2 * REP, PACKED, LANES), BF16),
             dma((2, REP)),
             dma((2, REP)),
-            vmem((4, 3, 8, LANES), F32),
-            vmem((4, 3, 8, LANES), F32),
-            vmem((DEPTH, 3, 8, LANES), F32),
-            vmem((4, 3, 8, LANES), F32),
-            dma((4,)),
-            dma((4,)),
+            vmem((DEPTH, CHUNK, LANES), F32),
+            vmem((CREW, CHUNK, LANES), BF16),
+            vmem((CREW, CHUNK, LANES), BF16),
+            dma((CREW,)),
+            dma((CREW,)),
             dma((DEPTH,)),
             dma((DEPTH,)),
-            dma((4,)),
-            dma((4,)),
-            dma((REP,)),
-            dma((REP,)),
+            dma((CREW,)),
+            dma((CREW,)),
             *spread_scratch(CODED),
             *spread_scratch(TILE),
             *scatter_scratch(2, TILE, LANES, F32),
             *scatter_scratch(2, PACKED, LANES, BF16),
-            *scatter_scratch(1, chunk, WIDE, BF16),
         ],
         compiler_params=pltpu.CompilerParams(
             collective_id=0, has_side_effects=True, vmem_limit_bytes=VMEM_LIMIT

time: 138 us -> 135 us (0.978)
  Pallas kernels: 138 us -> 134 us
    pallas_call x1, Pallas kernels: 136 us -> 132 us  [on_device(): pl.pallas_call(lambda *refs: step_kernel(scale, *refs), out_shape=(shape(...]
where the time goes in v6:
time: 135 us
  Pallas kernels  134 us (99%)
    pallas_call x1, Pallas kernels, on_device(): pl.pallas_call(lambda *refs: step_kernel(scale, *refs), out_shape=(shape(...  132 us

profile of v6, /device:TPU:1, one launch (start us, length us, event | category | flops | bytes accessed | tf_op | source)
XLA Modules:
  0.0 134.6 jit_solution(14939129497347230426)
XLA Ops:
  0.6 132.2 %training_step.1 = (f32[172,256]{1,0:T(8,128)}, bf16[32,24,128]{2,1,0:T(8,128)(2,1)}) custom-call(s32[4]{0:T(128)} %bitcast.19, s32[4,16]{1,0:T(4,128)} %bitcast.14, bf16[2,128,128]{2,1,0:T(8,128)(2,1)} %bitcast.13, s32[2,128]{1,0:T(2,128)} %bitcast.15, s32[2,128]{1,0:T(2,128)} %bitcast.16, s32[2,128]{1,0:T(2,128)} %bitcast.17, ...), custom_call_target="tpu_custom_call" | custom-call | tf_op jit(solution)/shard_map/training_step/pallas_call | solution.py:864
  132.8 1.8 %results.1 = (f32[172,1,256]{2,1,0:T(1,128)}, f32[128,256]{1,0:T(8,128)}, f32[172,256]{1,0:T(8,128)}) custom-call(f32[172,256]{1,0:T(8,128)} %get-tuple-element.8.refs_0_, bf16[32,24,128]{2,1,0:T(8,128)(2,1)} %get-tuple-element.9.refs_1_), custom_call_target="tpu_custom_call" | custom-call | tf_op jit(solution)/shard_map/results/pallas_call | solution.py:931

commit v7 on v6

--- a/solution.py
+++ b/solution.py
@@ -425,6 +425,7 @@
     in_sum,
     out_sum,
     slopes,
+    wide_slopes,
     slope_send,
     slope_arrive,
     depth_in,
@@ -467,16 +468,24 @@
     ]
     for copy in input_copies:
         copy.start()
-    fill_tables(place, count, table_values)
     table_copy = pltpu.make_async_copy(table_values, table, input_sems.at[len(input_copies)])
-    table_copy.start()
-    running[NONE] = jnp.zeros((TILE, WIDE), F32)
-    wide_out[...] = jnp.zeros_like(wide_out)
-    wide_bias[...] = jnp.zeros_like(wide_bias)
-    wide_bias[:, :CLASSES] = bias[...]
+
+    def prepare(section):
+        if section == 0:
+            fill_tables(place, count, table_values)
+            table_copy.start()
+        elif section == 1:
+            running[NONE] = jnp.zeros((TILE, WIDE), F32)
+            wide_out[...] = jnp.zeros_like(wide_out)
+            wide_bias[...] = jnp.zeros_like(wide_bias)
+            wide_bias[:, :CLASSES] = bias[...]
+            input_copies[1].wait()
+            wide_out[:CLASSES, :] = weight_out[...]
+            input_copies[2].wait()
+            input_copies[3].wait()
+            table_copy.wait()
+
     input_copies[0].wait()
-    input_copies[1].wait()
-    wide_out[:CLASSES, :] = weight_out[...]
     code_rows = lax.broadcasted_iota(jnp.int32, (CODED - TILE, LANES), 0)
     for half in range(2):
         coded[half, :TILE] = x[half]
@@ -509,7 +518,7 @@
                 )
             return carry
 
-        lax.fori_loop(0, SLOTS // 4, some, 0)
+        lax.fori_loop(0, SLOTS // 4, some, 0, unroll=2)
 
     def first_products(section):
         products(section, LANES, lambda index: first_sections[section][index, :TILE])
@@ -570,10 +579,7 @@
     first_spread.start_low()
     first_spread.start_high()
     first_spread.pass_on()
-    first_spread.chains()
-    input_copies[2].wait()
-    input_copies[3].wait()
-    table_copy.wait()
+    first_spread.chains(prepare)
     first_products(1)
     first_products(2)
     first_spread.last_arrivals()
@@ -647,6 +653,12 @@
 
     lax.fori_loop(1, REP, slope_waits, 0)
 
+    def widen(index, carry):
+        wide_slopes[index] = unpack(slopes[index])
+        return carry
+
+    lax.fori_loop(0, 2 * REP, widen, 0, unroll=4)
+
     def back_products(section):
         def some(group, carry):
             made = []
@@ -655,7 +667,7 @@
                 made.append(
                     lax.dot_general(
                         tiles[section * SLOTS + slot],
-                        unpack(slopes[table[ROW + section, slot]]),
+                        wide_slopes[table[ROW + section, slot]],
                         (((0,), (0,)), ((), ())),
                         preferred_element_type=F32,
                     )
@@ -667,7 +679,7 @@
                 )
             return carry
 
-        lax.fori_loop(0, SLOTS // 4, some, 0)
+        lax.fori_loop(0, SLOTS // 4, some, 0, unroll=2)
 
         def gather(piece, carry):
             for half in range(2):
@@ -896,6 +908,7 @@
             vmem((width, WIDE), F32),
             vmem((WIDE, WIDE), F32),
             vmem((2 * REP, PACKED, LANES), BF16),
+            vmem((2 * REP, TILE, WIDE), BF16),
             dma((2, REP)),
             dma((2, REP)),
             vmem((DEPTH, CHUNK, LANES), F32),

time: 135 us -> 131 us (0.970)
  Pallas kernels: 134 us -> 131 us
    pallas_call x1, Pallas kernels: 132 us -> 129 us  [on_device(): pl.pallas_call(lambda *refs: step_kernel(scale, *refs), out_shape=(shape(...]
where the time goes in v7:
time: 131 us
  Pallas kernels  131 us (100%)
    pallas_call x1, Pallas kernels, on_device(): pl.pallas_call(lambda *refs: step_kernel(scale, *refs), out_shape=(shape(...  129 us

profile of v7, /device:TPU:1, one launch (start us, length us, event | category | flops | bytes accessed | tf_op | source)
XLA Modules:
  0.0 131.3 jit_solution(17217934307485789387)
XLA Ops:
  0.6 128.8 %training_step.1 = (f32[172,256]{1,0:T(8,128)}, bf16[32,24,128]{2,1,0:T(8,128)(2,1)}) custom-call(s32[4]{0:T(128)} %bitcast.19, s32[4,16]{1,0:T(4,128)} %bitcast.14, bf16[2,128,128]{2,1,0:T(8,128)(2,1)} %bitcast.13, s32[2,128]{1,0:T(2,128)} %bitcast.15, s32[2,128]{1,0:T(2,128)} %bitcast.16, s32[2,128]{1,0:T(2,128)} %bitcast.17, ...), custom_call_target="tpu_custom_call" | custom-call | tf_op jit(solution)/shard_map/training_step/pallas_call | solution.py:876
  129.5 1.8 %results.1 = (f32[172,1,256]{2,1,0:T(1,128)}, f32[128,256]{1,0:T(8,128)}, f32[172,256]{1,0:T(8,128)}) custom-call(f32[172,256]{1,0:T(8,128)} %get-tuple-element.8.refs_0_, bf16[32,24,128]{2,1,0:T(8,128)(2,1)} %get-tuple-element.9.refs_1_), custom_call_target="tpu_custom_call" | custom-call | tf_op jit(solution)/shard_map/results/pallas_call | solution.py:944

commit v8 on v7

--- a/solution.py
+++ b/solution.py
@@ -221,7 +221,9 @@
             other_section = SEC - 1 - section
 
             def hop(step, carry, section=section, other_section=other_section):
-                piece = lax.rem(spot.rep + REP - step, REP)
+                pair = step // 2
+                far = pair + pair // 2 - 2 * (pair // 3)
+                piece = 2 * lax.rem(spot.rep // 2 + far, 4) + lax.rem(spot.rep + step, 2)
                 if section == 0:
                     @pl.when(jnp.logical_not(spot.local(piece)))
                     def _():
@@ -741,7 +743,7 @@
             copy(lax.rem(me + step, CREW), me).start()
             return carry
 
-        lax.fori_loop(1, CREW, one, 0)
+        lax.fori_loop(1, CREW, one, 0, unroll=8)
 
     def wait_all(copy):
         def one(step, carry):
@@ -751,7 +753,7 @@
             both.wait_send()
             return carry
 
-        lax.fori_loop(1, CREW, one, 0)
+        lax.fori_loop(1, CREW, one, 0, unroll=8)
 
     start_all(reduce_copy)
     pieces_in[me] = pieces[me]

time: 131 us -> 131 us (level)
  no operation moved by 1% of the time
where the time goes in v8:
time: 131 us
  Pallas kernels  130 us (99%)
    pallas_call x1, Pallas kernels, on_device(): pl.pallas_call(lambda *refs: step_kernel(scale, *refs), out_shape=(shape(...  128 us

profile of v8, /device:TPU:1, one launch (start us, length us, event | category | flops | bytes accessed | tf_op | source)
XLA Modules:
  0.0 130.9 jit_solution(10287795378229148445)
XLA Ops:
  0.6 128.5 %training_step.1 = (f32[172,256]{1,0:T(8,128)}, bf16[32,24,128]{2,1,0:T(8,128)(2,1)}) custom-call(s32[4]{0:T(128)} %bitcast.19, s32[4,16]{1,0:T(4,128)} %bitcast.14, bf16[2,128,128]{2,1,0:T(8,128)(2,1)} %bitcast.13, s32[2,128]{1,0:T(2,128)} %bitcast.15, s32[2,128]{1,0:T(2,128)} %bitcast.16, s32[2,128]{1,0:T(2,128)} %bitcast.17, ...), custom_call_target="tpu_custom_call" | custom-call | tf_op jit(solution)/shard_map/training_step/pallas_call | solution.py:878
  129.1 1.8 %results.1 = (f32[172,1,256]{2,1,0:T(1,128)}, f32[128,256]{1,0:T(8,128)}, f32[172,256]{1,0:T(8,128)}) custom-call(f32[172,256]{1,0:T(8,128)} %get-tuple-element.8.refs_0_, bf16[32,24,128]{2,1,0:T(8,128)(2,1)} %get-tuple-element.9.refs_1_), custom_call_target="tpu_custom_call" | custom-call | tf_op jit(solution)/shard_map/results/pallas_call | solution.py:946

commit v9 on v8

--- a/solution.py
+++ b/solution.py
@@ -323,7 +323,7 @@
             self.copy(half, other, rep).start()
             return carry
 
-        lax.fori_loop(0, REP - 1, one, 0)
+        lax.fori_loop(0, REP - 1, one, 0, unroll=7)
         self.landing[half, rep] = make(rep)
 
     def total(self, half):

time: 131 us -> 130 us (level)
    pallas_call x1, Pallas kernels: 128 us -> 127 us  [on_device(): pl.pallas_call(lambda *refs: step_kernel(scale, *refs), out_shape=(shape(...]
where the time goes in v9:
time: 130 us
  Pallas kernels  129 us (99%)
    pallas_call x1, Pallas kernels, on_device(): pl.pallas_call(lambda *refs: step_kernel(scale, *refs), out_shape=(shape(...  127 us

profile of v9, /device:TPU:1, one launch (start us, length us, event | category | flops | bytes accessed | tf_op | source)
XLA Modules:
  0.0 129.6 jit_solution(16549694421360838078)
XLA Ops:
  0.6 127.1 %training_step.1 = (f32[172,256]{1,0:T(8,128)}, bf16[32,24,128]{2,1,0:T(8,128)(2,1)}) custom-call(s32[4]{0:T(128)} %bitcast.19, s32[4,16]{1,0:T(4,128)} %bitcast.14, bf16[2,128,128]{2,1,0:T(8,128)(2,1)} %bitcast.13, s32[2,128]{1,0:T(2,128)} %bitcast.15, s32[2,128]{1,0:T(2,128)} %bitcast.16, s32[2,128]{1,0:T(2,128)} %bitcast.17, ...), custom_call_target="tpu_custom_call" | custom-call | tf_op jit(solution)/shard_map/training_step/pallas_call | solution.py:878
  127.7 1.8 %results.1 = (f32[172,1,256]{2,1,0:T(1,128)}, f32[128,256]{1,0:T(8,128)}, f32[172,256]{1,0:T(8,128)}) custom-call(f32[172,256]{1,0:T(8,128)} %get-tuple-element.8.refs_0_, bf16[32,24,128]{2,1,0:T(8,128)(2,1)} %get-tuple-element.9.refs_1_), custom_call_target="tpu_custom_call" | custom-call | tf_op jit(solution)/shard_map/results/pallas_call | solution.py:946
